TPU v7x, 32 devices: a whole 2x2x4 slice. The times are simulated.
32 devices in a mesh: scen: 2 (over x), hour: 4 (over z), reg: 4 (over y, core).
Axes of the slice: x: 2, y: 2, z: 4, core: 2. Of those that a mesh axis runs over, the one named last changes fastest.
Arguments:
- cost_rate: float32 [8, 672, 2048], P('scen', 'hour', 'reg'), may hold values from 0.05 to 1
- invest_cost: float32 [3, 2048], P(None, 'reg'), may hold values from 0.1 to 1
- tile: bfloat16 [4, 256, 2048], P('hour', None, 'reg'), may hold values from -0.1875 to 0.1875
- tile_mask: int32 [4, 256, 2048], P('hour', None, 'reg'), may hold values 0 or 1
- demand: float32 [8, 672, 256], P('scen', 'hour'), may hold values from -6 to 6
- dispatch: float32 [8, 672, 2048], P('scen', 'hour', 'reg'), may hold values from 0 to 1
- dual: float32 [8, 672, 256], P('scen', 'hour'), may hold values from 0 to 1
- cap_dual: float32 [8, 672, 2048], P('scen', 'hour', 'reg'), may hold values from 0 to 1
- capacity: float32 [8, 3, 2048], P('scen', None, 'reg'), may hold values from 0 to 2
- multiplier: float32 [8, 3, 2048], P('scen', None, 'reg'), may hold values from -3 to 3
- consensus: float32 [8, 3, 2048], P('scen', None, 'reg'), may hold values from 0 to 2
- scen_weight: float32 [8], P('scen'), may hold values from 0.1 to 1
- node_of: int32 [3, 8], P(None, 'scen'), may hold values from 0 to 3, as said below
Outputs:
- dispatch_out: float32 [8, 672, 2048], P('scen', 'hour', 'reg')
- dual_out: float32 [8, 672, 256], P('scen', 'hour', 'reg')
- capacity_out: float32 [8, 3, 2048], P('scen', None, 'reg')
- multiplier_out: float32 [8, 3, 2048], P('scen', None, 'reg')
Inputs may be any that keep to these rules, and one draw needn't show every extreme that they name: `node_of`: at each section the nodes are runs of consecutive scenarios, numbered in order from 0; each node of a section lies within one node of the section before; section 0 is one node, the last section has 4 nodes, and node counts grow from section to section.
All inputs are finite; a program needn't handle non-finite values. No bound on the sum of `tile_mask` on one device may be relied on, other than what follows from the above.
Results may differ from a plain program's by a relative error of at most 0.0015.
Values may be sent and summed in bfloat16 or wider, within the bound.
No kernel may reach another device: no remote copies, remote signals or barrier semaphores. Data moves between devices by JAX's collectives and lax.ppermute only.
A program may use at most 64 MiB of HBM per device.

v0:
```python
import jax
import jax.numpy as jnp
from jax import lax
from jax.sharding import PartitionSpec as P

ITERS = 8


RAMP_WEIGHT = 0.5
PENALTY = 1.0
STEP_PRIMAL = 0.3
STEP_INVEST = 0.5
STEP_DUAL = 0.3
STEP_CAP = 0.05


def with_halo(cells, sides, width):
    for axis, dim in sides:
        count = lax.axis_size(axis)
        ends = count - 1
        head = lax.slice_in_dim(cells, 0, width, axis=dim)
        tail = lax.slice_in_dim(cells, cells.shape[dim] - width, cells.shape[dim], axis=dim)
        cells = jnp.concatenate(
            [
                lax.ppermute(tail, axis, [(i, (i + 1) % count) for i in range(ends)]),
                cells,
                lax.ppermute(head, axis, [((i + 1) % count, i) for i in range(ends)]),
            ],
            axis=dim,
        )
    return cells


def safe_average(node_sum, node_mass):
    safe_mass = node_mass + (node_mass <= 0.0).astype(jnp.float32)
    return node_sum / safe_mass[:, :, None]


def shards(
    cost_rate,
    invest_cost,
    tile,
    tile_mask,
    demand,
    dispatch,
    dual,
    cap_dual,
    capacity,
    multiplier,
    consensus,
    scen_weight,
    node_of,
):
    matrix = tile[0] * tile_mask[0].astype(jnp.bfloat16)
    hours_all = dispatch.shape[1] * lax.axis_size("hour")
    reg_count = lax.axis_size("reg")
    reg_place = lax.axis_index("reg")
    cons_part = dual.shape[2] // reg_count
    first_row = reg_place * cons_part
    primal = dispatch
    cap_var = cap_dual
    invest = capacity
    dual_low = dual.astype(jnp.bfloat16)
    dual_var = lax.dynamic_slice_in_dim(dual, first_row, cons_part, 2)
    demand_use = lax.dynamic_slice_in_dim(demand, first_row, cons_part, 2)
    for step_index in range(ITERS):
        padded = with_halo(primal, (("hour", 1),), 1)
        rough = 2.0 * primal - padded[:, :-2] - padded[:, 2:]
        pulled = jnp.einsum("shr,rc->shc", dual_low, matrix, preferred_element_type=jnp.float32)
        grad_x = cost_rate + RAMP_WEIGHT * rough - pulled + cap_var
        zmean = lax.psum(jnp.sum(cap_var, axis=1), "hour") / hours_all
        grad_u = invest_cost[None] + multiplier + PENALTY * (invest - consensus) - zmean[:, None, :]
        primal_new = jnp.maximum(primal - STEP_PRIMAL * grad_x, 0.0)
        invest_new = jnp.maximum(invest - STEP_INVEST * grad_u, 0.0)
        primal_ext = 2.0 * primal_new - primal
        invest_ext = 2.0 * invest_new - invest
        partial_rows = jnp.einsum(
            "shc,rc->shr",
            primal_ext.astype(jnp.bfloat16),
            matrix,
            preferred_element_type=jnp.float32,
        )
        image = lax.psum_scatter(partial_rows, "reg", scatter_dimension=2, tiled=True)
        dual_var = jnp.maximum(dual_var + STEP_DUAL * (demand_use - image), 0.0)
        if step_index + 1 < ITERS:
            dual_low = lax.all_gather(dual_var.astype(jnp.bfloat16), "reg", axis=2, tiled=True)
        cap_var = jnp.maximum(
            cap_var + STEP_CAP * (primal_ext - jnp.sum(invest_ext, axis=1)[:, None, :]), 0.0
        )
        primal = primal_new
        invest = invest_new
    node_count = node_of.shape[1] * lax.axis_size("scen") // 2
    node_ids = jnp.arange(node_count, dtype=jnp.int32)
    one_hot = (node_of[:, :, None] == node_ids[None, None, :]).astype(jnp.float32)
    weighted = scen_weight[:, None, None] * invest
    node_sum = jnp.einsum("gsn,sgc->gnc", one_hot, weighted, precision=lax.Precision.HIGHEST)
    node_mass = jnp.einsum("gsn,s->gn", one_hot, scen_weight, precision=lax.Precision.HIGHEST)
    sum_total, mass_total = lax.psum((node_sum, node_mass), "scen")
    average = safe_average(sum_total, mass_total)
    spread_back = jnp.einsum("gsn,gnc->sgc", one_hot, average, precision=lax.Precision.HIGHEST)
    multiplier_out = multiplier + PENALTY * (invest - spread_back)
    return (primal, dual_var, invest, multiplier_out)


def solution(mesh):
    placed = (
        P("scen", "hour", "reg"),
        P(None, "reg"),
        P("hour", None, "reg"),
        P("hour", None, "reg"),
        P("scen", "hour", None),
        P("scen", "hour", "reg"),
        P("scen", "hour", None),
        P("scen", "hour", "reg"),
        P("scen", None, "reg"),
        P("scen", None, "reg"),
        P("scen", None, "reg"),
        P("scen"),
        P(None, "scen"),
    )
    return jax.shard_map(
        shards,
        mesh=mesh,
        in_specs=placed,
        out_specs=(
            P("scen", "hour", "reg"),
            P("scen", "hour", "reg"),
            P("scen", None, "reg"),
            P("scen", None, "reg"),
        ),
        check_vma=False,
    )
```

profile of v0, /device:TPU:0, one launch (start us, length us, event | category | flops | bytes accessed | tf_op | source)
XLA Modules:
  0.0 344.3 jit_solution(13150075542989649014)
XLA Ops:
  16.1 13.2 %psum.70 = f32[4,512]{1,0:T(4,128)S(1)} all-reduce(f32[4,512]{1,0:T(4,128)S(1)} %reduce_sum.135), channel_id=1, replica_groups=mesh['scen'=2,'hour'=4,'reg'=4] {'hour'}, use_global_device_ids=true, to_apply=%region_2.0 | all-reduce | flops 2048 | bytes 16384 | tf_op jit(solution)/shard_map/psum | solution.py:71
  29.4 5.6 %fusion.161 = (f32[4,512]{1,0:T(4,128)S(1)}, f32[4,168,512]{2,1,0:T(8,128)}, f32[4,168,512]{2,1,0:T(8,128)S(1)}) fusion(f32[4,168,512]{2,1,0:T(8,128)} %param.20, f32[4,512]{1,0:T(4,128)S(1)} %get-tuple-element.24, f32[4,168,512]{2,1,0:T(8,128)} %param.18, f32[4,168,256]{2,1,0:T(8,128)S(1)} %copy-done.19, ...), kind=kOutput, calls=%fused_computation.216 | convolution fusion | flops 182867968 | bytes 7864320 | tf_op jit(solution)/shard_map/shr,rc->shc/dot_general | solution.py:69
  41.0 11.5 %psum.71 = f32[4,512]{1,0:T(4,128)S(1)} all-reduce(f32[4,512]{1,0:T(4,128)S(1)} %get-tuple-element.22), channel_id=1, replica_groups=mesh['scen'=2,'hour'=4,'reg'=4] {'hour'}, use_global_device_ids=true, to_apply=%region_6.0 | all-reduce | flops 2048 | bytes 16384 | tf_op jit(solution)/shard_map/psum | solution.py:71
  52.5 7.2 %reduce-scatter.9.cloned.1.call-done = f32[4,168,64]{1,2,0:T(8,128)} async-done(((f32[4,168,256]{1,2,0:T(8,128)}), f32[4,168,64]{1,2,0:T(8,128)}) %reduce-scatter.9.cloned.1.call-update) | async-done | bytes 172048 | tf_op jit(solution)/shard_map/reduce_scatter | solution.py:83
  60.9 6.6 %all_gather.21 = bf16[4,168,256]{1,2,0:T(8,128)(2,1)S(1)} all-gather(bf16[4,168,64]{1,2,0:T(8,128)(2,1)S(1)} %fusion.131), channel_id=1, replica_groups=mesh['scen'=2,'hour'=4,'reg'=4] {'reg'}, dimensions={2}, use_global_device_ids=true | all-gather | bytes 430080 | tf_op jit(solution)/shard_map/all_gather | solution.py:86
  79.4 13.1 %psum.72 = f32[4,512]{1,0:T(4,128)S(1)} all-reduce(f32[4,512]{1,0:T(4,128)S(1)} %get-tuple-element.18), channel_id=1, replica_groups=mesh['scen'=2,'hour'=4,'reg'=4] {'hour'}, use_global_device_ids=true, to_apply=%region_10.0 | all-reduce | flops 2048 | bytes 16384 | tf_op jit(solution)/shard_map/psum | solution.py:71
  92.6 6.6 %reduce-scatter.11.cloned.1.call-done = f32[4,168,64]{1,2,0:T(8,128)} async-done(((f32[4,168,256]{1,2,0:T(8,128)}), f32[4,168,64]{1,2,0:T(8,128)}) %reduce-scatter.11.cloned.1.call-update) | async-done | bytes 172048 | tf_op jit(solution)/shard_map/reduce_scatter | solution.py:83
  100.2 6.6 %all_gather.22 = bf16[4,168,256]{1,2,0:T(8,128)(2,1)S(1)} all-gather(bf16[4,168,64]{1,2,0:T(8,128)(2,1)S(1)} %get-tuple-element.20), channel_id=1, replica_groups=mesh['scen'=2,'hour'=4,'reg'=4] {'reg'}, dimensions={2}, use_global_device_ids=true | all-gather | bytes 430080 | tf_op jit(solution)/shard_map/all_gather | solution.py:86
  119.1 13.1 %psum.73 = f32[4,512]{1,0:T(4,128)S(1)} all-reduce(f32[4,512]{1,0:T(4,128)S(1)} %get-tuple-element.16), channel_id=1, replica_groups=mesh['scen'=2,'hour'=4,'reg'=4] {'hour'}, use_global_device_ids=true, to_apply=%region_14.0 | all-reduce | flops 2048 | bytes 16384 | tf_op jit(solution)/shard_map/psum | solution.py:71
  132.2 6.7 %reduce-scatter.13.cloned.1.call-done = f32[4,168,64]{1,2,0:T(8,128)} async-done(((f32[4,168,256]{1,2,0:T(8,128)}), f32[4,168,64]{1,2,0:T(8,128)}) %reduce-scatter.13.cloned.1.call-update) | async-done | bytes 172048 | tf_op jit(solution)/shard_map/reduce_scatter | solution.py:83
  139.9 6.6 %all_gather.23 = bf16[4,168,256]{1,2,0:T(8,128)(2,1)S(1)} all-gather(bf16[4,168,64]{1,2,0:T(8,128)(2,1)S(1)} %fusion.132), channel_id=1, replica_groups=mesh['scen'=2,'hour'=4,'reg'=4] {'reg'}, dimensions={2}, use_global_device_ids=true | all-gather | bytes 430080 | tf_op jit(solution)/shard_map/all_gather | solution.py:86
  158.2 13.6 %psum.74 = f32[4,512]{1,0:T(4,128)S(1)} all-reduce(f32[4,512]{1,0:T(4,128)S(1)} %get-tuple-element.12), channel_id=1, replica_groups=mesh['scen'=2,'hour'=4,'reg'=4] {'hour'}, use_global_device_ids=true, to_apply=%region_18.0 | all-reduce | flops 2048 | bytes 16384 | tf_op jit(solution)/shard_map/psum | solution.py:71
  171.9 7.0 %reduce-scatter.15.cloned.1.call-done = f32[4,168,64]{1,2,0:T(8,128)} async-done(((f32[4,168,256]{1,2,0:T(8,128)}), f32[4,168,64]{1,2,0:T(8,128)}) %reduce-scatter.15.cloned.1.call-update) | async-done | bytes 172048 | tf_op jit(solution)/shard_map/reduce_scatter | solution.py:83
  180.1 6.8 %all_gather.24 = bf16[4,168,256]{1,2,0:T(8,128)(2,1)S(1)} all-gather(bf16[4,168,64]{1,2,0:T(8,128)(2,1)S(1)} %get-tuple-element.14), channel_id=1, replica_groups=mesh['scen'=2,'hour'=4,'reg'=4] {'reg'}, dimensions={2}, use_global_device_ids=true | all-gather | bytes 430080 | tf_op jit(solution)/shard_map/all_gather | solution.py:86
  198.7 13.1 %psum.75 = f32[4,512]{1,0:T(4,128)S(1)} all-reduce(f32[4,512]{1,0:T(4,128)S(1)} %get-tuple-element.10), channel_id=1, replica_groups=mesh['scen'=2,'hour'=4,'reg'=4] {'hour'}, use_global_device_ids=true, to_apply=%region_22.0 | all-reduce | flops 2048 | bytes 16384 | tf_op jit(solution)/shard_map/psum | solution.py:71
  211.9 6.7 %reduce-scatter.17.cloned.1.call-done = f32[4,168,64]{1,2,0:T(8,128)} async-done(((f32[4,168,256]{1,2,0:T(8,128)}), f32[4,168,64]{1,2,0:T(8,128)}) %reduce-scatter.17.cloned.1.call-update) | async-done | bytes 172048 | tf_op jit(solution)/shard_map/reduce_scatter | solution.py:83
  219.6 6.6 %all_gather.25 = bf16[4,168,256]{1,2,0:T(8,128)(2,1)S(1)} all-gather(bf16[4,168,64]{1,2,0:T(8,128)(2,1)S(1)} %fusion.133), channel_id=1, replica_groups=mesh['scen'=2,'hour'=4,'reg'=4] {'reg'}, dimensions={2}, use_global_device_ids=true | all-gather | bytes 430080 | tf_op jit(solution)/shard_map/all_gather | solution.py:86
  238.4 13.0 %psum.76 = f32[4,512]{1,0:T(4,128)S(1)} all-reduce(f32[4,512]{1,0:T(4,128)S(1)} %get-tuple-element.6), channel_id=1, replica_groups=mesh['scen'=2,'hour'=4,'reg'=4] {'hour'}, use_global_device_ids=true, to_apply=%region_26.0 | all-reduce | flops 2048 | bytes 16384 | tf_op jit(solution)/shard_map/psum | solution.py:71
  251.6 7.0 %reduce-scatter.19.cloned.1.call-done = f32[4,168,64]{1,2,0:T(8,128)} async-done(((f32[4,168,256]{1,2,0:T(8,128)}), f32[4,168,64]{1,2,0:T(8,128)}) %reduce-scatter.19.cloned.1.call-update) | async-done | bytes 172048 | tf_op jit(solution)/shard_map/reduce_scatter | solution.py:83
  259.7 6.6 %all_gather.26 = bf16[4,168,256]{1,2,0:T(8,128)(2,1)S(1)} all-gather(bf16[4,168,64]{1,2,0:T(8,128)(2,1)S(1)} %get-tuple-element.8), channel_id=1, replica_groups=mesh['scen'=2,'hour'=4,'reg'=4] {'reg'}, dimensions={2}, use_global_device_ids=true | all-gather | bytes 430080 | tf_op jit(solution)/shard_map/all_gather | solution.py:86
  277.1 19.9 %reduce-scatter.21.cloned.1.call-done = f32[4,168,64]{1,2,0:T(8,128)} async-done(((f32[4,168,256]{1,2,0:T(8,128)}), f32[4,168,64]{1,2,0:T(8,128)}) %reduce-scatter.21.cloned.1.call-update) | async-done | bytes 172048 | tf_op jit(solution)/shard_map/reduce_scatter | solution.py:83
  298.1 6.6 %all_gather.27 = bf16[4,168,256]{1,2,0:T(8,128)(2,1)S(1)} all-gather(bf16[4,168,64]{1,2,0:T(8,128)(2,1)S(1)} %fusion.134), channel_id=1, replica_groups=mesh['scen'=2,'hour'=4,'reg'=4] {'reg'}, dimensions={2}, use_global_device_ids=true | all-gather | bytes 430080 | tf_op jit(solution)/shard_map/all_gather | solution.py:86
  310.4 11.8 %psum.77 = f32[4,512]{1,0:T(4,128)S(1)} all-reduce(f32[4,512]{1,0:T(4,128)S(1)} %get-tuple-element.48), channel_id=1, replica_groups=mesh['scen'=2,'hour'=4,'reg'=4] {'hour'}, use_global_device_ids=true, to_apply=%region_30.0 | all-reduce | flops 2048 | bytes 16384 | tf_op jit(solution)/shard_map/psum | solution.py:71
  322.7 8.3 %all-reduce = (f32[3,4,512]{2,1,0:T(4,128)S(1)}, f32[3,4]{1,0:T(4,128)S(1)}) all-reduce(f32[3,4,512]{2,1,0:T(4,128)S(1)} %fusion.135, f32[3,4]{1,0:T(4,128)S(1)} %bitcast.85), channel_id=1, replica_groups=mesh['scen'=2,'hour'=4,'reg'=4] {'scen'}, use_global_device_ids=true, to_apply=%region_31.0 | all-reduce | flops 6156 | bytes 49248 | tf_op jit(solution)/shard_map/psum | solution.py:98
  (163 shorter events, 105.7 us)
Async XLA Ops:
  7.3 52.5 %reduce-scatter.9.cloned.1.call-start = ((), (), s32[]{:S(2)}) async-start(), calls=%async_computation.8 | async-start | bytes 1310720 | tf_op jit(solution)/shard_map/reduce_scatter | solution.py:83
  8.3 21.1 %collective-permute-start = (f32[4,1,512]{2,1,0:T(1,128)S(1)}, f32[4,1,512]{2,1,0:T(1,128)S(1)}, u32[]{:S(2)}, u32[]{:S(2)}) collective-permute-start(f32[4,1,512]{2,1,0:T(1,128)S(1)} %get-tuple-element.40), channel_id=1, source_target_pairs={{0,4},{4,8},{8,12},{1,5},{5,9},{9,13},{2,6},{6,10},{10,14},{3,7},{... | collective-permute-start | bytes 24584 | tf_op jit(solution)/shard_map/ppermute | solution.py:25
  13.3 16.1 %collective-permute-start.1 = (f32[4,1,512]{2,1,0:T(1,128)S(1)}, f32[4,1,512]{2,1,0:T(1,128)S(1)}, u32[]{:S(2)}, u32[]{:S(2)}) collective-permute-start(f32[4,1,512]{2,1,0:T(1,128)S(1)} %get-tuple-element.41), channel_id=1, source_target_pairs={{4,0},{8,4},{12,8},{5,1},{9,5},{13,9},{6,2},{10,6},{14,10},{7,3},{... | collective-permute-start | bytes 24584 | tf_op jit(solution)/shard_map/ppermute | solution.py:27
  36.6 62.6 %reduce-scatter.11.cloned.1.call-start = ((), (), s32[]{:S(2)}) async-start(), calls=%async_computation.9 | async-start | bytes 1310720 | tf_op jit(solution)/shard_map/reduce_scatter | solution.py:83
  38.4 29.1 %collective-permute-start.2 = (f32[4,1,512]{2,1,0:T(1,128)S(1)}, f32[4,1,512]{2,1,0:T(1,128)S(1)}, u32[]{:S(2)}, u32[]{:S(2)}) collective-permute-start(f32[4,1,512]{2,1,0:T(1,128)S(1)} %get-tuple-element.38), channel_id=1, source_target_pairs={{0,4},{4,8},{8,12},{1,5},{5,9},{9,13},{2,6},{6,10},{10,14},{3,7},{... | collective-permute-start | bytes 24584 | tf_op jit(solution)/shard_map/ppermute | solution.py:25
  39.7 27.8 %collective-permute-start.3 = (f32[4,1,512]{2,1,0:T(1,128)S(1)}, f32[4,1,512]{2,1,0:T(1,128)S(1)}, u32[]{:S(2)}, u32[]{:S(2)}) collective-permute-start(f32[4,1,512]{2,1,0:T(1,128)S(1)} %get-tuple-element.39), channel_id=1, source_target_pairs={{4,0},{8,4},{12,8},{5,1},{9,5},{13,9},{6,2},{10,6},{14,10},{7,3},{... | collective-permute-start | bytes 24584 | tf_op jit(solution)/shard_map/ppermute | solution.py:27
  73.7 65.2 %reduce-scatter.13.cloned.1.call-start = ((), (), s32[]{:S(2)}) async-start(), calls=%async_computation.10 | async-start | bytes 1310720 | tf_op jit(solution)/shard_map/reduce_scatter | solution.py:83
  74.7 32.1 %collective-permute-start.4 = (f32[4,1,512]{2,1,0:T(1,128)S(1)}, f32[4,1,512]{2,1,0:T(1,128)S(1)}, u32[]{:S(2)}, u32[]{:S(2)}) collective-permute-start(f32[4,1,512]{2,1,0:T(1,128)S(1)} %get-tuple-element.36), channel_id=1, source_target_pairs={{0,4},{4,8},{8,12},{1,5},{5,9},{9,13},{2,6},{6,10},{10,14},{3,7},{... | collective-permute-start | bytes 24584 | tf_op jit(solution)/shard_map/ppermute | solution.py:25
  78.1 28.7 %collective-permute-start.5 = (f32[4,1,512]{2,1,0:T(1,128)S(1)}, f32[4,1,512]{2,1,0:T(1,128)S(1)}, u32[]{:S(2)}, u32[]{:S(2)}) collective-permute-start(f32[4,1,512]{2,1,0:T(1,128)S(1)} %get-tuple-element.37), channel_id=1, source_target_pairs={{4,0},{8,4},{12,8},{5,1},{9,5},{13,9},{6,2},{10,6},{14,10},{7,3},{... | collective-permute-start | bytes 24584 | tf_op jit(solution)/shard_map/ppermute | solution.py:27
  113.4 65.5 %reduce-scatter.15.cloned.1.call-start = ((), (), s32[]{:S(2)}) async-start(), calls=%async_computation.11 | async-start | bytes 1310720 | tf_op jit(solution)/shard_map/reduce_scatter | solution.py:83
  114.4 32.2 %collective-permute-start.6 = (f32[4,1,512]{2,1,0:T(1,128)S(1)}, f32[4,1,512]{2,1,0:T(1,128)S(1)}, u32[]{:S(2)}, u32[]{:S(2)}) collective-permute-start(f32[4,1,512]{2,1,0:T(1,128)S(1)} %get-tuple-element.34), channel_id=1, source_target_pairs={{0,4},{4,8},{8,12},{1,5},{5,9},{9,13},{2,6},{6,10},{10,14},{3,7},{... | collective-permute-start | bytes 24584 | tf_op jit(solution)/shard_map/ppermute | solution.py:25
  117.8 28.8 %collective-permute-start.7 = (f32[4,1,512]{2,1,0:T(1,128)S(1)}, f32[4,1,512]{2,1,0:T(1,128)S(1)}, u32[]{:S(2)}, u32[]{:S(2)}) collective-permute-start(f32[4,1,512]{2,1,0:T(1,128)S(1)} %get-tuple-element.35), channel_id=1, source_target_pairs={{4,0},{8,4},{12,8},{5,1},{9,5},{13,9},{6,2},{10,6},{14,10},{7,3},{... | collective-permute-start | bytes 24584 | tf_op jit(solution)/shard_map/ppermute | solution.py:27
  153.4 65.1 %reduce-scatter.17.cloned.1.call-start = ((), (), s32[]{:S(2)}) async-start(), calls=%async_computation.12 | async-start | bytes 1310720 | tf_op jit(solution)/shard_map/reduce_scatter | solution.py:83
  153.5 33.4 %collective-permute-start.8 = (f32[4,1,512]{2,1,0:T(1,128)S(1)}, f32[4,1,512]{2,1,0:T(1,128)S(1)}, u32[]{:S(2)}, u32[]{:S(2)}) collective-permute-start(f32[4,1,512]{2,1,0:T(1,128)S(1)} %get-tuple-element.32), channel_id=1, source_target_pairs={{0,4},{4,8},{8,12},{1,5},{5,9},{9,13},{2,6},{6,10},{10,14},{3,7},{... | collective-permute-start | bytes 24584 | tf_op jit(solution)/shard_map/ppermute | solution.py:25
  156.9 30.0 %collective-permute-start.9 = (f32[4,1,512]{2,1,0:T(1,128)S(1)}, f32[4,1,512]{2,1,0:T(1,128)}, u32[]{:S(2)}, u32[]{:S(2)}) collective-permute-start(f32[4,1,512]{2,1,0:T(1,128)S(1)} %get-tuple-element.33), channel_id=1, source_target_pairs={{4,0},{8,4},{12,8},{5,1},{9,5},{13,9},{6,2},{10,6},{14,10},{7,3},{... | collective-permute-start | bytes 24584 | tf_op jit(solution)/shard_map/ppermute | solution.py:27
  193.1 65.5 %reduce-scatter.19.cloned.1.call-start = ((), (), s32[]{:S(2)}) async-start(), calls=%async_computation.13 | async-start | bytes 1310720 | tf_op jit(solution)/shard_map/reduce_scatter | solution.py:83
  194.0 32.2 %collective-permute-start.10 = (f32[4,1,512]{2,1,0:T(1,128)S(1)}, f32[4,1,512]{2,1,0:T(1,128)S(1)}, u32[]{:S(2)}, u32[]{:S(2)}) collective-permute-start(f32[4,1,512]{2,1,0:T(1,128)S(1)} %get-tuple-element.30), channel_id=1, source_target_pairs={{0,4},{4,8},{8,12},{1,5},{5,9},{9,13},{2,6},{6,10},{10,14},{3,7},{... | collective-permute-start | bytes 24584 | tf_op jit(solution)/shard_map/ppermute | solution.py:25
  197.4 28.8 %collective-permute-start.11 = (f32[4,1,512]{2,1,0:T(1,128)S(1)}, f32[4,1,512]{2,1,0:T(1,128)S(1)}, u32[]{:S(2)}, u32[]{:S(2)}) collective-permute-start(f32[4,1,512]{2,1,0:T(1,128)S(1)} %get-tuple-element.31), channel_id=1, source_target_pairs={{4,0},{8,4},{12,8},{5,1},{9,5},{13,9},{6,2},{10,6},{14,10},{7,3},{... | collective-permute-start | bytes 24584 | tf_op jit(solution)/shard_map/ppermute | solution.py:27
  233.1 63.9 %reduce-scatter.21.cloned.1.call-start = ((), (), s32[]{:S(2)}) async-start(), calls=%async_computation.14 | async-start | bytes 1310720 | tf_op jit(solution)/shard_map/reduce_scatter | solution.py:83
  233.2 33.2 %collective-permute-start.12 = (f32[4,1,512]{2,1,0:T(1,128)S(1)}, f32[4,1,512]{2,1,0:T(1,128)}, u32[]{:S(2)}, u32[]{:S(2)}) collective-permute-start(f32[4,1,512]{2,1,0:T(1,128)S(1)} %get-tuple-element.28), channel_id=1, source_target_pairs={{0,4},{4,8},{8,12},{1,5},{5,9},{9,13},{2,6},{6,10},{10,14},{3,7},{... | collective-permute-start | bytes 24584 | tf_op jit(solution)/shard_map/ppermute | solution.py:25
  237.1 29.2 %collective-permute-start.13 = (f32[4,1,512]{2,1,0:T(1,128)S(1)}, f32[4,1,512]{2,1,0:T(1,128)}, u32[]{:S(2)}, u32[]{:S(2)}) collective-permute-start(f32[4,1,512]{2,1,0:T(1,128)S(1)} %get-tuple-element.29), channel_id=1, source_target_pairs={{4,0},{8,4},{12,8},{5,1},{9,5},{13,9},{6,2},{10,6},{14,10},{7,3},{... | collective-permute-start | bytes 24584 | tf_op jit(solution)/shard_map/ppermute | solution.py:27
  271.5 64.2 %reduce-scatter.23.cloned.1.call-start = ((), (), s32[]{:S(2)}) async-start(), calls=%async_computation.15 | async-start | bytes 1310720 | tf_op jit(solution)/shard_map/reduce_scatter | solution.py:83
  272.5 32.3 %collective-permute-start.14 = (f32[4,1,512]{2,1,0:T(1,128)S(1)}, f32[4,1,512]{2,1,0:T(1,128)S(1)}, u32[]{:S(2)}, u32[]{:S(2)}) collective-permute-start(f32[4,1,512]{2,1,0:T(1,128)S(1)} %get-tuple-element.26), channel_id=1, source_target_pairs={{0,4},{4,8},{8,12},{1,5},{5,9},{9,13},{2,6},{6,10},{10,14},{3,7},{... | collective-permute-start | bytes 24584 | tf_op jit(solution)/shard_map/ppermute | solution.py:25
  275.8 28.9 %collective-permute-start.15 = (f32[4,1,512]{2,1,0:T(1,128)S(1)}, f32[4,1,512]{2,1,0:T(1,128)S(1)}, u32[]{:S(2)}, u32[]{:S(2)}) collective-permute-start(f32[4,1,512]{2,1,0:T(1,128)S(1)} %get-tuple-element.27), channel_id=1, source_target_pairs={{4,0},{8,4},{12,8},{5,1},{9,5},{13,9},{6,2},{10,6},{14,10},{7,3},{... | collective-permute-start | bytes 24584 | tf_op jit(solution)/shard_map/ppermute | solution.py:27
  (28 other events, 390.7 us)
Sparse Core Ops, SparseCore 0:
  36.7 23.0 reduce-scatter.8
  73.8 25.3 reduce-scatter.10
  113.6 25.3 reduce-scatter.12
  153.6 25.3 reduce-scatter.14
  193.2 25.3 reduce-scatter.16
  233.2 25.3 reduce-scatter.18
  271.6 25.3 reduce-scatter.20
  310.3 25.3 reduce-scatter.22
where the time goes:
time: 346 us; the launch traced here: 344 us
  blocking collectives  157 us (45%)
  waiting for transfers between devices  65.1 us (19%)
  matrix products  46.1 us (13%)
  starting transfers between devices  37.8 us (11%)
  between operations  14.8 us (4%)
  local copies, waits for them, and re-layouts  11.9 us (3%)
  other arithmetic  11.5 us (3%)
    psum x8, blocking collectives, shards(): zmean = lax.psum(jnp.sum(cap_var, axis=1), 'hour') / hours_all  102 us
    reduce_scatter x8, waiting for transfers between devices, shards(): lax.psum_scatter(partial_rows, 'reg', scatter_dimension=2, tiled=True)  64.9 us
    all_gather x7, blocking collectives, shards(): lax.all_gather(dual_var.astype(jnp.bfloat16), 'reg', axis=2, tiled=True)  46.4 us
    dot_general x8, matrix products, shards(): jnp.einsum('shr,rc->shc', dual_low, matrix, preferred_element_type=jnp.fl...  32.9 us
    ppermute x8, starting transfers between devices, with_halo(): lax.ppermute(tail, axis, [(i, (i + 1) % count) for i in range(ends)])  27.1 us
    dot_general x8, matrix products, shards(): jnp.einsum('shc,rc->shr', primal_ext.astype(jnp.bfloat16), matrix, prefer...  11.9 us
    ppermute x8, starting transfers between devices, with_halo(): lax.ppermute(head, axis, [((i + 1) % count, i) for i in range(ends)])  10.3 us
    psum x1, blocking collectives, shards(): sum_total, mass_total = lax.psum((node_sum, node_mass), 'scen')  8.32 us
  transfers between devices with their start and end apart: 24, of which 8 were waited for; matrix products, arithmetic and copies ran while one was open for 5% of the time, Pallas kernels for 0%

commit v1 on v0

v1 whole, which is shorter than its diff:
```python
import functools

import jax
import jax.numpy as jnp
from jax import lax
from jax.experimental import pallas as pl
from jax.experimental.pallas import tpu as pltpu
from jax.sharding import PartitionSpec as P

ITERS = 8
RAMP_WEIGHT = 0.5
PENALTY = 1.0
STEP_PRIMAL = 0.3
STEP_INVEST = 0.5
STEP_DUAL = 0.3
STEP_CAP = 0.05

F32 = jnp.float32
BF16 = jnp.bfloat16
COL_TILE = 256
VMEM_LIMIT = 24 * 1024 * 1024

IN_VMEM = pl.BlockSpec(memory_space=pltpu.VMEM)
IN_PLACE = pl.BlockSpec(memory_space=pl.ANY)


def call(body, name, outs, args, arg_specs=None, scratch=(), aliases=None, flops=0):
    bytes_moved = sum(a.size * a.dtype.itemsize for a in args)
    bytes_moved += sum(o.size * o.dtype.itemsize for o in outs)
    return pl.pallas_call(
        body,
        out_shape=tuple(outs),
        in_specs=arg_specs or [IN_VMEM] * len(args),
        out_specs=tuple(IN_VMEM for _ in outs),
        scratch_shapes=list(scratch),
        input_output_aliases=aliases or {},
        compiler_params=pltpu.CompilerParams(vmem_limit_bytes=VMEM_LIMIT),
        cost_estimate=pl.CostEstimate(flops=flops, bytes_accessed=bytes_moved, transcendentals=0),
        name=name,
    )(*args)


def shape(dims, dtype=F32):
    return jax.ShapeDtypeStruct(tuple(dims), dtype)


def tiles(width):
    return [slice(at, at + COL_TILE) for at in range(0, width, COL_TILE)]


def load_body(mine, *refs):
    (cost, cost_in, disp, disp_in, cap, cap_in, dual, dem,
     cost_out, prim_out, cap_out, dual_out, dem_out, up, down, sems) = refs
    core = lax.rem(lax.axis_index("reg"), 2)
    held = pl.ds(core * mine, mine)
    width = cost.shape[2]
    copies = []
    at = 0
    for src, twin, dst in ((cap, cap_in, cap_out), (disp, disp_in, prim_out), (cost, cost_in, cost_out)):
        copies.append(pltpu.make_async_copy(src.at[held], dst.at[:, :, pl.ds(0, width)], sems.at[at]))
        copies.append(pltpu.make_async_copy(twin, dst.at[:, :, pl.ds(width, width)], sems.at[at + 1]))
        at += 2
    for src, dst in ((dual, dual_out), (dem, dem_out)):
        copies.append(pltpu.make_async_copy(src.at[held], dst, sems.at[at]))
        at += 1
    for copy in copies:
        copy.start()
    for copy in copies:
        copy.wait()
    last = prim_out.shape[1] - 1
    for s in range(mine):
        for cols in tiles(2 * width):
            hour_sum = jnp.sum(cap_out[s, :, cols], axis=0, keepdims=True)
            up[pl.ds(s, 1), cols] = hour_sum
            down[pl.ds(s, 1), cols] = hour_sum
            up[pl.ds(mine + s, 1), cols] = prim_out[s, last:last + 1, cols]
            down[pl.ds(mine + s, 1), cols] = prim_out[s, 0:1, cols]


def primal_body(first, last, others, *refs):
    refs = list(refs)
    take = lambda count: [refs.pop(0) for _ in range(count)]
    matrix, cost, prim, cap, dual, up, down = take(7)
    if not first:
        dem, sent, carry = take(3)
        received = take(others)
    if last:
        keep, give = take(2)
    else:
        prim_out = take(1)[0]
    if not first:
        dual_out = take(1)[0]
    if last:
        rows_out = take(1)[0]
    else:
        sent_out, carry_out = take(2)
    ext_low = take(1)[0]
    mine, hours, width = prim.shape
    hour_place = lax.axis_index("hour")
    hour_ends = lax.axis_size("hour") - 1
    has_prev = (hour_place > 0).astype(F32)
    has_next = (hour_place < hour_ends).astype(F32)
    row = lax.broadcasted_iota(jnp.int32, (hours, COL_TILE), 0)
    half = width // 2
    for s in range(mine):
        multipliers = dual[s]
        if not first:
            image = sent[s].astype(F32)
            for other in received:
                image = image + other[s].astype(F32)
            multipliers = jnp.maximum(multipliers + STEP_DUAL * (dem[s] - image), 0.0)
            dual_out[s] = multipliers
        low = multipliers.astype(BF16)
        for cols in tiles(width):
            pulled = jnp.dot(low, matrix[:, cols], preferred_element_type=F32)
            x = prim[s, :, cols]
            before = up[mine + s:mine + s + 1, cols] * has_prev
            after = down[mine + s:mine + s + 1, cols] * has_next
            prev = jnp.where(row == 0, before, pltpu.roll(x, 1, 0))
            follow = jnp.where(row == hours - 1, after, pltpu.roll(x, hours - 1, 0))
            rough = 2.0 * x - prev - follow
            grad = cost[s, :, cols] + RAMP_WEIGHT * rough - pulled + cap[s, :, cols]
            new = jnp.maximum(x - STEP_PRIMAL * grad, 0.0)
            if last:
                if cols.start < half:
                    keep[s, :, cols] = new
                else:
                    give[s, :, cols.start - half:cols.stop - half] = new
            else:
                prim_out[s, :, cols] = new
            ext_low[:, cols] = (2.0 * new - x).astype(BF16)
        total = lax.dot_general(
            ext_low[...], matrix[...], (((1,), (1,)), ((), ())), preferred_element_type=F32
        )
        if not first:
            total = total + carry[s]
        if last:
            rows_out[s] = total
        else:
            low_sum = total.astype(BF16)
            sent_out[s] = low_sum
            carry_out[s] = total - low_sum.astype(F32)


def mean_and_invest(hours_all, parts, invest, const, s):
    sums = [p[s:s + 1, :] for p in parts]
    while len(sums) > 1:
        sums = [a + b for a, b in zip(sums[0::2], sums[1::2])]
    mean = sums[0] / hours_all
    old = invest[s]
    grad = const[s] + PENALTY * old - mean
    new = jnp.maximum(old - STEP_INVEST * grad, 0.0)
    return old, new


def cap_body(hours_all, parts_count, *refs):
    prim, new, cap, invest, const = refs[:5]
    parts = refs[5:5 + parts_count]
    cap_out, invest_out, up, down = refs[5 + parts_count:]
    mine, hours, width = prim.shape
    for s in range(mine):
        old_inv, new_inv = mean_and_invest(hours_all, parts, invest, const, s)
        invest_out[s] = new_inv
        limit = jnp.sum(2.0 * new_inv - old_inv, axis=0, keepdims=True)
        for cols in tiles(width):
            fresh = new[s, :, cols]
            ext = 2.0 * fresh - prim[s, :, cols]
            c = jnp.maximum(cap[s, :, cols] + STEP_CAP * (ext - limit[:, cols]), 0.0)
            cap_out[s, :, cols] = c
            hour_sum = jnp.sum(c, axis=0, keepdims=True)
            up[pl.ds(s, 1), cols] = hour_sum
            down[pl.ds(s, 1), cols] = hour_sum
            up[pl.ds(mine + s, 1), cols] = fresh[hours - 1:hours]
            down[pl.ds(mine + s, 1), cols] = fresh[0:1]


def invest_body(hours_all, parts_count, *refs):
    invest, const = refs[:2]
    parts = refs[2:2 + parts_count]
    out = refs[2 + parts_count]
    for s in range(invest.shape[0]):
        out[s] = mean_and_invest(hours_all, parts, invest, const, s)[1]


def rotate(x, axis, by):
    count = lax.axis_size(axis)
    return lax.ppermute(x, axis, [(i, (i + by) % count) for i in range(count)])


def hour_exchange(up, down, mine):
    count = lax.axis_size("hour")
    from_prev = rotate(up, "hour", 1)
    from_next = rotate(down, "hour", count - 1)
    own = up[:mine]
    if count == 4:
        far = rotate(own, "hour", 2)
        return from_prev, from_next, (up, far, from_prev, from_next)
    return from_prev, from_next, (lax.psum(own, "hour"),)


def shards(
    cost_rate,
    invest_cost,
    tile,
    tile_mask,
    demand,
    dispatch,
    dual,
    cap_dual,
    capacity,
    multiplier,
    consensus,
    scen_weight,
    node_of,
):
    reg_count = lax.axis_size("reg")
    chips = reg_count // 2
    place = lax.axis_index("reg")
    core = place % 2
    chip = place // 2
    nscen, hours, width = dispatch.shape
    rows = dual.shape[2]
    mine = nscen // 2
    hours_all = float(hours * lax.axis_size("hour"))
    twin = [(i, i ^ 1) for i in range(reg_count)]

    def swap(x):
        return lax.ppermute(x, "reg", twin)

    def held(x):
        return lax.dynamic_slice_in_dim(x, core * mine, mine, 0)

    def given(x):
        return lax.dynamic_slice_in_dim(x, (1 - core) * mine, mine, 0)

    def join(kept, got):
        first = jnp.where(core == 0, kept, got)
        second = jnp.where(core == 0, got, kept)
        return jnp.concatenate([first, second], axis=0)

    cap_in = swap(given(cap_dual))
    disp_in = swap(given(dispatch))
    cost_in = swap(given(cost_rate))
    matrix_own = tile[0] * tile_mask[0].astype(BF16)
    matrix = jnp.concatenate([matrix_own, swap(matrix_own)], axis=1)
    small = jnp.concatenate([invest_cost[None] + multiplier - PENALTY * consensus, capacity], axis=1)
    small_all = jnp.concatenate([held(small), swap(given(small))], axis=2)
    sections = capacity.shape[1]
    const, invest = small_all[:, :sections], small_all[:, sections:]

    full = shape((mine, hours, 2 * width))
    dual_like = shape((mine, hours, rows))
    message = shape((2 * mine, 2 * width))
    cost, prim, cap, dual_var, dem, up, down = call(
        functools.partial(load_body, mine),
        "load",
        (full, full, full, dual_like, dual_like, message, message),
        (cost_rate, cost_in, dispatch, disp_in, cap_dual, cap_in, dual, demand),
        arg_specs=[IN_PLACE] * 8,
        scratch=(pltpu.SemaphoreType.DMA((8,)),),
    )
    flops = 4 * mine * hours * rows * 2 * width
    sent = carry = None
    received = ()
    for step in range(ITERS):
        first, last = step == 0, step + 1 == ITERS
        from_prev, from_next, parts = hour_exchange(up, down, mine)
        args = [matrix, cost, prim, cap, dual_var, from_prev, from_next]
        outs = [shape((mine, hours, width))] * 2 if last else [full]
        aliases = {}
        if not first:
            args += [dem, sent, carry, *received]
            aliases[4] = len(outs)
            outs += [dual_like]
        if last:
            outs += [dual_like]
        else:
            if not first:
                aliases[9] = len(outs) + 1
            outs += [shape(dual_like.shape, BF16), dual_like]
        got = list(
            call(
                functools.partial(primal_body, first, last, chips - 1),
                f"primal_{step}",
                outs,
                args,
                scratch=(pltpu.VMEM((hours, 2 * width), BF16),),
                aliases=aliases,
                flops=flops,
            )
        )
        if last:
            keep, give = got.pop(0), got.pop(0)
        else:
            fresh = got.pop(0)
        if not first:
            dual_var = got.pop(0)
        if last:
            row_sums = got.pop(0)
            (invest,) = call(
                functools.partial(invest_body, hours_all, len(parts)),
                "invest_last",
                (shape(invest.shape),),
                (invest, const, *parts),
            )
        else:
            sent, carry = got
            received = [rotate(sent, "reg", 2 * d) for d in range(1, chips)]
            cap, invest, up, down = call(
                functools.partial(cap_body, hours_all, len(parts)),
                f"cap_{step}",
                (full, shape(invest.shape), message, message),
                (prim, fresh, cap, invest, const, *parts),
                aliases={2: 0, 3: 1},
            )
            prim = fresh

    dispatch_out = join(keep, swap(give))

    chip_rows = rows // chips

    def rows_of(x, c):
        return lax.dynamic_slice_in_dim(x, (c % chips) * chip_rows, chip_rows, 2)

    image = rows_of(row_sums, chip)
    for d in range(1, chips):
        image = image + rotate(rows_of(row_sums, chip + d), "reg", 2 * d)
    dual_last = jnp.maximum(
        rows_of(dual_var, chip) + STEP_DUAL * (rows_of(dem, chip) - image), 0.0
    )
    own_rows = chip_rows // 2
    dual_keep = lax.dynamic_slice_in_dim(dual_last, core * own_rows, own_rows, 2)
    dual_give = lax.dynamic_slice_in_dim(dual_last, (1 - core) * own_rows, own_rows, 2)
    dual_out = join(dual_keep, swap(dual_give))

    capacity_out = join(invest[:, :, :width], swap(invest[:, :, width:]))

    scen_count = lax.axis_size("scen")
    node_count = node_of.shape[1] * scen_count // 2
    node_ids = jnp.arange(node_count, dtype=jnp.int32)
    one_hot = (node_of[:, :, None] == node_ids[None, None, :]).astype(F32)
    weights = one_hot * scen_weight[None, :, None]
    node_sum = jnp.sum(
        weights[:, :, :, None] * jnp.transpose(capacity_out, (1, 0, 2))[:, :, None, :], axis=1
    )
    node_mass = jnp.sum(weights, axis=1)
    packed = jnp.concatenate(
        [node_sum, jnp.broadcast_to(node_mass[:, :, None], node_mass.shape + (128,))], axis=2
    )
    if scen_count == 2:
        packed = packed + rotate(packed, "scen", 1)
    else:
        packed = lax.psum(packed, "scen")
    sum_total, mass_total = packed[:, :, :width], packed[:, :, width:width + 1]
    average = sum_total / (mass_total + (mass_total <= 0.0).astype(F32))
    spread_back = jnp.sum(one_hot[:, :, :, None] * average[:, None, :, :], axis=2)
    multiplier_out = multiplier + PENALTY * (capacity_out - jnp.transpose(spread_back, (1, 0, 2)))
    return (dispatch_out, dual_out, capacity_out, multiplier_out)


def solution(mesh):
    placed = (
        P("scen", "hour", "reg"),
        P(None, "reg"),
        P("hour", None, "reg"),
        P("hour", None, "reg"),
        P("scen", "hour", None),
        P("scen", "hour", "reg"),
        P("scen", "hour", None),
        P("scen", "hour", "reg"),
        P("scen", None, "reg"),
        P("scen", None, "reg"),
        P("scen", None, "reg"),
        P("scen"),
        P(None, "scen"),
    )
    return jax.shard_map(
        shards,
        mesh=mesh,
        in_specs=placed,
        out_specs=(
            P("scen", "hour", "reg"),
            P("scen", "hour", "reg"),
            P("scen", None, "reg"),
            P("scen", None, "reg"),
        ),
        check_vma=False,
    )
```

time: 346 us -> 147 us (0.42)
  blocking collectives: 157 us -> 0 us
  matrix products: 46.1 us -> 0 us
  waiting for transfers between devices: 65.1 us -> 36.9 us
  starting transfers between devices: 37.8 us -> 61.3 us
  Pallas kernels: 0 us -> 18.1 us
  between operations: 14.8 us -> 1.09 us
  local copies, waits for them, and re-layouts: 11.9 us -> 21.6 us
  other arithmetic: 11.5 us -> 7.36 us
    psum x9 -> x0, blocking collectives: 111 us -> none  [the longest x8 102 us: shards(): zmean = lax.psum(jnp.sum(cap_var, axis=1), 'hour') / hours_all]
    reduce_scatter x8 -> x0, waiting for transfers between devices: 64.9 us -> none  [shards(): lax.psum_scatter(partial_rows, 'reg', scatter_dimension=2, tiled=True)]
    all_gather x7 -> x0, blocking collectives: 46.4 us -> none  [shards(): lax.all_gather(dual_var.astype(jnp.bfloat16), 'reg', axis=2, tiled=True)]
    dot_general x19 -> x0, matrix products: 46.1 us -> none  [the longest x8 32.9 us: shards(): jnp.einsum('shr,rc->shc', dual_low, matrix, preferred_element_type=jnp.fl...]
    ppermute x16 -> x41, waiting for transfers between devices: 0.04 us -> 36.9 us  [the longest x33 36.1 us: rotate(): return lax.ppermute(x, axis, [(i, (i + by) % count) for i in range(count)])]
    ppermute x16 -> x41, starting transfers between devices: 37.5 us -> 61.3 us  [the longest x33 59.8 us: rotate(): return lax.ppermute(x, axis, [(i, (i + by) % count) for i in range(count)])]
    pallas_call x0 -> x17, Pallas kernels: none -> 18.1 us  [call(): pl.pallas_call(body, out_shape=tuple(outs), in_specs=arg_specs or [IN_VME...]
    unnamed x58 -> x68, local copies, waits for them, and re-layouts: 5.85 us -> 17.5 us
  transfers between devices with their start and end apart: 24 -> 41, of which waited for: 8 -> 22; matrix products, arithmetic and copies ran while one was open for 5% -> 5% of each run, Pallas kernels for 0% -> 5%
where the time goes in v1:
time: 147 us; the launch traced here: 146 us
  starting transfers between devices  61.3 us (42%)
  waiting for transfers between devices  36.9 us (25%)
  local copies, waits for them, and re-layouts  21.6 us (15%)
  Pallas kernels  18.1 us (12%)
  other arithmetic  7.36 us (5%)
    ppermute x33, starting transfers between devices, rotate(): return lax.ppermute(x, axis, [(i, (i + by) % count) for i in range(count)])  59.8 us
    ppermute x33, waiting for transfers between devices, rotate(): return lax.ppermute(x, axis, [(i, (i + by) % count) for i in range(count)])  36.1 us
    pallas_call x17, Pallas kernels, call(): pl.pallas_call(body, out_shape=tuple(outs), in_specs=arg_specs or [IN_VME...  18.1 us
    unnamed x68, local copies, waits for them, and re-layouts  17.5 us
    dynamic_slice x3, local copies, waits for them, and re-layouts, given(): return lax.dynamic_slice_in_dim(x, (1 - core) * mine, mine, 0)  3.14 us
  transfers between devices with their start and end apart: 41, of which 22 were waited for; matrix products, arithmetic and copies ran while one was open for 5% of the time, Pallas kernels for 5%

profile of v1, /device:TPU:0, one launch (start us, length us, event | category | flops | bytes accessed | tf_op | source)
XLA Modules:
  0.0 146.3 jit_solution(8893803967588582644)
XLA Ops:
  0.7 2.1 %constant_dynamic-slice_fusion.4 = f32[2,168,512]{2,1,0:T(8,128)} fusion(f32[4,168,512]{2,1,0:T(8,128)} %refs_0_.1, s32[]{:T(128)S(6)} %select_n.84), kind=kLoop, calls=%fused_computation.38 | loop fusion | bytes 1376260 | tf_op jit(solution)/shard_map/dynamic_slice | solution.py:234
  17.7 3.0 %collective-permute-start.4 = (f32[4,1024]{1,0:T(4,128)S(1)}, f32[4,1024]{1,0:T(4,128)S(1)}, u32[]{:S(2)}, u32[]{:S(2)}) collective-permute-start(f32[4,1024]{1,0:T(4,128)S(1)} %get-tuple-element.74.refs_5_), channel_id=1, source_target_pairs={{0,4},{4,8},{8,12},{12,0},{1,5},{5,9},{9,13},{13,1},{2,6},{6,10},{... | collective-permute-start | bytes 49160 | tf_op jit(solution)/shard_map/ppermute | solution.py:187
  20.7 2.1 %collective-permute-start.5 = (f32[4,1024]{1,0:T(4,128)S(1)}, f32[4,1024]{1,0:T(4,128)S(1)}, u32[]{:S(2)}, u32[]{:S(2)}) collective-permute-start(f32[4,1024]{1,0:T(4,128)S(1)} %get-tuple-element.75), channel_id=1, source_target_pairs={{0,12},{4,0},{8,4},{12,8},{1,13},{5,1},{9,5},{13,9},{2,14},{6,2},{... | collective-permute-start | bytes 49160 | tf_op jit(solution)/shard_map/ppermute | solution.py:187
  27.7 2.4 %collective-permute-start.7 = (f32[2,1024]{1,0:T(2,128)S(1)}, f32[2,1024]{1,0:T(2,128)S(1)}, u32[]{:S(2)}, u32[]{:S(2)}) collective-permute-start(f32[2,1024]{1,0:T(2,128)S(1)} %slice.44), channel_id=1, source_target_pairs={{0,8},{4,12},{8,0},{12,4},{1,9},{5,13},{9,1},{13,5},{2,10},{6,14},... | collective-permute-start | bytes 24584 | tf_op jit(solution)/shard_map/ppermute | solution.py:187
  30.2 2.2 %collective-permute-done.7.refs_6_ = f32[2,1024]{1,0:T(2,128)S(1)} collective-permute-done((f32[2,1024]{1,0:T(2,128)S(1)}, f32[2,1024]{1,0:T(2,128)S(1)}, u32[]{:S(2)}, u32[]{:S(2)}) %collective-permute-start.7) | collective-permute-done | bytes 8224 | tf_op jit(solution)/shard_map/ppermute | solution.py:187
  34.7 2.4 %collective-permute-start.9 = (f32[4,1024]{1,0:T(4,128)S(1)}, f32[4,1024]{1,0:T(4,128)S(1)}, u32[]{:S(2)}, u32[]{:S(2)}) collective-permute-start(f32[4,1024]{1,0:T(4,128)S(1)} %get-tuple-element.79), channel_id=1, source_target_pairs={{0,12},{4,0},{8,4},{12,8},{1,13},{5,1},{9,5},{13,9},{2,14},{6,2},{... | collective-permute-start | bytes 49160 | tf_op jit(solution)/shard_map/ppermute | solution.py:187
  40.8 2.4 %collective-permute-start.11 = (f32[2,1024]{1,0:T(2,128)S(1)}, f32[2,1024]{1,0:T(2,128)S(1)}, u32[]{:S(2)}, u32[]{:S(2)}) collective-permute-start(f32[2,1024]{1,0:T(2,128)S(1)} %slice.45), channel_id=1, source_target_pairs={{0,8},{4,12},{8,0},{12,4},{1,9},{5,13},{9,1},{13,5},{2,10},{6,14},... | collective-permute-start | bytes 24584 | tf_op jit(solution)/shard_map/ppermute | solution.py:187
  43.1 2.2 %collective-permute-done.11.refs_6_ = f32[2,1024]{1,0:T(2,128)S(1)} collective-permute-done((f32[2,1024]{1,0:T(2,128)S(1)}, f32[2,1024]{1,0:T(2,128)S(1)}, u32[]{:S(2)}, u32[]{:S(2)}) %collective-permute-start.11) | collective-permute-done | bytes 8224 | tf_op jit(solution)/shard_map/ppermute | solution.py:187
  47.6 2.5 %collective-permute-start.13 = (f32[4,1024]{1,0:T(4,128)S(1)}, f32[4,1024]{1,0:T(4,128)S(1)}, u32[]{:S(2)}, u32[]{:S(2)}) collective-permute-start(f32[4,1024]{1,0:T(4,128)S(1)} %get-tuple-element.88), channel_id=1, source_target_pairs={{0,12},{4,0},{8,4},{12,8},{1,13},{5,1},{9,5},{13,9},{2,14},{6,2},{... | collective-permute-start | bytes 49160 | tf_op jit(solution)/shard_map/ppermute | solution.py:187
  54.7 2.6 %collective-permute-start.15 = (f32[2,1024]{1,0:T(2,128)S(1)}, f32[2,1024]{1,0:T(2,128)S(1)}, u32[]{:S(2)}, u32[]{:S(2)}) collective-permute-start(f32[2,1024]{1,0:T(2,128)S(1)} %slice.46), channel_id=1, source_target_pairs={{0,8},{4,12},{8,0},{12,4},{1,9},{5,13},{9,1},{13,5},{2,10},{6,14},... | collective-permute-start | bytes 24584 | tf_op jit(solution)/shard_map/ppermute | solution.py:187
  61.8 2.4 %collective-permute-start.17 = (f32[4,1024]{1,0:T(4,128)S(1)}, f32[4,1024]{1,0:T(4,128)S(1)}, u32[]{:S(2)}, u32[]{:S(2)}) collective-permute-start(f32[4,1024]{1,0:T(4,128)S(1)} %get-tuple-element.96), channel_id=1, source_target_pairs={{0,12},{4,0},{8,4},{12,8},{1,13},{5,1},{9,5},{13,9},{2,14},{6,2},{... | collective-permute-start | bytes 49160 | tf_op jit(solution)/shard_map/ppermute | solution.py:187
  67.7 2.6 %collective-permute-start.19 = (f32[2,1024]{1,0:T(2,128)S(1)}, f32[2,1024]{1,0:T(2,128)S(1)}, u32[]{:S(2)}, u32[]{:S(2)}) collective-permute-start(f32[2,1024]{1,0:T(2,128)S(1)} %slice.47), channel_id=1, source_target_pairs={{0,8},{4,12},{8,0},{12,4},{1,9},{5,13},{9,1},{13,5},{2,10},{6,14},... | collective-permute-start | bytes 24584 | tf_op jit(solution)/shard_map/ppermute | solution.py:187
  74.7 2.6 %collective-permute-start.21 = (f32[4,1024]{1,0:T(4,128)S(1)}, f32[4,1024]{1,0:T(4,128)S(1)}, u32[]{:S(2)}, u32[]{:S(2)}) collective-permute-start(f32[4,1024]{1,0:T(4,128)S(1)} %get-tuple-element.104), channel_id=1, source_target_pairs={{0,12},{4,0},{8,4},{12,8},{1,13},{5,1},{9,5},{13,9},{2,14},{6,2},{... | collective-permute-start | bytes 49160 | tf_op jit(solution)/shard_map/ppermute | solution.py:187
  81.8 2.6 %collective-permute-start.23 = (f32[2,1024]{1,0:T(2,128)S(1)}, f32[2,1024]{1,0:T(2,128)S(1)}, u32[]{:S(2)}, u32[]{:S(2)}) collective-permute-start(f32[2,1024]{1,0:T(2,128)S(1)} %slice.48), channel_id=1, source_target_pairs={{0,8},{4,12},{8,0},{12,4},{1,9},{5,13},{9,1},{13,5},{2,10},{6,14},... | collective-permute-start | bytes 24584 | tf_op jit(solution)/shard_map/ppermute | solution.py:187
  84.4 2.0 %collective-permute-done.23.refs_6_ = f32[2,1024]{1,0:T(2,128)S(1)} collective-permute-done((f32[2,1024]{1,0:T(2,128)S(1)}, f32[2,1024]{1,0:T(2,128)S(1)}, u32[]{:S(2)}, u32[]{:S(2)}) %collective-permute-start.23) | collective-permute-done | bytes 8224 | tf_op jit(solution)/shard_map/ppermute | solution.py:187
  88.9 2.4 %collective-permute-start.25 = (f32[4,1024]{1,0:T(4,128)S(1)}, f32[4,1024]{1,0:T(4,128)S(1)}, u32[]{:S(2)}, u32[]{:S(2)}) collective-permute-start(f32[4,1024]{1,0:T(4,128)S(1)} %get-tuple-element.112), channel_id=1, source_target_pairs={{0,12},{4,0},{8,4},{12,8},{1,13},{5,1},{9,5},{13,9},{2,14},{6,2},{... | collective-permute-start | bytes 49160 | tf_op jit(solution)/shard_map/ppermute | solution.py:187
  95.0 2.6 %collective-permute-start.27 = (f32[2,1024]{1,0:T(2,128)S(1)}, f32[2,1024]{1,0:T(2,128)S(1)}, u32[]{:S(2)}, u32[]{:S(2)}) collective-permute-start(f32[2,1024]{1,0:T(2,128)S(1)} %slice.49), channel_id=1, source_target_pairs={{0,8},{4,12},{8,0},{12,4},{1,9},{5,13},{9,1},{13,5},{2,10},{6,14},... | collective-permute-start | bytes 24584 | tf_op jit(solution)/shard_map/ppermute | solution.py:187
  97.6 2.1 %collective-permute-done.27.refs_6_ = f32[2,1024]{1,0:T(2,128)S(1)} collective-permute-done((f32[2,1024]{1,0:T(2,128)S(1)}, f32[2,1024]{1,0:T(2,128)S(1)}, u32[]{:S(2)}, u32[]{:S(2)}) %collective-permute-start.27) | collective-permute-done | bytes 8224 | tf_op jit(solution)/shard_map/ppermute | solution.py:187
  102.1 2.3 %collective-permute-start.29 = (f32[4,1024]{1,0:T(4,128)S(1)}, f32[4,1024]{1,0:T(4,128)S(1)}, u32[]{:S(2)}, u32[]{:S(2)}) collective-permute-start(f32[4,1024]{1,0:T(4,128)S(1)} %get-tuple-element.120), channel_id=1, source_target_pairs={{0,12},{4,0},{8,4},{12,8},{1,13},{5,1},{9,5},{13,9},{2,14},{6,2},{... | collective-permute-start | bytes 49160 | tf_op jit(solution)/shard_map/ppermute | solution.py:187
  110.2 3.6 %collective-permute-start.33 = (f32[4,1024]{1,0:T(4,128)S(1)}, f32[4,1024]{1,0:T(4,128)S(1)}, u32[]{:S(2)}, u32[]{:S(2)}) collective-permute-start(f32[4,1024]{1,0:T(4,128)S(1)} %get-tuple-element.128), channel_id=1, source_target_pairs={{0,12},{4,0},{8,4},{12,8},{1,13},{5,1},{9,5},{13,9},{2,14},{6,2},{... | collective-permute-start | bytes 49160 | tf_op jit(solution)/shard_map/ppermute | solution.py:187
  113.8 4.5 %collective-permute-done.38.refs_3_ = f32[2,1024]{1,0:T(2,128)S(1)} collective-permute-done((f32[2,1024]{1,0:T(2,128)S(1)}, f32[2,1024]{1,0:T(2,128)S(1)}, u32[]{:S(2)}, u32[]{:S(2)}) %collective-permute-start.38) | collective-permute-done | bytes 8224 | tf_op jit(solution)/shard_map/ppermute | solution.py:187
  127.0 3.4 %collective-permute-done.34.refs_10_ = bf16[2,168,256]{2,1,0:T(8,128)(2,1)S(1)} collective-permute-done((bf16[2,168,256]{2,1,0:T(8,128)(2,1)S(1)}, bf16[2,168,256]{2,1,0:T(8,128)(2,1)S(1)}, u32[]{:S(2)}, u32[]{:S(2)}) %collective-permute-start.34) | collective-permute-done | bytes 172064 | tf_op jit(solution)/shard_map/ppermute | solution.py:187
  134.7 2.0 %primal_7.1 = (f32[2,168,512]{2,1,0:T(8,128)S(1)}, f32[2,168,512]{2,1,0:T(8,128)}, f32[2,168,256]{2,1,0:T(8,128)S(1)}, f32[2,168,256]{2,1,0:T(8,128)S(1)}) custom-call(bf16[256,1024]{1,0:T(8,128)(2,1)S(1)} %pad_maximum_fusion.1.refs_0_, f32[2,168,1024]{2,1,0:T(8,128)S(1)} %get-tuple-element.70.refs_1_, ...), custom_call_target="tpu_custom_call", output_to_operand_aliasing={{2}: (4, {})} | custom-call | flops 352321536 | bytes 8126464 | tf_op jit(solution)/shard_map/primal_7/pallas_call | solution.py:30
  138.4 3.8 %collective-permute-done.36 = f32[2,168,128]{2,1,0:T(8,128)S(1)} collective-permute-done((f32[2,168,128]{2,1,0:T(8,128)S(1)}, f32[2,168,128]{2,1,0:T(8,128)S(1)}, u32[]{:S(2)}, u32[]{:S(2)}) %collective-permute-start.36) | collective-permute-done | bytes 172064 | tf_op jit(solution)/shard_map/ppermute | solution.py:187
  (181 shorter events, 82.2 us)
Async XLA Ops:
  5.7 17.1 %collective-permute-start = (bf16[256,512]{1,0:T(8,128)(2,1)}, bf16[256,512]{1,0:T(8,128)(2,1)}, u32[]{:S(2)}, u32[]{:S(2)}) collective-permute-start(bf16[256,512]{1,0:T(8,128)(2,1)} %multiply_bitcast_fusion), channel_id=1, source_target_pairs={{0,1},{1,0},{2,3},{3,2},{4,5},{5,4},{6,7},{7,6},{8,9},{9,8},{10,11... | collective-permute-start | bytes 786440 | tf_op jit(solution)/shard_map/ppermute | solution.py:228
  17.7 6.9 %collective-permute-start.4 = (f32[4,1024]{1,0:T(4,128)S(1)}, f32[4,1024]{1,0:T(4,128)S(1)}, u32[]{:S(2)}, u32[]{:S(2)}) collective-permute-start(f32[4,1024]{1,0:T(4,128)S(1)} %get-tuple-element.74.refs_5_), channel_id=1, source_target_pairs={{0,4},{4,8},{8,12},{12,0},{1,5},{5,9},{9,13},{13,1},{2,6},{6,10},{... | collective-permute-start | bytes 49160 | tf_op jit(solution)/shard_map/ppermute | solution.py:187
  26.0 12.9 %collective-permute-start.10 = (bf16[2,168,256]{2,1,0:T(8,128)(2,1)S(1)}, bf16[2,168,256]{2,1,0:T(8,128)(2,1)S(1)}, u32[]{:S(2)}, u32[]{:S(2)}) collective-permute-start(bf16[2,168,256]{2,1,0:T(8,128)(2,1)S(1)} %get-tuple-element.81.refs_8_), channel_id=1, source_target_pairs={{0,2},{1,3},{2,0},{3,1},{4,6},{5,7},{6,4},{7,5},{8,10},{9,11},{10,... | collective-permute-start | bytes 516104 | tf_op jit(solution)/shard_map/ppermute | solution.py:187
  27.7 4.6 %collective-permute-start.7 = (f32[2,1024]{1,0:T(2,128)S(1)}, f32[2,1024]{1,0:T(2,128)S(1)}, u32[]{:S(2)}, u32[]{:S(2)}) collective-permute-start(f32[2,1024]{1,0:T(2,128)S(1)} %slice.44), channel_id=1, source_target_pairs={{0,8},{4,12},{8,0},{12,4},{1,9},{5,13},{9,1},{13,5},{2,10},{6,14},... | collective-permute-start | bytes 24584 | tf_op jit(solution)/shard_map/ppermute | solution.py:187
  33.2 5.6 %collective-permute-start.8 = (f32[4,1024]{1,0:T(4,128)S(1)}, f32[4,1024]{1,0:T(4,128)S(1)}, u32[]{:S(2)}, u32[]{:S(2)}) collective-permute-start(f32[4,1024]{1,0:T(4,128)S(1)} %get-tuple-element.78.refs_5_), channel_id=1, source_target_pairs={{0,4},{4,8},{8,12},{12,0},{1,5},{5,9},{9,13},{13,1},{2,6},{6,10},{... | collective-permute-start | bytes 49160 | tf_op jit(solution)/shard_map/ppermute | solution.py:187
  40.2 11.6 %collective-permute-start.14 = (bf16[2,168,256]{2,1,0:T(8,128)(2,1)S(1)}, bf16[2,168,256]{2,1,0:T(8,128)(2,1)S(1)}, u32[]{:S(2)}, u32[]{:S(2)}) collective-permute-start(bf16[2,168,256]{2,1,0:T(8,128)(2,1)S(1)} %get-tuple-element.89.refs_8_), channel_id=1, source_target_pairs={{0,2},{1,3},{2,0},{3,1},{4,6},{5,7},{6,4},{7,5},{8,10},{9,11},{10,... | collective-permute-start | bytes 516104 | tf_op jit(solution)/shard_map/ppermute | solution.py:187
  40.8 4.5 %collective-permute-start.11 = (f32[2,1024]{1,0:T(2,128)S(1)}, f32[2,1024]{1,0:T(2,128)S(1)}, u32[]{:S(2)}, u32[]{:S(2)}) collective-permute-start(f32[2,1024]{1,0:T(2,128)S(1)} %slice.45), channel_id=1, source_target_pairs={{0,8},{4,12},{8,0},{12,4},{1,9},{5,13},{9,1},{13,5},{2,10},{6,14},... | collective-permute-start | bytes 24584 | tf_op jit(solution)/shard_map/ppermute | solution.py:187
  46.2 5.6 %collective-permute-start.12 = (f32[4,1024]{1,0:T(4,128)S(1)}, f32[4,1024]{1,0:T(4,128)S(1)}, u32[]{:S(2)}, u32[]{:S(2)}) collective-permute-start(f32[4,1024]{1,0:T(4,128)S(1)} %get-tuple-element.87.refs_5_), channel_id=1, source_target_pairs={{0,4},{4,8},{8,12},{12,0},{1,5},{5,9},{9,13},{13,1},{2,6},{6,10},{... | collective-permute-start | bytes 49160 | tf_op jit(solution)/shard_map/ppermute | solution.py:187
  53.1 12.8 %collective-permute-start.18 = (bf16[2,168,256]{2,1,0:T(8,128)(2,1)S(1)}, bf16[2,168,256]{2,1,0:T(8,128)(2,1)S(1)}, u32[]{:S(2)}, u32[]{:S(2)}) collective-permute-start(bf16[2,168,256]{2,1,0:T(8,128)(2,1)S(1)} %get-tuple-element.97.refs_8_), channel_id=1, source_target_pairs={{0,2},{1,3},{2,0},{3,1},{4,6},{5,7},{6,4},{7,5},{8,10},{9,11},{10,... | collective-permute-start | bytes 516104 | tf_op jit(solution)/shard_map/ppermute | solution.py:187
  54.7 4.6 %collective-permute-start.15 = (f32[2,1024]{1,0:T(2,128)S(1)}, f32[2,1024]{1,0:T(2,128)S(1)}, u32[]{:S(2)}, u32[]{:S(2)}) collective-permute-start(f32[2,1024]{1,0:T(2,128)S(1)} %slice.46), channel_id=1, source_target_pairs={{0,8},{4,12},{8,0},{12,4},{1,9},{5,13},{9,1},{13,5},{2,10},{6,14},... | collective-permute-start | bytes 24584 | tf_op jit(solution)/shard_map/ppermute | solution.py:187
  60.2 5.7 %collective-permute-start.16 = (f32[4,1024]{1,0:T(4,128)S(1)}, f32[4,1024]{1,0:T(4,128)S(1)}, u32[]{:S(2)}, u32[]{:S(2)}) collective-permute-start(f32[4,1024]{1,0:T(4,128)S(1)} %get-tuple-element.95.refs_5_), channel_id=1, source_target_pairs={{0,4},{4,8},{8,12},{12,0},{1,5},{5,9},{9,13},{13,1},{2,6},{6,10},{... | collective-permute-start | bytes 49160 | tf_op jit(solution)/shard_map/ppermute | solution.py:187
  67.2 11.5 %collective-permute-start.22 = (bf16[2,168,256]{2,1,0:T(8,128)(2,1)S(1)}, bf16[2,168,256]{2,1,0:T(8,128)(2,1)S(1)}, u32[]{:S(2)}, u32[]{:S(2)}) collective-permute-start(bf16[2,168,256]{2,1,0:T(8,128)(2,1)S(1)} %get-tuple-element.105.refs_8_), channel_id=1, source_target_pairs={{0,2},{1,3},{2,0},{3,1},{4,6},{5,7},{6,4},{7,5},{8,10},{9,11},{10,... | collective-permute-start | bytes 516104 | tf_op jit(solution)/shard_map/ppermute | solution.py:187
  73.1 5.7 %collective-permute-start.20 = (f32[4,1024]{1,0:T(4,128)S(1)}, f32[4,1024]{1,0:T(4,128)S(1)}, u32[]{:S(2)}, u32[]{:S(2)}) collective-permute-start(f32[4,1024]{1,0:T(4,128)S(1)} %get-tuple-element.103.refs_5_), channel_id=1, source_target_pairs={{0,4},{4,8},{8,12},{12,0},{1,5},{5,9},{9,13},{13,1},{2,6},{6,10},{... | collective-permute-start | bytes 49160 | tf_op jit(solution)/shard_map/ppermute | solution.py:187
  80.1 13.0 %collective-permute-start.26 = (bf16[2,168,256]{2,1,0:T(8,128)(2,1)S(1)}, bf16[2,168,256]{2,1,0:T(8,128)(2,1)S(1)}, u32[]{:S(2)}, u32[]{:S(2)}) collective-permute-start(bf16[2,168,256]{2,1,0:T(8,128)(2,1)S(1)} %get-tuple-element.113.refs_8_), channel_id=1, source_target_pairs={{0,2},{1,3},{2,0},{3,1},{4,6},{5,7},{6,4},{7,5},{8,10},{9,11},{10,... | collective-permute-start | bytes 516104 | tf_op jit(solution)/shard_map/ppermute | solution.py:187
  81.8 4.6 %collective-permute-start.23 = (f32[2,1024]{1,0:T(2,128)S(1)}, f32[2,1024]{1,0:T(2,128)S(1)}, u32[]{:S(2)}, u32[]{:S(2)}) collective-permute-start(f32[2,1024]{1,0:T(2,128)S(1)} %slice.48), channel_id=1, source_target_pairs={{0,8},{4,12},{8,0},{12,4},{1,9},{5,13},{9,1},{13,5},{2,10},{6,14},... | collective-permute-start | bytes 24584 | tf_op jit(solution)/shard_map/ppermute | solution.py:187
  87.2 5.8 %collective-permute-start.24 = (f32[4,1024]{1,0:T(4,128)S(1)}, f32[4,1024]{1,0:T(4,128)S(1)}, u32[]{:S(2)}, u32[]{:S(2)}) collective-permute-start(f32[4,1024]{1,0:T(4,128)S(1)} %get-tuple-element.111.refs_5_), channel_id=1, source_target_pairs={{0,4},{4,8},{8,12},{12,0},{1,5},{5,9},{9,13},{13,1},{2,6},{6,10},{... | collective-permute-start | bytes 49160 | tf_op jit(solution)/shard_map/ppermute | solution.py:187
  94.4 11.7 %collective-permute-start.30 = (bf16[2,168,256]{2,1,0:T(8,128)(2,1)S(1)}, bf16[2,168,256]{2,1,0:T(8,128)(2,1)S(1)}, u32[]{:S(2)}, u32[]{:S(2)}) collective-permute-start(bf16[2,168,256]{2,1,0:T(8,128)(2,1)S(1)} %get-tuple-element.121.refs_8_), channel_id=1, source_target_pairs={{0,2},{1,3},{2,0},{3,1},{4,6},{5,7},{6,4},{7,5},{8,10},{9,11},{10,... | collective-permute-start | bytes 516104 | tf_op jit(solution)/shard_map/ppermute | solution.py:187
  95.0 4.6 %collective-permute-start.27 = (f32[2,1024]{1,0:T(2,128)S(1)}, f32[2,1024]{1,0:T(2,128)S(1)}, u32[]{:S(2)}, u32[]{:S(2)}) collective-permute-start(f32[2,1024]{1,0:T(2,128)S(1)} %slice.49), channel_id=1, source_target_pairs={{0,8},{4,12},{8,0},{12,4},{1,9},{5,13},{9,1},{13,5},{2,10},{6,14},... | collective-permute-start | bytes 24584 | tf_op jit(solution)/shard_map/ppermute | solution.py:187
  100.5 5.6 %collective-permute-start.28 = (f32[4,1024]{1,0:T(4,128)S(1)}, f32[4,1024]{1,0:T(4,128)S(1)}, u32[]{:S(2)}, u32[]{:S(2)}) collective-permute-start(f32[4,1024]{1,0:T(4,128)S(1)} %get-tuple-element.119.refs_5_), channel_id=1, source_target_pairs={{0,4},{4,8},{8,12},{12,0},{1,5},{5,9},{9,13},{13,1},{2,6},{6,10},{... | collective-permute-start | bytes 49160 | tf_op jit(solution)/shard_map/ppermute | solution.py:187
  109.9 8.4 %collective-permute-start.32 = (f32[4,1024]{1,0:T(4,128)S(1)}, f32[4,1024]{1,0:T(4,128)S(1)}, u32[]{:S(2)}, u32[]{:S(2)}) collective-permute-start(f32[4,1024]{1,0:T(4,128)S(1)} %get-tuple-element.127.refs_2_), channel_id=1, source_target_pairs={{0,4},{4,8},{8,12},{12,0},{1,5},{5,9},{9,13},{13,1},{2,6},{6,10},{... | collective-permute-start | bytes 49160 | tf_op jit(solution)/shard_map/ppermute | solution.py:187
  110.2 8.2 %collective-permute-start.33 = (f32[4,1024]{1,0:T(4,128)S(1)}, f32[4,1024]{1,0:T(4,128)S(1)}, u32[]{:S(2)}, u32[]{:S(2)}) collective-permute-start(f32[4,1024]{1,0:T(4,128)S(1)} %get-tuple-element.128), channel_id=1, source_target_pairs={{0,12},{4,0},{8,4},{12,8},{1,13},{5,1},{9,5},{13,9},{2,14},{6,2},{... | collective-permute-start | bytes 49160 | tf_op jit(solution)/shard_map/ppermute | solution.py:187
  124.3 6.2 %collective-permute-start.34 = (bf16[2,168,256]{2,1,0:T(8,128)(2,1)S(1)}, bf16[2,168,256]{2,1,0:T(8,128)(2,1)S(1)}, u32[]{:S(2)}, u32[]{:S(2)}) collective-permute-start(bf16[2,168,256]{2,1,0:T(8,128)(2,1)S(1)} %get-tuple-element.129.refs_8_), channel_id=1, source_target_pairs={{0,2},{1,3},{2,0},{3,1},{4,6},{5,7},{6,4},{7,5},{8,10},{9,11},{10,... | collective-permute-start | bytes 516104 | tf_op jit(solution)/shard_map/ppermute | solution.py:187
  136.8 5.5 %collective-permute-start.36 = (f32[2,168,128]{2,1,0:T(8,128)S(1)}, f32[2,168,128]{2,1,0:T(8,128)S(1)}, u32[]{:S(2)}, u32[]{:S(2)}) collective-permute-start(f32[2,168,128]{2,1,0:T(8,128)S(1)} %constant_dynamic-slice_fusion), channel_id=1, source_target_pairs={{0,2},{1,3},{2,0},{3,1},{4,6},{5,7},{6,4},{7,5},{8,10},{9,11},{10,... | collective-permute-start | bytes 516104 | tf_op jit(solution)/shard_map/ppermute | solution.py:187
  138.3 6.6 %collective-permute-start.35 = (f32[2,168,512]{2,1,0:T(8,128)}, f32[2,168,512]{2,1,0:T(8,128)S(1)}, u32[]{:S(2)}, u32[]{:S(2)}) collective-permute-start(f32[2,168,512]{2,1,0:T(8,128)} %get-tuple-element.132), channel_id=1, source_target_pairs={{0,1},{1,0},{2,3},{3,2},{4,5},{5,4},{6,7},{7,6},{8,9},{9,8},{10,11... | collective-permute-start | bytes 2064392 | tf_op jit(solution)/shard_map/ppermute | solution.py:228
  (49 other events, 225.2 us)

commit v2 on v0

v2 whole, which is shorter than its diff:
```python
import functools
import math

import jax
import jax.numpy as jnp
from jax import lax
from jax.experimental import pallas as pl
from jax.experimental.pallas import tpu as pltpu
from jax.sharding import PartitionSpec as P

ITERS = 8
RAMP_WEIGHT = 0.5
PENALTY = 1.0
STEP_PRIMAL = 0.3
STEP_INVEST = 0.5
STEP_DUAL = 0.3
STEP_CAP = 0.05

F32 = jnp.float32
BF16 = jnp.bfloat16
COL_TILE = 256
VMEM_LIMIT = 24 * 1024 * 1024

IN_VMEM = pl.BlockSpec(memory_space=pltpu.VMEM)
IN_HBM = pl.BlockSpec(memory_space=pltpu.HBM)


def call(body, outs, args, arg_specs=None, out_specs=None, scratch=(), aliases=None, flops=0):
    if arg_specs is not None:
        args = [
            pltpu.with_memory_space_constraint(a, pltpu.HBM) if spec is IN_HBM else a
            for a, spec in zip(args, arg_specs)
        ]
    bytes_moved = sum(a.size * a.dtype.itemsize for a in args)
    bytes_moved += sum(math.prod(o.shape) * jnp.dtype(o.dtype).itemsize for o in outs)
    return pl.pallas_call(
        body,
        out_shape=tuple(outs),
        in_specs=arg_specs or [IN_VMEM] * len(args),
        out_specs=out_specs or tuple(IN_VMEM for _ in outs),
        scratch_shapes=list(scratch),
        input_output_aliases=aliases or {},
        compiler_params=pltpu.CompilerParams(vmem_limit_bytes=VMEM_LIMIT),
        cost_estimate=pl.CostEstimate(flops=flops, bytes_accessed=bytes_moved, transcendentals=0),
    )(*args)


def shape(dims, dtype=F32):
    return jax.ShapeDtypeStruct(tuple(dims), dtype)


def in_vmem(dims, dtype=F32):
    return pltpu.VMEM(tuple(dims), dtype)


def tiles(width):
    return [
        (half, slice(at, at + COL_TILE), slice(half * width + at, half * width + at + COL_TILE))
        for half in range(2)
        for at in range(0, width, COL_TILE)
    ]


def run_copies(pairs, sems):
    copies = [pltpu.make_async_copy(a, b, sems.at[i]) for i, (a, b) in enumerate(pairs)]
    for copy in copies:
        copy.start()
    for copy in copies:
        copy.wait()


def give_body(mine, *refs):
    count = (len(refs) - 1) // 2
    core = lax.rem(lax.axis_index("reg"), 2)
    given = pl.ds((1 - core) * mine, mine)
    run_copies([(refs[i].at[given], refs[count + i]) for i in range(count)], refs[-1])


def held_body(mine, *refs):
    count = (len(refs) - 1) // 2
    core = lax.rem(lax.axis_index("reg"), 2)
    held = pl.ds(core * mine, mine)
    run_copies([(refs[i].at[held], refs[count + i]) for i in range(count)], refs[-1])


def matrix_body(tile, mask, out):
    out[...] = tile[0] * mask[0].astype(F32).astype(BF16)


def message_body(paired, *refs):
    cap, prim, parts = refs[:2], refs[2:4], refs[4:6]
    matrix, near, far = refs[6:]
    mine, _, width = cap[0].shape
    for half in range(2):
        matrix[:, half * width:(half + 1) * width] = parts[half][...]
    for s in range(mine):
        for half, cols, flat in tiles(width):
            write_message(paired, near, far, s, flat, cap[half][s, :, cols], prim[half][s, :, cols])


def is_odd():
    return lax.rem(lax.axis_index("hour"), 2) == 1


def write_message(paired, near, far, s, flat, c, x):
    mine = near.shape[0] // 2
    hours = x.shape[0]
    hour_sum = jnp.sum(c, axis=0, keepdims=True)
    near[pl.ds(s, 1), flat] = hour_sum
    far[pl.ds(s, 1), flat] = hour_sum
    first, last = x[0:1], x[hours - 1:hours]
    if paired:
        odd = is_odd()
        first, last = jnp.where(odd, last, first), jnp.where(odd, first, last)
    near[pl.ds(mine + s, 1), flat] = last
    far[pl.ds(mine + s, 1), flat] = first


def step_body(hours_all, paired, sums_count, first, last, *refs):
    refs = list(refs)
    take = lambda count: [refs.pop(0) for _ in range(count)]
    matrix, cost, prim, cap = take(1)[0], take(2), take(2), take(2)
    dual, invest, const, near, far = take(5)
    sums = take(sums_count)
    if not first:
        dem, sent, carry, received = take(4)
    prim_out = take(2)
    if last:
        inv_keep, inv_give, base_out, rows_give = take(4)
    else:
        cap_out = take(2)
        invest_out, near_out, far_out, sent_out, carry_out = take(5)
        if not first:
            dual_out = take(1)[0]
    ext_low = take(1)[0]
    mine, hours, width = prim[0].shape
    chip = lax.axis_index("reg") // 2
    place = lax.axis_index("hour")
    has_prev = (place > 0).astype(F32)
    has_next = (place < lax.axis_size("hour") - 1).astype(F32)
    row = lax.broadcasted_iota(jnp.int32, (hours, COL_TILE), 0)
    for s in range(mine):
        multipliers = dual[s]
        if not first:
            image = sent[s].astype(F32) + received[s].astype(F32)
            multipliers = jnp.maximum(multipliers + STEP_DUAL * (dem[s] - image), 0.0)
            if not last:
                dual_out[s] = multipliers
        low = multipliers.astype(BF16)
        parts = [part[s:s + 1, :] for part in sums]
        while len(parts) > 1:
            parts = [u + v for u, v in zip(parts[0::2], parts[1::2])]
        old_inv = invest[s]
        grad_inv = const[s] + PENALTY * old_inv - parts[0] / hours_all
        new_inv = jnp.maximum(old_inv - STEP_INVEST * grad_inv, 0.0)
        if last:
            inv_keep[s] = new_inv[:, :width]
            inv_give[s] = new_inv[:, width:]
        else:
            invest_out[s] = new_inv
        limit = jnp.sum(2.0 * new_inv - old_inv, axis=0, keepdims=True)
        before = near[mine + s:mine + s + 1, :]
        after = far[mine + s:mine + s + 1, :]
        if paired:
            odd = is_odd()
            before, after = jnp.where(odd, before, after), jnp.where(odd, after, before)
        before = before * has_prev
        after = after * has_next
        for half, cols, flat in tiles(width):
            pulled = jnp.dot(low, matrix[:, flat], preferred_element_type=F32)
            x = prim[half][s, :, cols]
            prev = jnp.where(row == 0, before[:, flat], pltpu.roll(x, 1, 0))
            follow = jnp.where(row == hours - 1, after[:, flat], pltpu.roll(x, hours - 1, 0))
            rough = 2.0 * x - prev - follow
            c = cap[half][s, :, cols]
            grad = cost[half][s, :, cols] + RAMP_WEIGHT * rough - pulled + c
            new = jnp.maximum(x - STEP_PRIMAL * grad, 0.0)
            prim_out[half][s, :, cols] = new
            ext = 2.0 * new - x
            ext_low[:, flat] = ext.astype(BF16)
            if not last:
                c = jnp.maximum(c + STEP_CAP * (ext - limit[:, flat]), 0.0)
                cap_out[half][s, :, cols] = c
                write_message(paired, near_out, far_out, s, flat, c, new)
        total = lax.dot_general(
            ext_low[...], matrix[...], (((1,), (1,)), ((), ())), preferred_element_type=F32
        )
        if not first:
            total = total + carry[s]
        if last:
            rows = total.shape[1] // 2
            low_chip = chip == 0
            keep = jnp.where(low_chip, total[:, :rows], total[:, rows:])
            rows_give[s] = jnp.where(low_chip, total[:, rows:], total[:, :rows])
            base = multipliers + STEP_DUAL * dem[s]
            base_out[s] = jnp.where(low_chip, base[:, :rows], base[:, rows:]) - STEP_DUAL * keep
        else:
            low_sum = total.astype(BF16)
            sent_out[s] = low_sum
            carry_out[s] = total - low_sum.astype(F32)


def join_body(*refs):
    kept, got, out, sems = refs
    mine = kept.shape[0]
    core = lax.rem(lax.axis_index("reg"), 2)
    run_copies(
        [(kept, out.at[pl.ds(core * mine, mine)]), (got, out.at[pl.ds((1 - core) * mine, mine)])],
        sems,
    )


def join(kept, got):
    mine = kept.shape[0]
    return call(
        join_body,
        (shape((2 * mine,) + kept.shape[1:]),),
        (kept, got),
        out_specs=(IN_HBM,),
        scratch=(pltpu.SemaphoreType.DMA((2,)),),
    )[0]


def dual_body(base, got, keep, give):
    core = lax.rem(lax.axis_index("reg"), 2)
    part = keep.shape[2]
    for s in range(base.shape[0]):
        new = jnp.maximum(base[s] - STEP_DUAL * got[s], 0.0)
        low, high = new[:, :part], new[:, part:]
        keep[s] = jnp.where(core == 0, low, high)
        give[s] = jnp.where(core == 0, high, low)


def hour_exchange(near, far, mine, paired):
    count = lax.axis_size("hour")
    if not paired:
        near_in = lax.ppermute(near, "hour", [(i, (i + 1) % count) for i in range(count)])
        far_in = lax.ppermute(far, "hour", [((i + 1) % count, i) for i in range(count)])
        return near_in, far_in, (lax.psum(near[:mine], "hour"),)
    partners = lambda by: [(i, i ^ by) for i in range(count)]
    far_in = lax.ppermute(far, "hour", partners(3))
    near_in = lax.ppermute(near, "hour", partners(1))
    across = lax.ppermute(near[:mine], "hour", partners(2))
    return near_in, far_in, (near, near_in, across, far_in)


def shards(
    cost_rate,
    invest_cost,
    tile,
    tile_mask,
    demand,
    dispatch,
    dual,
    cap_dual,
    capacity,
    multiplier,
    consensus,
    scen_weight,
    node_of,
):
    reg_count = lax.axis_size("reg")
    assert reg_count == 4
    paired = lax.axis_size("hour") == 4
    core = lax.axis_index("reg") % 2
    nscen, hours, width = dispatch.shape
    rows = dual.shape[2]
    mine = nscen // 2
    sections = capacity.shape[1]
    hours_all = float(hours * lax.axis_size("hour"))
    twin = [(i, i ^ 1) for i in range(reg_count)]
    other_chip = [(i, i ^ 2) for i in range(reg_count)]
    half_full = in_vmem((mine, hours, width))
    dual_like = in_vmem((mine, hours, rows))
    message = in_vmem((2 * mine, 2 * width))
    invest_like = in_vmem((mine, sections, 2 * width))

    def held(x):
        return lax.dynamic_slice_in_dim(x, core * mine, mine, 0)

    def given(x):
        return lax.dynamic_slice_in_dim(x, (1 - core) * mine, mine, 0)

    prim_give, cap_give, cost_give = call(
        functools.partial(give_body, mine),
        (half_full,) * 3,
        (dispatch, cap_dual, cost_rate),
        arg_specs=[IN_HBM] * 3,
        scratch=(pltpu.SemaphoreType.DMA((3,)),),
    )
    prim_twin = lax.ppermute(prim_give, "reg", twin)
    cap_twin = lax.ppermute(cap_give, "reg", twin)
    cost_twin = lax.ppermute(cost_give, "reg", twin)
    (matrix_own,) = call(matrix_body, (in_vmem(tile.shape[1:], BF16),), (tile, tile_mask))
    matrix_twin = lax.ppermute(matrix_own, "reg", twin)
    prim_own, cap_own, cost_own, dual_var, dem = call(
        functools.partial(held_body, mine),
        (half_full,) * 3 + (dual_like,) * 2,
        (dispatch, cap_dual, cost_rate, dual, demand),
        arg_specs=[IN_HBM] * 5,
        scratch=(pltpu.SemaphoreType.DMA((5,)),),
    )
    prim, cap, cost = (prim_own, prim_twin), (cap_own, cap_twin), (cost_own, cost_twin)
    matrix, near, far = call(
        functools.partial(message_body, paired),
        (in_vmem((rows, 2 * width), BF16), message, message),
        (*cap, *prim, matrix_own, matrix_twin),
    )
    small = jnp.concatenate(
        [invest_cost[None] + multiplier - PENALTY * consensus, capacity], axis=1
    )
    small_all = jnp.concatenate([held(small), lax.ppermute(given(small), "reg", twin)], axis=2)
    const, invest = small_all[:, :sections], small_all[:, sections:]

    flops = 4 * mine * hours * rows * 2 * width
    sent = carry = received = None
    for step in range(ITERS):
        first, last = step == 0, step + 1 == ITERS
        near_in, far_in, sums = hour_exchange(near, far, mine, paired)
        args = [matrix, *cost, *prim, *cap, dual_var, invest, const, near_in, far_in, *sums]
        if not first:
            args += [dem, sent, carry, received]
        if last:
            outs = [half_full] * 2 + [in_vmem((mine, sections, width))] * 2
            outs += [in_vmem((mine, hours, rows // 2))] * 2
        else:
            outs = [half_full] * 4 + [invest_like, message, message]
            outs += [in_vmem((mine, hours, rows), BF16), dual_like]
            if not first:
                outs += [dual_like]
        got = call(
            functools.partial(step_body, hours_all, paired, len(sums), first, last),
            outs,
            args,
            scratch=(pltpu.VMEM((hours, 2 * width), BF16),),
            flops=flops,
        )
        prim = got[:2]
        if last:
            inv_keep, inv_give, base, rows_give = got[2:]
        else:
            cap = got[2:4]
            invest, near, far, sent, carry = got[4:9]
            received = lax.ppermute(sent, "reg", other_chip)
            if not first:
                dual_var = got[9]

    rows_got = lax.ppermute(rows_give, "reg", other_chip)
    prim_got = lax.ppermute(prim[1], "reg", twin)
    inv_got = lax.ppermute(inv_give, "reg", twin)
    capacity_out = jnp.where(
        core == 0,
        jnp.concatenate([inv_keep, inv_got], axis=0),
        jnp.concatenate([inv_got, inv_keep], axis=0),
    )
    scen_count = lax.axis_size("scen")
    node_count = node_of.shape[1] * scen_count // 2
    node_ids = jnp.arange(node_count, dtype=jnp.int32)
    one_hot = (node_of[:, :, None] == node_ids[None, None, :]).astype(F32)
    weights = one_hot * scen_weight[None, :, None]
    node_sum = jnp.sum(
        weights[:, :, :, None] * jnp.transpose(capacity_out, (1, 0, 2))[:, :, None, :], axis=1
    )
    node_mass = jnp.sum(weights, axis=1)
    packed = jnp.concatenate(
        [node_sum, jnp.broadcast_to(node_mass[:, :, None], node_mass.shape + (128,))], axis=2
    )
    if scen_count == 2:
        packed = packed + lax.ppermute(packed, "scen", [(0, 1), (1, 0)])
    else:
        packed = lax.psum(packed, "scen")
    sum_total, mass_total = packed[:, :, :width], packed[:, :, width:width + 1]
    average = sum_total / (mass_total + (mass_total <= 0.0).astype(F32))
    spread_back = jnp.sum(one_hot[:, :, :, None] * average[:, None, :, :], axis=2)
    multiplier_out = multiplier + PENALTY * (capacity_out - jnp.transpose(spread_back, (1, 0, 2)))

    dispatch_out = join(prim[0], prim_got)
    dual_keep, dual_give = call(
        dual_body, (in_vmem((mine, hours, rows // reg_count)),) * 2, (base, rows_got)
    )
    dual_got = lax.ppermute(dual_give, "reg", twin)
    dual_out = jnp.where(
        core == 0,
        jnp.concatenate([dual_keep, dual_got], axis=0),
        jnp.concatenate([dual_got, dual_keep], axis=0),
    )
    return (dispatch_out, dual_out, capacity_out, multiplier_out)


def solution(mesh):
    placed = (
        P("scen", "hour", "reg"),
        P(None, "reg"),
        P("hour", None, "reg"),
        P("hour", None, "reg"),
        P("scen", "hour", None),
        P("scen", "hour", "reg"),
        P("scen", "hour", None),
        P("scen", "hour", "reg"),
        P("scen", None, "reg"),
        P("scen", None, "reg"),
        P("scen", None, "reg"),
        P("scen"),
        P(None, "scen"),
    )
    return jax.shard_map(
        shards,
        mesh=mesh,
        in_specs=placed,
        out_specs=(
            P("scen", "hour", "reg"),
            P("scen", "hour", "reg"),
            P("scen", None, "reg"),
            P("scen", None, "reg"),
        ),
        check_vma=False,
    )
```

time: 346 us -> 101 us (0.29)
  blocking collectives: 157 us -> 0 us
  matrix products: 46.1 us -> 0 us
  waiting for transfers between devices: 65.1 us -> 35 us
  Pallas kernels: 0 us -> 18 us
  between operations: 14.8 us -> 1.13 us
  other arithmetic: 11.5 us -> 0.73 us
  local copies, waits for them, and re-layouts: 11.9 us -> 2.29 us
  starting transfers between devices: 37.8 us -> 43.3 us
    psum x9 -> x0, blocking collectives: 111 us -> none  [the longest x8 102 us: shards(): zmean = lax.psum(jnp.sum(cap_var, axis=1), 'hour') / hours_all]
    reduce_scatter x8 -> x0, waiting for transfers between devices: 64.9 us -> none  [shards(): lax.psum_scatter(partial_rows, 'reg', scatter_dimension=2, tiled=True)]
    all_gather x7 -> x0, blocking collectives: 46.4 us -> none  [shards(): lax.all_gather(dual_var.astype(jnp.bfloat16), 'reg', axis=2, tiled=True)]
    dot_general x19 -> x0, matrix products: 46.1 us -> none  [the longest x8 32.9 us: shards(): jnp.einsum('shr,rc->shc', dual_low, matrix, preferred_element_type=jnp.fl...]
    ppermute x16 -> x41, waiting for transfers between devices: 0.04 us -> 35 us  [the longest x8 24.6 us: hour_exchange(): across = lax.ppermute(near[:mine], 'hour', partners(2))]
    pallas_call x0 -> x14, Pallas kernels: none -> 18 us  [call(): pl.pallas_call(body, out_shape=tuple(outs), in_specs=arg_specs or [IN_VME...]
    convert_element_type x7 -> x1, other arithmetic: 7.56 us -> 0.07 us  [shards(): one_hot = (node_of[:, :, None] == node_ids[None, None, :]).astype(F32)]
    ppermute x16 -> x41, starting transfers between devices: 37.5 us -> 43.3 us  [the longest x8 13.5 us: hour_exchange(): far_in = lax.ppermute(far, 'hour', partners(3))]
  transfers between devices with their start and end apart: 24 -> 41, of which waited for: 8 -> 15; matrix products, arithmetic and copies ran while one was open for 5% -> 3% of each run, Pallas kernels for 0% -> 2%
where the time goes in v2:
time: 101 us; the launch traced here: 100 us
  starting transfers between devices  43.3 us (43%)
  waiting for transfers between devices  35 us (35%)
  Pallas kernels  18 us (18%)
  local copies, waits for them, and re-layouts  2.29 us (2%)
  between operations  1.13 us (1%)
    ppermute x8, waiting for transfers between devices, hour_exchange(): across = lax.ppermute(near[:mine], 'hour', partners(2))  24.6 us
    pallas_call x14, Pallas kernels, call(): pl.pallas_call(body, out_shape=tuple(outs), in_specs=arg_specs or [IN_VME...  18 us
    ppermute x8, starting transfers between devices, hour_exchange(): far_in = lax.ppermute(far, 'hour', partners(3))  13.5 us
    ppermute x8, starting transfers between devices, hour_exchange(): across = lax.ppermute(near[:mine], 'hour', partners(2))  12 us
    ppermute x7, starting transfers between devices, shards(): received = lax.ppermute(sent, 'reg', other_chip)  8.57 us
    ppermute x8, starting transfers between devices, hour_exchange(): near_in = lax.ppermute(near, 'hour', partners(1))  5 us
    ppermute x8, waiting for transfers between devices, hour_exchange(): far_in = lax.ppermute(far, 'hour', partners(3))  3.84 us
    ppermute x1, waiting for transfers between devices, shards(): rows_got = lax.ppermute(rows_give, 'reg', other_chip)  3.5 us
  transfers between devices with their start and end apart: 41, of which 15 were waited for; matrix products, arithmetic and copies ran while one was open for 3% of the time, Pallas kernels for 2%

profile of v2, /device:TPU:0, one launch (start us, length us, event | category | flops | bytes accessed | tf_op | source)
XLA Modules:
  0.0 100.4 jit_solution(3331292257629751945)
XLA Ops:
  0.7 2.7 %shard_map.157 = (f32[2,168,512]{2,1,0:T(8,128)}, f32[2,168,512]{2,1,0:T(8,128)}, f32[2,168,512]{2,1,0:T(8,128)S(1)}) custom-call(f32[4,168,512]{2,1,0:T(8,128)} %refs_0_.3, f32[4,168,512]{2,1,0:T(8,128)} %refs_1_.3, f32[4,168,512]{2,1,0:T(8,128)} %refs_2_.3), custom_call_target="tpu_custom_call" | custom-call | bytes 6193152 | tf_op jit(solution)/shard_map/pallas_call | solution.py:36
  5.3 1.7 %shard_map.156 = (f32[2,168,512]{2,1,0:T(8,128)S(1)}, f32[2,168,512]{2,1,0:T(8,128)S(1)}, f32[2,168,512]{2,1,0:T(8,128)S(1)}, f32[2,168,256]{2,1,0:T(8,128)S(1)}, f32[2,168,256]{2,1,0:T(8,128)S(1)}) custom-call(f32[4,168,512]{2,1,0:T(8,128)} %refs_0_.3, f32[4,168,512]{2,1,0:T(8,128)} %refs_1_.3, f32[4,168,512]{2,1,0:T(8,128)} %refs_2_.3, ...), custom_call_target="tpu_custom_call" | custom-call | bytes 8257536 | tf_op jit(solution)/shard_map/pallas_call | solution.py:36
  7.4 3.0 %collective-permute-start.5 = (f32[4,1024]{1,0:T(4,128)S(1)}, f32[4,1024]{1,0:T(4,128)S(1)}, u32[]{:S(2)}, u32[]{:S(2)}) collective-permute-start(f32[4,1024]{1,0:T(4,128)S(1)} %get-tuple-element.100.refs_12_), channel_id=1, source_target_pairs={{0,4},{4,0},{8,12},{12,8},{1,5},{5,1},{9,13},{13,9},{2,6},{6,2},{1... | collective-permute-start | bytes 49160 | tf_op jit(solution)/shard_map/ppermute | solution.py:242
  10.4 2.6 %collective-permute-start.7 = (f32[2,1024]{1,0:T(2,128)S(1)}, f32[2,1024]{1,0:T(2,128)S(1)}, u32[]{:S(2)}, u32[]{:S(2)}) collective-permute-start(f32[2,1024]{1,0:T(2,128)S(1)} %slice.38), channel_id=1, source_target_pairs={{0,8},{4,12},{8,0},{12,4},{1,9},{5,13},{9,1},{13,5},{2,10},{6,14},... | collective-permute-start | bytes 24584 | tf_op jit(solution)/shard_map/ppermute | solution.py:243
  13.1 1.9 %collective-permute-done.7.refs_14_ = f32[2,1024]{1,0:T(2,128)S(1)} collective-permute-done((f32[2,1024]{1,0:T(2,128)S(1)}, f32[2,1024]{1,0:T(2,128)S(1)}, u32[]{:S(2)}, u32[]{:S(2)}) %collective-permute-start.7) | collective-permute-done | bytes 8224 | tf_op jit(solution)/shard_map/ppermute | solution.py:243
  15.0 3.6 %collective-permute-done.6.refs_11_.refs_15_ = f32[4,1024]{1,0:T(4,128)S(1)} collective-permute-done((f32[4,1024]{1,0:T(4,128)S(1)}, f32[4,1024]{1,0:T(4,128)S(1)}, u32[]{:S(2)}, u32[]{:S(2)}) %collective-permute-start.6) | collective-permute-done | bytes 16416 | tf_op jit(solution)/shard_map/ppermute | solution.py:241
  22.1 3.0 %collective-permute-start.10 = (f32[2,1024]{1,0:T(2,128)S(1)}, f32[2,1024]{1,0:T(2,128)S(1)}, u32[]{:S(2)}, u32[]{:S(2)}) collective-permute-start(f32[2,1024]{1,0:T(2,128)S(1)} %slice.39), channel_id=1, source_target_pairs={{0,8},{4,12},{8,0},{12,4},{1,9},{5,13},{9,1},{13,5},{2,10},{6,14},... | collective-permute-start | bytes 24584 | tf_op jit(solution)/shard_map/ppermute | solution.py:243
  25.1 1.8 %collective-permute-done.10.refs_14_ = f32[2,1024]{1,0:T(2,128)S(1)} collective-permute-done((f32[2,1024]{1,0:T(2,128)S(1)}, f32[2,1024]{1,0:T(2,128)S(1)}, u32[]{:S(2)}, u32[]{:S(2)}) %collective-permute-start.10) | collective-permute-done | bytes 8224 | tf_op jit(solution)/shard_map/ppermute | solution.py:243
  30.4 2.9 %collective-permute-start.13 = (f32[4,1024]{1,0:T(4,128)S(1)}, f32[4,1024]{1,0:T(4,128)S(1)}, u32[]{:S(2)}, u32[]{:S(2)}) collective-permute-start(f32[4,1024]{1,0:T(4,128)S(1)} %get-tuple-element.119), channel_id=1, source_target_pairs={{0,12},{4,8},{8,4},{12,0},{1,13},{5,9},{9,5},{13,1},{2,14},{6,10},... | collective-permute-start | bytes 49160 | tf_op jit(solution)/shard_map/ppermute | solution.py:241
  33.3 4.5 %collective-permute-done.14.refs_14_ = f32[2,1024]{1,0:T(2,128)S(1)} collective-permute-done((f32[2,1024]{1,0:T(2,128)S(1)}, f32[2,1024]{1,0:T(2,128)S(1)}, u32[]{:S(2)}, u32[]{:S(2)}) %collective-permute-start.14) | collective-permute-done | bytes 8224 | tf_op jit(solution)/shard_map/ppermute | solution.py:243
  41.0 1.7 %collective-permute-start.17 = (f32[4,1024]{1,0:T(4,128)S(1)}, f32[4,1024]{1,0:T(4,128)S(1)}, u32[]{:S(2)}, u32[]{:S(2)}) collective-permute-start(f32[4,1024]{1,0:T(4,128)S(1)} %get-tuple-element.129), channel_id=1, source_target_pairs={{0,12},{4,8},{8,4},{12,0},{1,13},{5,9},{9,5},{13,1},{2,14},{6,10},... | collective-permute-start | bytes 49160 | tf_op jit(solution)/shard_map/ppermute | solution.py:241
  42.7 1.8 %collective-permute-start.18 = (f32[2,1024]{1,0:T(2,128)S(1)}, f32[2,1024]{1,0:T(2,128)S(1)}, u32[]{:S(2)}, u32[]{:S(2)}) collective-permute-start(f32[2,1024]{1,0:T(2,128)S(1)} %slice.41), channel_id=1, source_target_pairs={{0,8},{4,12},{8,0},{12,4},{1,9},{5,13},{9,1},{13,5},{2,10},{6,14},... | collective-permute-start | bytes 24584 | tf_op jit(solution)/shard_map/ppermute | solution.py:243
  44.5 2.7 %collective-permute-done.18.refs_14_ = f32[2,1024]{1,0:T(2,128)S(1)} collective-permute-done((f32[2,1024]{1,0:T(2,128)S(1)}, f32[2,1024]{1,0:T(2,128)S(1)}, u32[]{:S(2)}, u32[]{:S(2)}) %collective-permute-start.18) | collective-permute-done | bytes 8224 | tf_op jit(solution)/shard_map/ppermute | solution.py:243
  50.0 2.6 %collective-permute-start.21 = (f32[4,1024]{1,0:T(4,128)S(1)}, f32[4,1024]{1,0:T(4,128)S(1)}, u32[]{:S(2)}, u32[]{:S(2)}) collective-permute-start(f32[4,1024]{1,0:T(4,128)S(1)} %get-tuple-element.139), channel_id=1, source_target_pairs={{0,12},{4,8},{8,4},{12,0},{1,13},{5,9},{9,5},{13,1},{2,14},{6,10},... | collective-permute-start | bytes 49160 | tf_op jit(solution)/shard_map/ppermute | solution.py:241
  53.1 4.1 %collective-permute-done.22.refs_14_ = f32[2,1024]{1,0:T(2,128)S(1)} collective-permute-done((f32[2,1024]{1,0:T(2,128)S(1)}, f32[2,1024]{1,0:T(2,128)S(1)}, u32[]{:S(2)}, u32[]{:S(2)}) %collective-permute-start.22) | collective-permute-done | bytes 8224 | tf_op jit(solution)/shard_map/ppermute | solution.py:243
  60.4 1.6 %collective-permute-start.25 = (f32[4,1024]{1,0:T(4,128)S(1)}, f32[4,1024]{1,0:T(4,128)S(1)}, u32[]{:S(2)}, u32[]{:S(2)}) collective-permute-start(f32[4,1024]{1,0:T(4,128)S(1)} %get-tuple-element.149), channel_id=1, source_target_pairs={{0,12},{4,8},{8,4},{12,0},{1,13},{5,9},{9,5},{13,1},{2,14},{6,10},... | collective-permute-start | bytes 49160 | tf_op jit(solution)/shard_map/ppermute | solution.py:241
  62.0 1.8 %collective-permute-start.26 = (f32[2,1024]{1,0:T(2,128)S(1)}, f32[2,1024]{1,0:T(2,128)S(1)}, u32[]{:S(2)}, u32[]{:S(2)}) collective-permute-start(f32[2,1024]{1,0:T(2,128)S(1)} %slice.43), channel_id=1, source_target_pairs={{0,8},{4,12},{8,0},{12,4},{1,9},{5,13},{9,1},{13,5},{2,10},{6,14},... | collective-permute-start | bytes 24584 | tf_op jit(solution)/shard_map/ppermute | solution.py:243
  63.9 2.7 %collective-permute-done.26.refs_14_ = f32[2,1024]{1,0:T(2,128)S(1)} collective-permute-done((f32[2,1024]{1,0:T(2,128)S(1)}, f32[2,1024]{1,0:T(2,128)S(1)}, u32[]{:S(2)}, u32[]{:S(2)}) %collective-permute-start.26) | collective-permute-done | bytes 8224 | tf_op jit(solution)/shard_map/ppermute | solution.py:243
  69.4 2.6 %collective-permute-start.29 = (f32[4,1024]{1,0:T(4,128)S(1)}, f32[4,1024]{1,0:T(4,128)S(1)}, u32[]{:S(2)}, u32[]{:S(2)}) collective-permute-start(f32[4,1024]{1,0:T(4,128)S(1)} %get-tuple-element.159), channel_id=1, source_target_pairs={{0,12},{4,8},{8,4},{12,0},{1,13},{5,9},{9,5},{13,1},{2,14},{6,10},... | collective-permute-start | bytes 49160 | tf_op jit(solution)/shard_map/ppermute | solution.py:241
  72.5 4.1 %collective-permute-done.30.refs_14_ = f32[2,1024]{1,0:T(2,128)S(1)} collective-permute-done((f32[2,1024]{1,0:T(2,128)S(1)}, f32[2,1024]{1,0:T(2,128)S(1)}, u32[]{:S(2)}, u32[]{:S(2)}) %collective-permute-start.30) | collective-permute-done | bytes 8224 | tf_op jit(solution)/shard_map/ppermute | solution.py:243
  79.9 1.6 %collective-permute-start.33 = (f32[4,1024]{1,0:T(4,128)S(1)}, f32[4,1024]{1,0:T(4,128)S(1)}, u32[]{:S(2)}, u32[]{:S(2)}) collective-permute-start(f32[4,1024]{1,0:T(4,128)S(1)} %get-tuple-element.169), channel_id=1, source_target_pairs={{0,12},{4,8},{8,4},{12,0},{1,13},{5,9},{9,5},{13,1},{2,14},{6,10},... | collective-permute-start | bytes 49160 | tf_op jit(solution)/shard_map/ppermute | solution.py:241
  81.4 1.8 %collective-permute-start.34 = (f32[2,1024]{1,0:T(2,128)S(1)}, f32[2,1024]{1,0:T(2,128)S(1)}, u32[]{:S(2)}, u32[]{:S(2)}) collective-permute-start(f32[2,1024]{1,0:T(2,128)S(1)} %slice.45), channel_id=1, source_target_pairs={{0,8},{4,12},{8,0},{12,4},{1,9},{5,13},{9,1},{13,5},{2,10},{6,14},... | collective-permute-start | bytes 24584 | tf_op jit(solution)/shard_map/ppermute | solution.py:243
  83.3 2.7 %collective-permute-done.34.refs_14_ = f32[2,1024]{1,0:T(2,128)S(1)} collective-permute-done((f32[2,1024]{1,0:T(2,128)S(1)}, f32[2,1024]{1,0:T(2,128)S(1)}, u32[]{:S(2)}, u32[]{:S(2)}) %collective-permute-start.34) | collective-permute-done | bytes 8224 | tf_op jit(solution)/shard_map/ppermute | solution.py:243
  93.1 3.5 %collective-permute-done.37.got = f32[2,168,128]{2,1,0:T(8,128)S(1)} collective-permute-done((f32[2,168,128]{2,1,0:T(8,128)S(1)}, f32[2,168,128]{2,1,0:T(8,128)S(1)}, u32[]{:S(2)}, u32[]{:S(2)}) %collective-permute-start.37) | collective-permute-done | bytes 172064 | tf_op jit(solution)/shard_map/ppermute | solution.py:348
  (117 shorter events, 36.1 us)
Async XLA Ops:
  4.6 8.5 %collective-permute-start.3 = (f32[2,168,512]{2,1,0:T(8,128)S(1)}, f32[2,168,512]{2,1,0:T(8,128)S(1)}, u32[]{:S(2)}, u32[]{:S(2)}) collective-permute-start(f32[2,168,512]{2,1,0:T(8,128)S(1)} %get-tuple-element.98), channel_id=1, source_target_pairs={{0,1},{1,0},{2,3},{3,2},{4,5},{5,4},{6,7},{7,6},{8,9},{9,8},{10,11... | collective-permute-start | bytes 2064392 | tf_op jit(solution)/shard_map/ppermute | solution.py:293
  4.8 8.2 %collective-permute-start.4 = (f32[2,6,512]{2,1,0:T(8,128)S(1)}, f32[2,6,512]{2,1,0:T(8,128)S(1)}, u32[]{:S(2)}, u32[]{:S(2)}) collective-permute-start(f32[2,6,512]{2,1,0:T(8,128)S(1)} %get-tuple-element.202), channel_id=1, source_target_pairs={{0,1},{1,0},{2,3},{3,2},{4,5},{5,4},{6,7},{7,6},{8,9},{9,8},{10,11... | collective-permute-start | bytes 73736 | tf_op jit(solution)/shard_map/ppermute | solution.py:312
  7.4 7.6 %collective-permute-start.5 = (f32[4,1024]{1,0:T(4,128)S(1)}, f32[4,1024]{1,0:T(4,128)S(1)}, u32[]{:S(2)}, u32[]{:S(2)}) collective-permute-start(f32[4,1024]{1,0:T(4,128)S(1)} %get-tuple-element.100.refs_12_), channel_id=1, source_target_pairs={{0,4},{4,0},{8,12},{12,8},{1,5},{5,1},{9,13},{13,9},{2,6},{6,2},{1... | collective-permute-start | bytes 49160 | tf_op jit(solution)/shard_map/ppermute | solution.py:242
  20.1 7.1 %collective-permute-start.11 = (bf16[2,168,256]{2,1,0:T(8,128)(2,1)S(1)}, bf16[2,168,256]{2,1,0:T(8,128)(2,1)S(1)}, u32[]{:S(2)}, u32[]{:S(2)}) collective-permute-start(bf16[2,168,256]{2,1,0:T(8,128)(2,1)S(1)} %get-tuple-element.110.refs_17_), channel_id=1, source_target_pairs={{0,2},{1,3},{2,0},{3,1},{4,6},{5,7},{6,4},{7,5},{8,10},{9,11},{10,... | collective-permute-start | bytes 516104 | tf_op jit(solution)/shard_map/ppermute | solution.py:344
  28.7 9.1 %collective-permute-start.15 = (bf16[2,168,256]{2,1,0:T(8,128)(2,1)S(1)}, bf16[2,168,256]{2,1,0:T(8,128)(2,1)S(1)}, u32[]{:S(2)}, u32[]{:S(2)}) collective-permute-start(bf16[2,168,256]{2,1,0:T(8,128)(2,1)S(1)} %get-tuple-element.120.refs_17_), channel_id=1, source_target_pairs={{0,2},{1,3},{2,0},{3,1},{4,6},{5,7},{6,4},{7,5},{8,10},{9,11},{10,... | collective-permute-start | bytes 516104 | tf_op jit(solution)/shard_map/ppermute | solution.py:344
  29.3 8.6 %collective-permute-start.12 = (f32[4,1024]{1,0:T(4,128)S(1)}, f32[4,1024]{1,0:T(4,128)S(1)}, u32[]{:S(2)}, u32[]{:S(2)}) collective-permute-start(f32[4,1024]{1,0:T(4,128)S(1)} %get-tuple-element.118.refs_12_), channel_id=1, source_target_pairs={{0,4},{4,0},{8,12},{12,8},{1,5},{5,1},{9,13},{13,9},{2,6},{6,2},{1... | collective-permute-start | bytes 49160 | tf_op jit(solution)/shard_map/ppermute | solution.py:242
  30.4 7.5 %collective-permute-start.13 = (f32[4,1024]{1,0:T(4,128)S(1)}, f32[4,1024]{1,0:T(4,128)S(1)}, u32[]{:S(2)}, u32[]{:S(2)}) collective-permute-start(f32[4,1024]{1,0:T(4,128)S(1)} %get-tuple-element.119), channel_id=1, source_target_pairs={{0,12},{4,8},{8,4},{12,0},{1,13},{5,9},{9,5},{13,1},{2,14},{6,10},... | collective-permute-start | bytes 49160 | tf_op jit(solution)/shard_map/ppermute | solution.py:241
  39.4 7.8 %collective-permute-start.19 = (bf16[2,168,256]{2,1,0:T(8,128)(2,1)S(1)}, bf16[2,168,256]{2,1,0:T(8,128)(2,1)S(1)}, u32[]{:S(2)}, u32[]{:S(2)}) collective-permute-start(bf16[2,168,256]{2,1,0:T(8,128)(2,1)S(1)} %get-tuple-element.130.refs_17_), channel_id=1, source_target_pairs={{0,2},{1,3},{2,0},{3,1},{4,6},{5,7},{6,4},{7,5},{8,10},{9,11},{10,... | collective-permute-start | bytes 516104 | tf_op jit(solution)/shard_map/ppermute | solution.py:344
  41.0 6.2 %collective-permute-start.16 = (f32[4,1024]{1,0:T(4,128)S(1)}, f32[4,1024]{1,0:T(4,128)S(1)}, u32[]{:S(2)}, u32[]{:S(2)}) collective-permute-start(f32[4,1024]{1,0:T(4,128)S(1)} %get-tuple-element.128.refs_12_), channel_id=1, source_target_pairs={{0,4},{4,0},{8,12},{12,8},{1,5},{5,1},{9,13},{13,9},{2,6},{6,2},{1... | collective-permute-start | bytes 49160 | tf_op jit(solution)/shard_map/ppermute | solution.py:242
  41.0 6.2 %collective-permute-start.17 = (f32[4,1024]{1,0:T(4,128)S(1)}, f32[4,1024]{1,0:T(4,128)S(1)}, u32[]{:S(2)}, u32[]{:S(2)}) collective-permute-start(f32[4,1024]{1,0:T(4,128)S(1)} %get-tuple-element.129), channel_id=1, source_target_pairs={{0,12},{4,8},{8,4},{12,0},{1,13},{5,9},{9,5},{13,1},{2,14},{6,10},... | collective-permute-start | bytes 49160 | tf_op jit(solution)/shard_map/ppermute | solution.py:241
  48.8 8.4 %collective-permute-start.23 = (bf16[2,168,256]{2,1,0:T(8,128)(2,1)S(1)}, bf16[2,168,256]{2,1,0:T(8,128)(2,1)S(1)}, u32[]{:S(2)}, u32[]{:S(2)}) collective-permute-start(bf16[2,168,256]{2,1,0:T(8,128)(2,1)S(1)} %get-tuple-element.140.refs_17_), channel_id=1, source_target_pairs={{0,2},{1,3},{2,0},{3,1},{4,6},{5,7},{6,4},{7,5},{8,10},{9,11},{10,... | collective-permute-start | bytes 516104 | tf_op jit(solution)/shard_map/ppermute | solution.py:344
  49.7 7.6 %collective-permute-start.20 = (f32[4,1024]{1,0:T(4,128)S(1)}, f32[4,1024]{1,0:T(4,128)S(1)}, u32[]{:S(2)}, u32[]{:S(2)}) collective-permute-start(f32[4,1024]{1,0:T(4,128)S(1)} %get-tuple-element.138.refs_12_), channel_id=1, source_target_pairs={{0,4},{4,0},{8,12},{12,8},{1,5},{5,1},{9,13},{13,9},{2,6},{6,2},{1... | collective-permute-start | bytes 49160 | tf_op jit(solution)/shard_map/ppermute | solution.py:242
  50.0 7.2 %collective-permute-start.21 = (f32[4,1024]{1,0:T(4,128)S(1)}, f32[4,1024]{1,0:T(4,128)S(1)}, u32[]{:S(2)}, u32[]{:S(2)}) collective-permute-start(f32[4,1024]{1,0:T(4,128)S(1)} %get-tuple-element.139), channel_id=1, source_target_pairs={{0,12},{4,8},{8,4},{12,0},{1,13},{5,9},{9,5},{13,1},{2,14},{6,10},... | collective-permute-start | bytes 49160 | tf_op jit(solution)/shard_map/ppermute | solution.py:241
  58.8 7.8 %collective-permute-start.27 = (bf16[2,168,256]{2,1,0:T(8,128)(2,1)S(1)}, bf16[2,168,256]{2,1,0:T(8,128)(2,1)S(1)}, u32[]{:S(2)}, u32[]{:S(2)}) collective-permute-start(bf16[2,168,256]{2,1,0:T(8,128)(2,1)S(1)} %get-tuple-element.150.refs_17_), channel_id=1, source_target_pairs={{0,2},{1,3},{2,0},{3,1},{4,6},{5,7},{6,4},{7,5},{8,10},{9,11},{10,... | collective-permute-start | bytes 516104 | tf_op jit(solution)/shard_map/ppermute | solution.py:344
  60.4 6.2 %collective-permute-start.24 = (f32[4,1024]{1,0:T(4,128)S(1)}, f32[4,1024]{1,0:T(4,128)S(1)}, u32[]{:S(2)}, u32[]{:S(2)}) collective-permute-start(f32[4,1024]{1,0:T(4,128)S(1)} %get-tuple-element.148.refs_12_), channel_id=1, source_target_pairs={{0,4},{4,0},{8,12},{12,8},{1,5},{5,1},{9,13},{13,9},{2,6},{6,2},{1... | collective-permute-start | bytes 49160 | tf_op jit(solution)/shard_map/ppermute | solution.py:242
  60.4 6.2 %collective-permute-start.25 = (f32[4,1024]{1,0:T(4,128)S(1)}, f32[4,1024]{1,0:T(4,128)S(1)}, u32[]{:S(2)}, u32[]{:S(2)}) collective-permute-start(f32[4,1024]{1,0:T(4,128)S(1)} %get-tuple-element.149), channel_id=1, source_target_pairs={{0,12},{4,8},{8,4},{12,0},{1,13},{5,9},{9,5},{13,1},{2,14},{6,10},... | collective-permute-start | bytes 49160 | tf_op jit(solution)/shard_map/ppermute | solution.py:241
  68.2 8.4 %collective-permute-start.31 = (bf16[2,168,256]{2,1,0:T(8,128)(2,1)S(1)}, bf16[2,168,256]{2,1,0:T(8,128)(2,1)S(1)}, u32[]{:S(2)}, u32[]{:S(2)}) collective-permute-start(bf16[2,168,256]{2,1,0:T(8,128)(2,1)S(1)} %get-tuple-element.160.refs_17_), channel_id=1, source_target_pairs={{0,2},{1,3},{2,0},{3,1},{4,6},{5,7},{6,4},{7,5},{8,10},{9,11},{10,... | collective-permute-start | bytes 516104 | tf_op jit(solution)/shard_map/ppermute | solution.py:344
  69.0 7.6 %collective-permute-start.28 = (f32[4,1024]{1,0:T(4,128)S(1)}, f32[4,1024]{1,0:T(4,128)S(1)}, u32[]{:S(2)}, u32[]{:S(2)}) collective-permute-start(f32[4,1024]{1,0:T(4,128)S(1)} %get-tuple-element.158.refs_12_), channel_id=1, source_target_pairs={{0,4},{4,0},{8,12},{12,8},{1,5},{5,1},{9,13},{13,9},{2,6},{6,2},{1... | collective-permute-start | bytes 49160 | tf_op jit(solution)/shard_map/ppermute | solution.py:242
  69.4 7.2 %collective-permute-start.29 = (f32[4,1024]{1,0:T(4,128)S(1)}, f32[4,1024]{1,0:T(4,128)S(1)}, u32[]{:S(2)}, u32[]{:S(2)}) collective-permute-start(f32[4,1024]{1,0:T(4,128)S(1)} %get-tuple-element.159), channel_id=1, source_target_pairs={{0,12},{4,8},{8,4},{12,0},{1,13},{5,9},{9,5},{13,1},{2,14},{6,10},... | collective-permute-start | bytes 49160 | tf_op jit(solution)/shard_map/ppermute | solution.py:241
  78.2 7.8 %collective-permute-start.35 = (bf16[2,168,256]{2,1,0:T(8,128)(2,1)S(1)}, bf16[2,168,256]{2,1,0:T(8,128)(2,1)S(1)}, u32[]{:S(2)}, u32[]{:S(2)}) collective-permute-start(bf16[2,168,256]{2,1,0:T(8,128)(2,1)S(1)} %get-tuple-element.170.refs_17_), channel_id=1, source_target_pairs={{0,2},{1,3},{2,0},{3,1},{4,6},{5,7},{6,4},{7,5},{8,10},{9,11},{10,... | collective-permute-start | bytes 516104 | tf_op jit(solution)/shard_map/ppermute | solution.py:344
  79.8 6.2 %collective-permute-start.32 = (f32[4,1024]{1,0:T(4,128)S(1)}, f32[4,1024]{1,0:T(4,128)S(1)}, u32[]{:S(2)}, u32[]{:S(2)}) collective-permute-start(f32[4,1024]{1,0:T(4,128)S(1)} %get-tuple-element.168.refs_12_), channel_id=1, source_target_pairs={{0,4},{4,0},{8,12},{12,8},{1,5},{5,1},{9,13},{13,9},{2,6},{6,2},{1... | collective-permute-start | bytes 49160 | tf_op jit(solution)/shard_map/ppermute | solution.py:242
  79.9 6.2 %collective-permute-start.33 = (f32[4,1024]{1,0:T(4,128)S(1)}, f32[4,1024]{1,0:T(4,128)S(1)}, u32[]{:S(2)}, u32[]{:S(2)}) collective-permute-start(f32[4,1024]{1,0:T(4,128)S(1)} %get-tuple-element.169), channel_id=1, source_target_pairs={{0,12},{4,8},{8,4},{12,0},{1,13},{5,9},{9,5},{13,1},{2,14},{6,10},... | collective-permute-start | bytes 49160 | tf_op jit(solution)/shard_map/ppermute | solution.py:241
  90.5 6.2 %collective-permute-start.37 = (f32[2,168,128]{2,1,0:T(8,128)S(1)}, f32[2,168,128]{2,1,0:T(8,128)S(1)}, u32[]{:S(2)}, u32[]{:S(2)}) collective-permute-start(f32[2,168,128]{2,1,0:T(8,128)S(1)} %get-tuple-element.175), channel_id=1, source_target_pairs={{0,2},{1,3},{2,0},{3,1},{4,6},{5,7},{6,4},{7,5},{8,10},{9,11},{10,... | collective-permute-start | bytes 516104 | tf_op jit(solution)/shard_map/ppermute | solution.py:348
  91.2 8.0 %collective-permute-start.36 = (f32[2,168,512]{2,1,0:T(8,128)S(1)}, f32[2,168,512]{2,1,0:T(8,128)S(1)}, u32[]{:S(2)}, u32[]{:S(2)}) collective-permute-start(f32[2,168,512]{2,1,0:T(8,128)S(1)} %get-tuple-element.173), channel_id=1, source_target_pairs={{0,1},{1,0},{2,3},{3,2},{4,5},{5,4},{6,7},{7,6},{8,9},{9,8},{10,11... | collective-permute-start | bytes 2064392 | tf_op jit(solution)/shard_map/ppermute | solution.py:349
  (25 other events, 96.0 us)

commit v3 on v2

--- a/solution.py
+++ b/solution.py
@@ -7,6 +7,7 @@
 from jax.experimental import pallas as pl
 from jax.experimental.pallas import tpu as pltpu
 from jax.sharding import PartitionSpec as P
+
 
 ITERS = 8
 RAMP_WEIGHT = 0.5
@@ -22,6 +23,7 @@
 VMEM_LIMIT = 24 * 1024 * 1024
 
 IN_VMEM = pl.BlockSpec(memory_space=pltpu.VMEM)
+IN_SMEM = pl.BlockSpec(memory_space=pltpu.SMEM)
 IN_HBM = pl.BlockSpec(memory_space=pltpu.HBM)
 
 
@@ -70,32 +72,49 @@
 
 
 def give_body(mine, *refs):
-    count = (len(refs) - 1) // 2
+    *sources, out, sems = refs
     core = lax.rem(lax.axis_index("reg"), 2)
     given = pl.ds((1 - core) * mine, mine)
-    run_copies([(refs[i].at[given], refs[count + i]) for i in range(count)], refs[-1])
+    run_copies([(src.at[given], out.at[i]) for i, src in enumerate(sources)], sems)
 
 
 def held_body(mine, *refs):
-    count = (len(refs) - 1) // 2
+    *sources, out, dual_out, dem_out, sems = refs
     core = lax.rem(lax.axis_index("reg"), 2)
     held = pl.ds(core * mine, mine)
-    run_copies([(refs[i].at[held], refs[count + i]) for i in range(count)], refs[-1])
+    targets = [out.at[0], out.at[1], out.at[2], dual_out, dem_out]
+    run_copies([(src.at[held], dst) for src, dst in zip(sources, targets)], sems)
+
+
+def small_body(cost, mult, cons, capacity, own, give):
+    sections = cost.shape[0]
+    mine = own.shape[1]
+    core = lax.rem(lax.axis_index("reg"), 2)
+    for g in range(sections):
+        const = cost[g:g + 1, :] + mult[g] - PENALTY * cons[g]
+        for at, x in ((g, const), (sections + g, capacity[g])):
+            own[at] = jnp.where(core == 0, x[:mine], x[mine:])
+            give[at] = jnp.where(core == 0, x[mine:], x[:mine])
 
 
 def matrix_body(tile, mask, out):
     out[...] = tile[0] * mask[0].astype(F32).astype(BF16)
 
 
-def message_body(paired, *refs):
-    cap, prim, parts = refs[:2], refs[2:4], refs[4:6]
-    matrix, near, far = refs[6:]
-    mine, _, width = cap[0].shape
-    for half in range(2):
-        matrix[:, half * width:(half + 1) * width] = parts[half][...]
+def message_body(paired, own, twin, part, part_in, small, small_in, *outs):
+    matrix, const, invest, near, far = outs
+    _, mine, _, width = own.shape
+    sections = invest.shape[0]
+    matrix[:, :width] = part[...]
+    matrix[:, width:] = part_in[...]
+    for src, cols in ((small, slice(0, width)), (small_in, slice(width, 2 * width))):
+        const[:, :, cols] = src[:sections]
+        invest[:, :, cols] = src[sections:]
+    both = (own, twin)
     for s in range(mine):
         for half, cols, flat in tiles(width):
-            write_message(paired, near, far, s, flat, cap[half][s, :, cols], prim[half][s, :, cols])
+            src = both[half]
+            write_message(paired, near, far, s, flat, src[1, s, :, cols], src[0, s, :, cols])
 
 
 def is_odd():
@@ -116,22 +135,56 @@
     far[pl.ds(mine + s, 1), flat] = first
 
 
+def new_invest(hours_all, sums, invest, const):
+    mine = invest.shape[1]
+    parts = [part[:mine, :] for part in sums]
+    while len(parts) > 1:
+        parts = [u + v for u, v in zip(parts[0::2], parts[1::2])]
+    mean = parts[0] / hours_all
+    olds = [invest[g] for g in range(invest.shape[0])]
+    news = [
+        jnp.maximum(old - STEP_INVEST * (const[g] + PENALTY * old - mean), 0.0)
+        for g, old in enumerate(olds)
+    ]
+    return olds, news
+
+
+def invest_body(hours_all, sums_count, *refs):
+    invest, const = refs[:2]
+    keep, give = refs[2 + sums_count:]
+    width = keep.shape[2]
+    for g, new in enumerate(new_invest(hours_all, refs[2:2 + sums_count], invest, const)[1]):
+        keep[g] = new[:, :width]
+        give[g] = new[:, width:]
+
+
 def step_body(hours_all, paired, sums_count, first, last, *refs):
     refs = list(refs)
     take = lambda count: [refs.pop(0) for _ in range(count)]
-    matrix, cost, prim, cap = take(1)[0], take(2), take(2), take(2)
-    dual, invest, const, near, far = take(5)
-    sums = take(sums_count)
-    if not first:
+    matrix, own, twin, dual, near, far = take(6)
+    both = (own, twin)
+    cost = [src.at[2] for src in both]
+    if first:
+        prim, cap = [src.at[0] for src in both], [src.at[1] for src in both]
+    else:
+        prim, cap = take(2), take(2)
         dem, sent, carry, received = take(4)
+    if not last:
+        invest, const = take(2)
+        sums = take(sums_count)
     prim_out = take(2)
     if last:
-        inv_keep, inv_give, base_out, rows_give = take(4)
+        base_out, rows_give = take(2)
     else:
         cap_out = take(2)
         invest_out, near_out, far_out, sent_out, carry_out = take(5)
         if not first:
             dual_out = take(1)[0]
+        olds, news = new_invest(hours_all, sums, invest, const)
+        limits = 0.0
+        for g, (old, new) in enumerate(zip(olds, news)):
+            invest_out[g] = new
+            limits = limits + (2.0 * new - old)
     ext_low = take(1)[0]
     mine, hours, width = prim[0].shape
     chip = lax.axis_index("reg") // 2
@@ -147,18 +200,8 @@
             if not last:
                 dual_out[s] = multipliers
         low = multipliers.astype(BF16)
-        parts = [part[s:s + 1, :] for part in sums]
-        while len(parts) > 1:
-            parts = [u + v for u, v in zip(parts[0::2], parts[1::2])]
-        old_inv = invest[s]
-        grad_inv = const[s] + PENALTY * old_inv - parts[0] / hours_all
-        new_inv = jnp.maximum(old_inv - STEP_INVEST * grad_inv, 0.0)
-        if last:
-            inv_keep[s] = new_inv[:, :width]
-            inv_give[s] = new_inv[:, width:]
-        else:
-            invest_out[s] = new_inv
-        limit = jnp.sum(2.0 * new_inv - old_inv, axis=0, keepdims=True)
+        if not last:
+            limit = limits[s:s + 1, :]
         before = near[mine + s:mine + s + 1, :]
         after = far[mine + s:mine + s + 1, :]
         if paired:
@@ -221,14 +264,61 @@
     )[0]
 
 
-def dual_body(base, got, keep, give):
-    core = lax.rem(lax.axis_index("reg"), 2)
-    part = keep.shape[2]
-    for s in range(base.shape[0]):
-        new = jnp.maximum(base[s] - STEP_DUAL * got[s], 0.0)
-        low, high = new[:, :part], new[:, part:]
-        keep[s] = jnp.where(core == 0, low, high)
+def dual_body(base, got, out, give, kept, sem):
+    core = lax.rem(lax.axis_index("reg"), 2)
+    mine, part = give.shape[:2]
+    for s in range(mine):
+        new = jnp.maximum(base[s] - STEP_DUAL * got[s], 0.0).T
+        low, high = new[:part], new[part:]
+        kept[s] = jnp.where(core == 0, low, high)
         give[s] = jnp.where(core == 0, high, low)
+    run_copies([(kept, out.at[pl.ds(core * mine, mine)])], sem)
+
+
+def rest_body(got, _, out, sem):
+    core = lax.rem(lax.axis_index("reg"), 2)
+    mine = got.shape[0]
+    run_copies([(got, out.at[pl.ds((1 - core) * mine, mine)])], sem)
+
+
+def node_weights(nodes, weights, g, s, n):
+    return jnp.where(nodes[g, s] == n, weights[s], 0.0)
+
+
+def nodes_body(node_count, keep, got, nodes, weights, capacity, packed):
+    core = lax.rem(lax.axis_index("reg"), 2)
+    sections, mine, width = keep.shape
+    for g in range(sections):
+        first = jnp.where(core == 0, keep[g], got[g])
+        second = jnp.where(core == 0, got[g], keep[g])
+        capacity[g, :mine] = first
+        capacity[g, mine:] = second
+        for n in range(node_count):
+            total = jnp.zeros((1, width), F32)
+            mass = jnp.zeros((1, 128), F32)
+            for s in range(2 * mine):
+                weight = node_weights(nodes, weights, g, s, n)
+                row = first[s:s + 1] if s < mine else second[s - mine:s - mine + 1]
+                total = total + weight * row
+                mass = mass + weight
+            packed[g, n:n + 1, :width] = total
+            packed[g, n:n + 1, width:] = mass
+
+
+def multiplier_body(mult, capacity, nodes, *refs):
+    *packs, out = refs
+    sections, scens, width = capacity.shape
+    for g in range(sections):
+        packed = packs[0][g]
+        for other in packs[1:]:
+            packed = packed + other[g]
+        mass = packed[:, width:width + 1]
+        average = packed[:, :width] / jnp.where(mass > 0.0, mass, 1.0)
+        for s in range(scens):
+            mine = jnp.zeros((1, width), F32)
+            for n in range(packed.shape[0]):
+                mine = mine + jnp.where(nodes[g, s] == n, average[n:n + 1], 0.0)
+            out[g, s:s + 1] = mult[g, s:s + 1] + PENALTY * (capacity[g, s:s + 1] - mine)
 
 
 def hour_exchange(near, far, mine, paired):
@@ -262,7 +352,6 @@
     reg_count = lax.axis_size("reg")
     assert reg_count == 4
     paired = lax.axis_size("hour") == 4
-    core = lax.axis_index("reg") % 2
     nscen, hours, width = dispatch.shape
     rows = dual.shape[2]
     mine = nscen // 2
@@ -271,60 +360,61 @@
     twin = [(i, i ^ 1) for i in range(reg_count)]
     other_chip = [(i, i ^ 2) for i in range(reg_count)]
     half_full = in_vmem((mine, hours, width))
+    three = in_vmem((3, mine, hours, width))
     dual_like = in_vmem((mine, hours, rows))
     message = in_vmem((2 * mine, 2 * width))
-    invest_like = in_vmem((mine, sections, 2 * width))
-
-    def held(x):
-        return lax.dynamic_slice_in_dim(x, core * mine, mine, 0)
-
-    def given(x):
-        return lax.dynamic_slice_in_dim(x, (1 - core) * mine, mine, 0)
-
-    prim_give, cap_give, cost_give = call(
+    invest_like = in_vmem((sections, mine, 2 * width))
+    small_like = in_vmem((2 * sections, mine, width))
+    inv_half = in_vmem((sections, mine, width))
+    by_section = lambda x: jnp.transpose(x, (1, 0, 2))
+    mult, cons, caps = by_section(multiplier), by_section(consensus), by_section(capacity)
+
+    (give,) = call(
         functools.partial(give_body, mine),
-        (half_full,) * 3,
+        (three,),
         (dispatch, cap_dual, cost_rate),
         arg_specs=[IN_HBM] * 3,
         scratch=(pltpu.SemaphoreType.DMA((3,)),),
     )
-    prim_twin = lax.ppermute(prim_give, "reg", twin)
-    cap_twin = lax.ppermute(cap_give, "reg", twin)
-    cost_twin = lax.ppermute(cost_give, "reg", twin)
-    (matrix_own,) = call(matrix_body, (in_vmem(tile.shape[1:], BF16),), (tile, tile_mask))
-    matrix_twin = lax.ppermute(matrix_own, "reg", twin)
-    prim_own, cap_own, cost_own, dual_var, dem = call(
+    twin_in = lax.ppermute(give, "reg", twin)
+    (part,) = call(matrix_body, (in_vmem(tile.shape[1:], BF16),), (tile, tile_mask))
+    part_in = lax.ppermute(part, "reg", twin)
+    small, small_give = call(small_body, (small_like,) * 2, (invest_cost, mult, cons, caps))
+    small_in = lax.ppermute(small_give, "reg", twin)
+    own, dual_var, dem = call(
         functools.partial(held_body, mine),
-        (half_full,) * 3 + (dual_like,) * 2,
+        (three, dual_like, dual_like),
         (dispatch, cap_dual, cost_rate, dual, demand),
         arg_specs=[IN_HBM] * 5,
         scratch=(pltpu.SemaphoreType.DMA((5,)),),
     )
-    prim, cap, cost = (prim_own, prim_twin), (cap_own, cap_twin), (cost_own, cost_twin)
-    matrix, near, far = call(
+    matrix, const, invest, near, far = call(
         functools.partial(message_body, paired),
-        (in_vmem((rows, 2 * width), BF16), message, message),
-        (*cap, *prim, matrix_own, matrix_twin),
-    )
-    small = jnp.concatenate(
-        [invest_cost[None] + multiplier - PENALTY * consensus, capacity], axis=1
-    )
-    small_all = jnp.concatenate([held(small), lax.ppermute(given(small), "reg", twin)], axis=2)
-    const, invest = small_all[:, :sections], small_all[:, sections:]
+        (in_vmem((rows, 2 * width), BF16), invest_like, invest_like, message, message),
+        (own, twin_in, part, part_in, small, small_in),
+    )
+    near_in, far_in, sums = hour_exchange(near, far, mine, paired)
 
     flops = 4 * mine * hours * rows * 2 * width
+    prim = cap = ()
     sent = carry = received = None
     for step in range(ITERS):
         first, last = step == 0, step + 1 == ITERS
-        near_in, far_in, sums = hour_exchange(near, far, mine, paired)
-        args = [matrix, *cost, *prim, *cap, dual_var, invest, const, near_in, far_in, *sums]
+        args = [matrix, own, twin_in, dual_var, near_in, far_in, *prim, *cap]
         if not first:
             args += [dem, sent, carry, received]
+        outs = [half_full] * 2
         if last:
-            outs = [half_full] * 2 + [in_vmem((mine, sections, width))] * 2
+            inv_keep, inv_give = call(
+                functools.partial(invest_body, hours_all, len(sums)),
+                (inv_half,) * 2,
+                (invest, const, *sums),
+            )
+            inv_got = lax.ppermute(inv_give, "reg", twin)
             outs += [in_vmem((mine, hours, rows // 2))] * 2
         else:
-            outs = [half_full] * 4 + [invest_like, message, message]
+            args += [invest, const, *sums]
+            outs += [half_full] * 2 + [invest_like, message, message]
             outs += [in_vmem((mine, hours, rows), BF16), dual_like]
             if not first:
                 outs += [dual_like]
@@ -336,55 +426,62 @@
             flops=flops,
         )
         prim = got[:2]
-        if last:
-            inv_keep, inv_give, base, rows_give = got[2:]
-        else:
+        if not last:
             cap = got[2:4]
             invest, near, far, sent, carry = got[4:9]
             received = lax.ppermute(sent, "reg", other_chip)
             if not first:
                 dual_var = got[9]
-
-    rows_got = lax.ppermute(rows_give, "reg", other_chip)
-    prim_got = lax.ppermute(prim[1], "reg", twin)
-    inv_got = lax.ppermute(inv_give, "reg", twin)
-    capacity_out = jnp.where(
-        core == 0,
-        jnp.concatenate([inv_keep, inv_got], axis=0),
-        jnp.concatenate([inv_got, inv_keep], axis=0),
-    )
-    scen_count = lax.axis_size("scen")
-    node_count = node_of.shape[1] * scen_count // 2
-    node_ids = jnp.arange(node_count, dtype=jnp.int32)
-    one_hot = (node_of[:, :, None] == node_ids[None, None, :]).astype(F32)
-    weights = one_hot * scen_weight[None, :, None]
-    node_sum = jnp.sum(
-        weights[:, :, :, None] * jnp.transpose(capacity_out, (1, 0, 2))[:, :, None, :], axis=1
-    )
-    node_mass = jnp.sum(weights, axis=1)
-    packed = jnp.concatenate(
-        [node_sum, jnp.broadcast_to(node_mass[:, :, None], node_mass.shape + (128,))], axis=2
-    )
-    if scen_count == 2:
-        packed = packed + lax.ppermute(packed, "scen", [(0, 1), (1, 0)])
-    else:
-        packed = lax.psum(packed, "scen")
-    sum_total, mass_total = packed[:, :, :width], packed[:, :, width:width + 1]
-    average = sum_total / (mass_total + (mass_total <= 0.0).astype(F32))
-    spread_back = jnp.sum(one_hot[:, :, :, None] * average[:, None, :, :], axis=2)
-    multiplier_out = multiplier + PENALTY * (capacity_out - jnp.transpose(spread_back, (1, 0, 2)))
-
-    dispatch_out = join(prim[0], prim_got)
-    dual_keep, dual_give = call(
-        dual_body, (in_vmem((mine, hours, rows // reg_count)),) * 2, (base, rows_got)
-    )
-    dual_got = lax.ppermute(dual_give, "reg", twin)
-    dual_out = jnp.where(
-        core == 0,
-        jnp.concatenate([dual_keep, dual_got], axis=0),
-        jnp.concatenate([dual_got, dual_keep], axis=0),
-    )
-    return (dispatch_out, dual_out, capacity_out, multiplier_out)
+            near_in, far_in, sums = hour_exchange(near, far, mine, paired)
+            continue
+        base, rows_give = got[2:]
+        rows_got = lax.ppermute(rows_give, "reg", other_chip)
+        prim_got = lax.ppermute(prim[1], "reg", twin)
+        scen_count = lax.axis_size("scen")
+        node_count = node_of.shape[1] * scen_count // 2
+        packed_like = in_vmem((sections, node_count, width + 128))
+        by_scen = in_vmem((sections, nscen, width))
+        capacity_out, packed = call(
+            functools.partial(nodes_body, node_count),
+            (by_scen, packed_like),
+            (inv_keep, inv_got, node_of, scen_weight),
+            arg_specs=[IN_VMEM, IN_VMEM, IN_SMEM, IN_SMEM],
+        )
+        if scen_count == 2:
+            packs = (packed, lax.ppermute(packed, "scen", [(0, 1), (1, 0)]))
+        else:
+            packs = (lax.psum(packed, "scen"),)
+        (multiplier_out,) = call(
+            multiplier_body,
+            (by_scen,),
+            (mult, capacity_out, node_of, *packs),
+            arg_specs=[IN_VMEM, IN_VMEM, IN_SMEM] + [IN_VMEM] * len(packs),
+        )
+        dispatch_out = join(prim[0], prim_got)
+        own_rows = rows // reg_count
+        dual_half, dual_give = call(
+            dual_body,
+            (shape((nscen, own_rows, hours)), in_vmem((mine, own_rows, hours))),
+            (base, rows_got),
+            out_specs=(IN_HBM, IN_VMEM),
+            scratch=(pltpu.VMEM((mine, own_rows, hours), F32), pltpu.SemaphoreType.DMA((1,))),
+        )
+        dual_got = lax.ppermute(dual_give, "reg", twin)
+        (dual_out,) = call(
+            rest_body,
+            (shape(dual_half.shape),),
+            (dual_got, dual_half),
+            arg_specs=[IN_VMEM, IN_HBM],
+            out_specs=(IN_HBM,),
+            scratch=(pltpu.SemaphoreType.DMA((1,)),),
+            aliases={1: 0},
+        )
+    return (
+        dispatch_out,
+        jnp.transpose(dual_out, (0, 2, 1)),
+        by_section(capacity_out),
+        by_section(multiplier_out),
+    )
 
 
 def solution(mesh):

time: 101 us -> 107 us (1.059)
  starting transfers between devices: 43.3 us -> 47.5 us
  Pallas kernels: 18 us -> 20 us
  waiting for transfers between devices: 35 us -> 36.8 us
    ppermute x8, starting transfers between devices: 13.5 us -> 19.7 us  [hour_exchange(): far_in = lax.ppermute(far, 'hour', partners(3))]
    ppermute x8, starting transfers between devices: 5 us -> 2.26 us  [hour_exchange(): near_in = lax.ppermute(near, 'hour', partners(1))]
    ppermute x1, waiting for transfers between devices: 3.5 us -> 5.91 us  [shards(): rows_got = lax.ppermute(rows_give, 'reg', other_chip)]
    ppermute x6 -> x4, waiting for transfers between devices: 1.19 us -> 3.46 us  [the longest x1 1.8 us: shards(): packs = (packed, lax.ppermute(packed, 'scen', [(0, 1), (1, 0)]))]
    pallas_call x14 -> x19, Pallas kernels: 18 us -> 20 us  [call(): pl.pallas_call(body, out_shape=tuple(outs), in_specs=arg_specs or [IN_VME...]
    ppermute x8, waiting for transfers between devices: 24.6 us -> 22.7 us  [hour_exchange(): across = lax.ppermute(near[:mine], 'hour', partners(2))]
    ppermute x8, starting transfers between devices: 12 us -> 13.8 us  [hour_exchange(): across = lax.ppermute(near[:mine], 'hour', partners(2))]
    unnamed x20 -> x18, local copies, waits for them, and re-layouts: 2.18 us -> 1.25 us
  transfers between devices with their start and end apart: 41 -> 39, of which waited for: 15 -> 13; matrix products, arithmetic and copies ran while one was open for 3% -> 1% of each run, Pallas kernels for 2% -> 4%
where the time goes in v3:
time: 107 us
  starting transfers between devices  47.5 us (44%)
  waiting for transfers between devices  36.8 us (34%)
  Pallas kernels  20 us (19%)
  local copies, waits for them, and re-layouts  1.28 us (1%)
  between operations  1.09 us (1%)
    ppermute x8, waiting for transfers between devices, hour_exchange(): across = lax.ppermute(near[:mine], 'hour', partners(2))  22.7 us
    pallas_call x19, Pallas kernels, call(): pl.pallas_call(body, out_shape=tuple(outs), in_specs=arg_specs or [IN_VME...  20 us
    ppermute x8, starting transfers between devices, hour_exchange(): far_in = lax.ppermute(far, 'hour', partners(3))  19.7 us
    ppermute x8, starting transfers between devices, hour_exchange(): across = lax.ppermute(near[:mine], 'hour', partners(2))  13.8 us
    ppermute x7, starting transfers between devices, shards(): received = lax.ppermute(sent, 'reg', other_chip)  7.99 us
    ppermute x1, waiting for transfers between devices, shards(): rows_got = lax.ppermute(rows_give, 'reg', other_chip)  5.91 us
    ppermute x8, waiting for transfers between devices, hour_exchange(): far_in = lax.ppermute(far, 'hour', partners(3))  3.54 us
    ppermute x8, starting transfers between devices, hour_exchange(): near_in = lax.ppermute(near, 'hour', partners(1))  2.26 us
  transfers between devices with their start and end apart: 39, of which 13 were waited for; matrix products, arithmetic and copies ran while one was open for 1% of the time, Pallas kernels for 4%

profile of v3, /device:TPU:0, one launch (start us, length us, event | category | flops | bytes accessed | tf_op | source)
XLA Modules:
  0.0 106.8 jit_solution(14108062985893735125)
XLA Ops:
  0.7 1.6 %shard_map.157 = f32[3,2,168,512]{3,2,1,0:T(8,128)S(1)} custom-call(f32[4,168,512]{2,1,0:T(8,128)} %refs_0_.3, f32[4,168,512]{2,1,0:T(8,128)} %refs_1_.3, f32[4,168,512]{2,1,0:T(8,128)} %refs_2_.3), custom_call_target="tpu_custom_call" | custom-call | bytes 6193152 | tf_op jit(solution)/shard_map/pallas_call | solution.py:38
  3.6 1.7 %shard_map.156 = (f32[3,2,168,512]{3,2,1,0:T(8,128)S(1)}, f32[2,168,256]{2,1,0:T(8,128)S(1)}, f32[2,168,256]{2,1,0:T(8,128)S(1)}) custom-call(f32[4,168,512]{2,1,0:T(8,128)} %refs_0_.3, f32[4,168,512]{2,1,0:T(8,128)} %refs_1_.3, f32[4,168,512]{2,1,0:T(8,128)} %refs_2_.3, f32[4,168,256]{2,1,0:T(8,128)} %refs_3_.1, f32[4,168,256]{2,1,0:T(8,128)} %refs_4_.1), custom_call_target="tpu_custom_call" | custom-call | bytes 8257536 | tf_op jit(solution)/shard_map/pallas_call | solution.py:38
  5.4 1.7 %collective-permute-done.2.small_in = f32[6,2,512]{2,1,0:T(2,128)S(1)} collective-permute-done((f32[6,2,512]{2,1,0:T(2,128)S(1)}, f32[6,2,512]{2,1,0:T(2,128)S(1)}, u32[]{:S(2)}, u32[]{:S(2)}) %collective-permute-start.2) | collective-permute-done | bytes 24608 | tf_op jit(solution)/shard_map/ppermute | solution.py:383
  7.2 5.0 %collective-permute-start.4 = (f32[4,1024]{1,0:T(4,128)S(1)}, f32[4,1024]{1,0:T(4,128)S(1)}, u32[]{:S(2)}, u32[]{:S(2)}) collective-permute-start(f32[4,1024]{1,0:T(4,128)S(1)} %get-tuple-element.99), channel_id=1, source_target_pairs={{0,12},{4,8},{8,4},{12,0},{1,13},{5,9},{9,5},{13,1},{2,14},{6,10},... | collective-permute-start | bytes 49160 | tf_op jit(solution)/shard_map/ppermute | solution.py:331
  12.8 3.9 %collective-permute-done.5.refs_10_ = f32[2,1024]{1,0:T(2,128)S(1)} collective-permute-done((f32[2,1024]{1,0:T(2,128)S(1)}, f32[2,1024]{1,0:T(2,128)S(1)}, u32[]{:S(2)}, u32[]{:S(2)}) %collective-permute-start.5) | collective-permute-done | bytes 8224 | tf_op jit(solution)/shard_map/ppermute | solution.py:333
  21.9 2.4 %collective-permute-start.9 = (f32[2,1024]{1,0:T(2,128)S(1)}, f32[2,1024]{1,0:T(2,128)S(1)}, u32[]{:S(2)}, u32[]{:S(2)}) collective-permute-start(f32[2,1024]{1,0:T(2,128)S(1)} %slice.25), channel_id=1, source_target_pairs={{0,8},{4,12},{8,0},{12,4},{1,9},{5,13},{9,1},{13,5},{2,10},{6,14},... | collective-permute-start | bytes 24584 | tf_op jit(solution)/shard_map/ppermute | solution.py:333
  24.3 2.2 %collective-permute-done.9.refs_18_ = f32[2,1024]{1,0:T(2,128)S(1)} collective-permute-done((f32[2,1024]{1,0:T(2,128)S(1)}, f32[2,1024]{1,0:T(2,128)S(1)}, u32[]{:S(2)}, u32[]{:S(2)}) %collective-permute-start.9) | collective-permute-done | bytes 8224 | tf_op jit(solution)/shard_map/ppermute | solution.py:333
  28.6 2.9 %collective-permute-start.11 = (f32[4,1024]{1,0:T(4,128)S(1)}, f32[4,1024]{1,0:T(4,128)S(1)}, u32[]{:S(2)}, u32[]{:S(2)}) collective-permute-start(f32[4,1024]{1,0:T(4,128)S(1)} %get-tuple-element.114), channel_id=1, source_target_pairs={{0,12},{4,8},{8,4},{12,0},{1,13},{5,9},{9,5},{13,1},{2,14},{6,10},... | collective-permute-start | bytes 49160 | tf_op jit(solution)/shard_map/ppermute | solution.py:331
  33.0 3.1 %collective-permute-done.13.refs_18_ = f32[2,1024]{1,0:T(2,128)S(1)} collective-permute-done((f32[2,1024]{1,0:T(2,128)S(1)}, f32[2,1024]{1,0:T(2,128)S(1)}, u32[]{:S(2)}, u32[]{:S(2)}) %collective-permute-start.13) | collective-permute-done | bytes 8224 | tf_op jit(solution)/shard_map/ppermute | solution.py:333
  41.3 2.4 %collective-permute-start.17 = (f32[2,1024]{1,0:T(2,128)S(1)}, f32[2,1024]{1,0:T(2,128)S(1)}, u32[]{:S(2)}, u32[]{:S(2)}) collective-permute-start(f32[2,1024]{1,0:T(2,128)S(1)} %slice.27), channel_id=1, source_target_pairs={{0,8},{4,12},{8,0},{12,4},{1,9},{5,13},{9,1},{13,5},{2,10},{6,14},... | collective-permute-start | bytes 24584 | tf_op jit(solution)/shard_map/ppermute | solution.py:333
  43.7 2.2 %collective-permute-done.17.refs_18_ = f32[2,1024]{1,0:T(2,128)S(1)} collective-permute-done((f32[2,1024]{1,0:T(2,128)S(1)}, f32[2,1024]{1,0:T(2,128)S(1)}, u32[]{:S(2)}, u32[]{:S(2)}) %collective-permute-start.17) | collective-permute-done | bytes 8224 | tf_op jit(solution)/shard_map/ppermute | solution.py:333
  45.9 1.6 %shard_map.164 = (f32[2,168,512]{2,1,0:T(8,128)S(1)}, f32[2,168,512]{2,1,0:T(8,128)S(1)}, f32[2,168,512]{2,1,0:T(8,128)S(1)}, f32[2,168,512]{2,1,0:T(8,128)S(1)}...) custom-call(bf16[256,1024]{1,0:T(8,128)(2,1)S(1)} %get-tuple-element, ...), custom_call_target="tpu_custom_call" | custom-call | flops 352321536 | bytes 12591104 | tf_op jit(solution)/shard_map/pallas_call | solution.py:38
  48.1 3.0 %collective-permute-start.19 = (f32[4,1024]{1,0:T(4,128)S(1)}, f32[4,1024]{1,0:T(4,128)S(1)}, u32[]{:S(2)}, u32[]{:S(2)}) collective-permute-start(f32[4,1024]{1,0:T(4,128)S(1)} %get-tuple-element.134), channel_id=1, source_target_pairs={{0,12},{4,8},{8,4},{12,0},{1,13},{5,9},{9,5},{13,1},{2,14},{6,10},... | collective-permute-start | bytes 49160 | tf_op jit(solution)/shard_map/ppermute | solution.py:331
  52.5 3.2 %collective-permute-done.21.refs_18_ = f32[2,1024]{1,0:T(2,128)S(1)} collective-permute-done((f32[2,1024]{1,0:T(2,128)S(1)}, f32[2,1024]{1,0:T(2,128)S(1)}, u32[]{:S(2)}, u32[]{:S(2)}) %collective-permute-start.21) | collective-permute-done | bytes 8224 | tf_op jit(solution)/shard_map/ppermute | solution.py:333
  60.8 2.4 %collective-permute-start.25 = (f32[2,1024]{1,0:T(2,128)S(1)}, f32[2,1024]{1,0:T(2,128)S(1)}, u32[]{:S(2)}, u32[]{:S(2)}) collective-permute-start(f32[2,1024]{1,0:T(2,128)S(1)} %slice.29), channel_id=1, source_target_pairs={{0,8},{4,12},{8,0},{12,4},{1,9},{5,13},{9,1},{13,5},{2,10},{6,14},... | collective-permute-start | bytes 24584 | tf_op jit(solution)/shard_map/ppermute | solution.py:333
  63.1 2.2 %collective-permute-done.25.refs_18_ = f32[2,1024]{1,0:T(2,128)S(1)} collective-permute-done((f32[2,1024]{1,0:T(2,128)S(1)}, f32[2,1024]{1,0:T(2,128)S(1)}, u32[]{:S(2)}, u32[]{:S(2)}) %collective-permute-start.25) | collective-permute-done | bytes 8224 | tf_op jit(solution)/shard_map/ppermute | solution.py:333
  67.6 2.9 %collective-permute-start.27 = (f32[4,1024]{1,0:T(4,128)S(1)}, f32[4,1024]{1,0:T(4,128)S(1)}, u32[]{:S(2)}, u32[]{:S(2)}) collective-permute-start(f32[4,1024]{1,0:T(4,128)S(1)} %get-tuple-element.154), channel_id=1, source_target_pairs={{0,12},{4,8},{8,4},{12,0},{1,13},{5,9},{9,5},{13,1},{2,14},{6,10},... | collective-permute-start | bytes 49160 | tf_op jit(solution)/shard_map/ppermute | solution.py:331
  72.0 3.1 %collective-permute-done.29.refs_18_ = f32[2,1024]{1,0:T(2,128)S(1)} collective-permute-done((f32[2,1024]{1,0:T(2,128)S(1)}, f32[2,1024]{1,0:T(2,128)S(1)}, u32[]{:S(2)}, u32[]{:S(2)}) %collective-permute-start.29) | collective-permute-done | bytes 8224 | tf_op jit(solution)/shard_map/ppermute | solution.py:333
  75.1 1.8 %shard_map.167 = (f32[2,168,512]{2,1,0:T(8,128)S(1)}, f32[2,168,512]{2,1,0:T(8,128)S(1)}, f32[2,168,512]{2,1,0:T(8,128)S(1)}, f32[2,168,512]{2,1,0:T(8,128)S(1)}...) custom-call(bf16[256,1024]{1,0:T(8,128)(2,1)S(1)} %get-tuple-element, ...), custom_call_target="tpu_custom_call" | custom-call | flops 352321536 | bytes 12591104 | tf_op jit(solution)/shard_map/pallas_call | solution.py:38
  80.4 3.5 %collective-permute-done.31.refs_5_ = f32[4,1024]{1,0:T(4,128)S(1)} collective-permute-done((f32[4,1024]{1,0:T(4,128)S(1)}, f32[4,1024]{1,0:T(4,128)S(1)}, u32[]{:S(2)}, u32[]{:S(2)}) %collective-permute-start.31) | collective-permute-done | bytes 16416 | tf_op jit(solution)/shard_map/ppermute | solution.py:331
  86.2 5.9 %collective-permute-done.34.got = f32[2,168,128]{2,1,0:T(8,128)S(1)} collective-permute-done((f32[2,168,128]{2,1,0:T(8,128)S(1)}, f32[2,168,128]{2,1,0:T(8,128)S(1)}, u32[]{:S(2)}, u32[]{:S(2)}) %collective-permute-start.34) | collective-permute-done | bytes 172064 | tf_op jit(solution)/shard_map/ppermute | solution.py:438
  93.0 1.7 %collective-permute-start.36 = (f32[2,1024]{1,0:T(2,128)S(1)}, f32[2,1024]{1,0:T(2,128)S(1)}, u32[]{:S(2)}, u32[]{:S(2)}) collective-permute-start(f32[2,1024]{1,0:T(2,128)S(1)} %slice.31), channel_id=1, source_target_pairs={{0,8},{4,12},{8,0},{12,4},{1,9},{5,13},{9,1},{13,5},{2,10},{6,14},... | collective-permute-start | bytes 24584 | tf_op jit(solution)/shard_map/ppermute | solution.py:333
  94.7 2.9 %collective-permute-done.36.refs_4_ = f32[2,1024]{1,0:T(2,128)S(1)} collective-permute-done((f32[2,1024]{1,0:T(2,128)S(1)}, f32[2,1024]{1,0:T(2,128)S(1)}, u32[]{:S(2)}, u32[]{:S(2)}) %collective-permute-start.36) | collective-permute-done | bytes 8224 | tf_op jit(solution)/shard_map/ppermute | solution.py:333
  101.7 1.8 %collective-permute-done.38.refs_1_ = f32[3,4,640]{2,1,0:T(4,128)S(1)} collective-permute-done((f32[3,4,640]{2,1,0:T(4,128)S(1)}, f32[3,4,640]{2,1,0:T(4,128)S(1)}, u32[]{:S(2)}, u32[]{:S(2)}) %collective-permute-start.38) | collective-permute-done | bytes 30752 | tf_op jit(solution)/shard_map/ppermute | solution.py:451
  (99 shorter events, 40.6 us)
Async XLA Ops:
  2.3 4.7 %collective-permute-start = (f32[3,2,168,512]{3,2,1,0:T(8,128)S(1)}, f32[3,2,168,512]{3,2,1,0:T(8,128)S(1)}, u32[]{:S(2)}, u32[]{:S(2)}) collective-permute-start(f32[3,2,168,512]{3,2,1,0:T(8,128)S(1)} %shard_map.157), channel_id=1, source_target_pairs={{0,1},{1,0},{2,3},{3,2},{4,5},{5,4},{6,7},{7,6},{8,9},{9,8},{10,11... | collective-permute-start | bytes 6193160 | tf_op jit(solution)/shard_map/ppermute | solution.py:379
  7.2 9.6 %collective-permute-start.4 = (f32[4,1024]{1,0:T(4,128)S(1)}, f32[4,1024]{1,0:T(4,128)S(1)}, u32[]{:S(2)}, u32[]{:S(2)}) collective-permute-start(f32[4,1024]{1,0:T(4,128)S(1)} %get-tuple-element.99), channel_id=1, source_target_pairs={{0,12},{4,8},{8,4},{12,0},{1,13},{5,9},{9,5},{13,1},{2,14},{6,10},... | collective-permute-start | bytes 49160 | tf_op jit(solution)/shard_map/ppermute | solution.py:331
  18.3 8.2 %collective-permute-start.8 = (bf16[2,168,256]{2,1,0:T(8,128)(2,1)S(1)}, bf16[2,168,256]{2,1,0:T(8,128)(2,1)S(1)}, u32[]{:S(2)}, u32[]{:S(2)}) collective-permute-start(bf16[2,168,256]{2,1,0:T(8,128)(2,1)S(1)} %get-tuple-element.109.refs_11_), channel_id=1, source_target_pairs={{0,2},{1,3},{2,0},{3,1},{4,6},{5,7},{6,4},{7,5},{8,10},{9,11},{10,... | collective-permute-start | bytes 516104 | tf_op jit(solution)/shard_map/ppermute | solution.py:432
  19.9 6.6 %collective-permute-start.7 = (f32[4,1024]{1,0:T(4,128)S(1)}, f32[4,1024]{1,0:T(4,128)S(1)}, u32[]{:S(2)}, u32[]{:S(2)}) collective-permute-start(f32[4,1024]{1,0:T(4,128)S(1)} %get-tuple-element.103), channel_id=1, source_target_pairs={{0,12},{4,8},{8,4},{12,0},{1,13},{5,9},{9,5},{13,1},{2,14},{6,10},... | collective-permute-start | bytes 49160 | tf_op jit(solution)/shard_map/ppermute | solution.py:331
  21.3 5.1 %collective-permute-start.6 = (f32[4,1024]{1,0:T(4,128)S(1)}, f32[4,1024]{1,0:T(4,128)S(1)}, u32[]{:S(2)}, u32[]{:S(2)}) collective-permute-start(f32[4,1024]{1,0:T(4,128)S(1)} %get-tuple-element.102.refs_16_), channel_id=1, source_target_pairs={{0,4},{4,0},{8,12},{12,8},{1,5},{5,1},{9,13},{13,9},{2,6},{6,2},{1... | collective-permute-start | bytes 49160 | tf_op jit(solution)/shard_map/ppermute | solution.py:332
  28.1 8.1 %collective-permute-start.12 = (bf16[2,168,256]{2,1,0:T(8,128)(2,1)S(1)}, bf16[2,168,256]{2,1,0:T(8,128)(2,1)S(1)}, u32[]{:S(2)}, u32[]{:S(2)}) collective-permute-start(bf16[2,168,256]{2,1,0:T(8,128)(2,1)S(1)} %get-tuple-element.119.refs_11_), channel_id=1, source_target_pairs={{0,2},{1,3},{2,0},{3,1},{4,6},{5,7},{6,4},{7,5},{8,10},{9,11},{10,... | collective-permute-start | bytes 516104 | tf_op jit(solution)/shard_map/ppermute | solution.py:432
  28.6 7.5 %collective-permute-start.11 = (f32[4,1024]{1,0:T(4,128)S(1)}, f32[4,1024]{1,0:T(4,128)S(1)}, u32[]{:S(2)}, u32[]{:S(2)}) collective-permute-start(f32[4,1024]{1,0:T(4,128)S(1)} %get-tuple-element.114), channel_id=1, source_target_pairs={{0,12},{4,8},{8,4},{12,0},{1,13},{5,9},{9,5},{13,1},{2,14},{6,10},... | collective-permute-start | bytes 49160 | tf_op jit(solution)/shard_map/ppermute | solution.py:331
  31.6 4.6 %collective-permute-start.10 = (f32[4,1024]{1,0:T(4,128)S(1)}, f32[4,1024]{1,0:T(4,128)S(1)}, u32[]{:S(2)}, u32[]{:S(2)}) collective-permute-start(f32[4,1024]{1,0:T(4,128)S(1)} %get-tuple-element.113.refs_16_), channel_id=1, source_target_pairs={{0,4},{4,0},{8,12},{12,8},{1,5},{5,1},{9,13},{13,9},{2,6},{6,2},{1... | collective-permute-start | bytes 49160 | tf_op jit(solution)/shard_map/ppermute | solution.py:332
  37.7 8.2 %collective-permute-start.16 = (bf16[2,168,256]{2,1,0:T(8,128)(2,1)S(1)}, bf16[2,168,256]{2,1,0:T(8,128)(2,1)S(1)}, u32[]{:S(2)}, u32[]{:S(2)}) collective-permute-start(bf16[2,168,256]{2,1,0:T(8,128)(2,1)S(1)} %get-tuple-element.129.refs_11_), channel_id=1, source_target_pairs={{0,2},{1,3},{2,0},{3,1},{4,6},{5,7},{6,4},{7,5},{8,10},{9,11},{10,... | collective-permute-start | bytes 516104 | tf_op jit(solution)/shard_map/ppermute | solution.py:432
  39.3 6.6 %collective-permute-start.15 = (f32[4,1024]{1,0:T(4,128)S(1)}, f32[4,1024]{1,0:T(4,128)S(1)}, u32[]{:S(2)}, u32[]{:S(2)}) collective-permute-start(f32[4,1024]{1,0:T(4,128)S(1)} %get-tuple-element.124), channel_id=1, source_target_pairs={{0,12},{4,8},{8,4},{12,0},{1,13},{5,9},{9,5},{13,1},{2,14},{6,10},... | collective-permute-start | bytes 49160 | tf_op jit(solution)/shard_map/ppermute | solution.py:331
  40.8 5.1 %collective-permute-start.14 = (f32[4,1024]{1,0:T(4,128)S(1)}, f32[4,1024]{1,0:T(4,128)S(1)}, u32[]{:S(2)}, u32[]{:S(2)}) collective-permute-start(f32[4,1024]{1,0:T(4,128)S(1)} %get-tuple-element.123.refs_16_), channel_id=1, source_target_pairs={{0,4},{4,0},{8,12},{12,8},{1,5},{5,1},{9,13},{13,9},{2,6},{6,2},{1... | collective-permute-start | bytes 49160 | tf_op jit(solution)/shard_map/ppermute | solution.py:332
  47.5 8.2 %collective-permute-start.20 = (bf16[2,168,256]{2,1,0:T(8,128)(2,1)S(1)}, bf16[2,168,256]{2,1,0:T(8,128)(2,1)S(1)}, u32[]{:S(2)}, u32[]{:S(2)}) collective-permute-start(bf16[2,168,256]{2,1,0:T(8,128)(2,1)S(1)} %get-tuple-element.139.refs_11_), channel_id=1, source_target_pairs={{0,2},{1,3},{2,0},{3,1},{4,6},{5,7},{6,4},{7,5},{8,10},{9,11},{10,... | collective-permute-start | bytes 516104 | tf_op jit(solution)/shard_map/ppermute | solution.py:432
  48.1 7.6 %collective-permute-start.19 = (f32[4,1024]{1,0:T(4,128)S(1)}, f32[4,1024]{1,0:T(4,128)S(1)}, u32[]{:S(2)}, u32[]{:S(2)}) collective-permute-start(f32[4,1024]{1,0:T(4,128)S(1)} %get-tuple-element.134), channel_id=1, source_target_pairs={{0,12},{4,8},{8,4},{12,0},{1,13},{5,9},{9,5},{13,1},{2,14},{6,10},... | collective-permute-start | bytes 49160 | tf_op jit(solution)/shard_map/ppermute | solution.py:331
  57.2 8.1 %collective-permute-start.24 = (bf16[2,168,256]{2,1,0:T(8,128)(2,1)S(1)}, bf16[2,168,256]{2,1,0:T(8,128)(2,1)S(1)}, u32[]{:S(2)}, u32[]{:S(2)}) collective-permute-start(bf16[2,168,256]{2,1,0:T(8,128)(2,1)S(1)} %get-tuple-element.149.refs_11_), channel_id=1, source_target_pairs={{0,2},{1,3},{2,0},{3,1},{4,6},{5,7},{6,4},{7,5},{8,10},{9,11},{10,... | collective-permute-start | bytes 516104 | tf_op jit(solution)/shard_map/ppermute | solution.py:432
  58.7 6.6 %collective-permute-start.23 = (f32[4,1024]{1,0:T(4,128)S(1)}, f32[4,1024]{1,0:T(4,128)S(1)}, u32[]{:S(2)}, u32[]{:S(2)}) collective-permute-start(f32[4,1024]{1,0:T(4,128)S(1)} %get-tuple-element.144), channel_id=1, source_target_pairs={{0,12},{4,8},{8,4},{12,0},{1,13},{5,9},{9,5},{13,1},{2,14},{6,10},... | collective-permute-start | bytes 49160 | tf_op jit(solution)/shard_map/ppermute | solution.py:331
  60.2 5.1 %collective-permute-start.22 = (f32[4,1024]{1,0:T(4,128)S(1)}, f32[4,1024]{1,0:T(4,128)S(1)}, u32[]{:S(2)}, u32[]{:S(2)}) collective-permute-start(f32[4,1024]{1,0:T(4,128)S(1)} %get-tuple-element.143.refs_16_), channel_id=1, source_target_pairs={{0,4},{4,0},{8,12},{12,8},{1,5},{5,1},{9,13},{13,9},{2,6},{6,2},{1... | collective-permute-start | bytes 49160 | tf_op jit(solution)/shard_map/ppermute | solution.py:332
  66.9 8.2 %collective-permute-start.28 = (bf16[2,168,256]{2,1,0:T(8,128)(2,1)S(1)}, bf16[2,168,256]{2,1,0:T(8,128)(2,1)S(1)}, u32[]{:S(2)}, u32[]{:S(2)}) collective-permute-start(bf16[2,168,256]{2,1,0:T(8,128)(2,1)S(1)} %get-tuple-element.159.refs_11_), channel_id=1, source_target_pairs={{0,2},{1,3},{2,0},{3,1},{4,6},{5,7},{6,4},{7,5},{8,10},{9,11},{10,... | collective-permute-start | bytes 516104 | tf_op jit(solution)/shard_map/ppermute | solution.py:432
  67.6 7.5 %collective-permute-start.27 = (f32[4,1024]{1,0:T(4,128)S(1)}, f32[4,1024]{1,0:T(4,128)S(1)}, u32[]{:S(2)}, u32[]{:S(2)}) collective-permute-start(f32[4,1024]{1,0:T(4,128)S(1)} %get-tuple-element.154), channel_id=1, source_target_pairs={{0,12},{4,8},{8,4},{12,0},{1,13},{5,9},{9,5},{13,1},{2,14},{6,10},... | collective-permute-start | bytes 49160 | tf_op jit(solution)/shard_map/ppermute | solution.py:331
  76.8 7.0 %collective-permute-start.32 = (bf16[2,168,256]{2,1,0:T(8,128)(2,1)S(1)}, bf16[2,168,256]{2,1,0:T(8,128)(2,1)S(1)}, u32[]{:S(2)}, u32[]{:S(2)}) collective-permute-start(bf16[2,168,256]{2,1,0:T(8,128)(2,1)S(1)} %get-tuple-element.169.refs_11_), channel_id=1, source_target_pairs={{0,2},{1,3},{2,0},{3,1},{4,6},{5,7},{6,4},{7,5},{8,10},{9,11},{10,... | collective-permute-start | bytes 516104 | tf_op jit(solution)/shard_map/ppermute | solution.py:432
  78.3 5.5 %collective-permute-start.31 = (f32[4,1024]{1,0:T(4,128)S(1)}, f32[4,1024]{1,0:T(4,128)S(1)}, u32[]{:S(2)}, u32[]{:S(2)}) collective-permute-start(f32[4,1024]{1,0:T(4,128)S(1)} %get-tuple-element.164), channel_id=1, source_target_pairs={{0,12},{4,8},{8,4},{12,0},{1,13},{5,9},{9,5},{13,1},{2,14},{6,10},... | collective-permute-start | bytes 49160 | tf_op jit(solution)/shard_map/ppermute | solution.py:331
  85.3 20.2 %collective-permute-start.33 = (f32[2,168,512]{2,1,0:T(8,128)S(1)}, f32[2,168,512]{2,1,0:T(8,128)S(1)}, u32[]{:S(2)}, u32[]{:S(2)}) collective-permute-start(f32[2,168,512]{2,1,0:T(8,128)S(1)} %get-tuple-element.172), channel_id=1, source_target_pairs={{0,1},{1,0},{2,3},{3,2},{4,5},{5,4},{6,7},{7,6},{8,9},{9,8},{10,11... | collective-permute-start | bytes 2064392 | tf_op jit(solution)/shard_map/ppermute | solution.py:439
  85.3 6.8 %collective-permute-start.34 = (f32[2,168,128]{2,1,0:T(8,128)S(1)}, f32[2,168,128]{2,1,0:T(8,128)S(1)}, u32[]{:S(2)}, u32[]{:S(2)}) collective-permute-start(f32[2,168,128]{2,1,0:T(8,128)S(1)} %get-tuple-element.174), channel_id=1, source_target_pairs={{0,2},{1,3},{2,0},{3,1},{4,6},{5,7},{6,4},{7,5},{8,10},{9,11},{10,... | collective-permute-start | bytes 516104 | tf_op jit(solution)/shard_map/ppermute | solution.py:438
  92.9 11.9 %collective-permute-start.35 = (f32[2,64,168]{2,1,0:T(8,128)S(1)}, f32[2,64,168]{2,1,0:T(8,128)S(1)}, u32[]{:S(2)}, u32[]{:S(2)}) collective-permute-start(f32[2,64,168]{2,1,0:T(8,128)S(1)} %get-tuple-element.175), channel_id=1, source_target_pairs={{0,1},{1,0},{2,3},{3,2},{4,5},{5,4},{6,7},{7,6},{8,9},{9,8},{10,11... | collective-permute-start | bytes 258056 | tf_op jit(solution)/shard_map/ppermute | solution.py:469
  93.0 4.6 %collective-permute-start.36 = (f32[2,1024]{1,0:T(2,128)S(1)}, f32[2,1024]{1,0:T(2,128)S(1)}, u32[]{:S(2)}, u32[]{:S(2)}) collective-permute-start(f32[2,1024]{1,0:T(2,128)S(1)} %slice.31), channel_id=1, source_target_pairs={{0,8},{4,12},{8,0},{12,4},{1,9},{5,13},{9,1},{13,5},{2,10},{6,14},... | collective-permute-start | bytes 24584 | tf_op jit(solution)/shard_map/ppermute | solution.py:333
  (23 other events, 106.9 us)

commit v4 on v3

--- a/solution.py
+++ b/solution.py
@@ -102,7 +102,7 @@
 
 
 def message_body(paired, own, twin, part, part_in, small, small_in, *outs):
-    matrix, const, invest, near, far = outs
+    matrix, const, invest, near, far, mean = outs
     _, mine, _, width = own.shape
     sections = invest.shape[0]
     matrix[:, :width] = part[...]
@@ -115,6 +115,7 @@
         for half, cols, flat in tiles(width):
             src = both[half]
             write_message(paired, near, far, s, flat, src[1, s, :, cols], src[0, s, :, cols])
+    mean[...] = near[:mine, :]
 
 
 def is_odd():
@@ -158,7 +159,7 @@
         give[g] = new[:, width:]
 
 
-def step_body(hours_all, paired, sums_count, first, last, *refs):
+def primal_body(paired, first, last, *refs):
     refs = list(refs)
     take = lambda count: [refs.pop(0) for _ in range(count)]
     matrix, own, twin, dual, near, far = take(6)
@@ -169,22 +170,13 @@
     else:
         prim, cap = take(2), take(2)
         dem, sent, carry, received = take(4)
-    if not last:
-        invest, const = take(2)
-        sums = take(sums_count)
     prim_out = take(2)
     if last:
         base_out, rows_give = take(2)
     else:
-        cap_out = take(2)
-        invest_out, near_out, far_out, sent_out, carry_out = take(5)
+        sent_out, carry_out = take(2)
         if not first:
             dual_out = take(1)[0]
-        olds, news = new_invest(hours_all, sums, invest, const)
-        limits = 0.0
-        for g, (old, new) in enumerate(zip(olds, news)):
-            invest_out[g] = new
-            limits = limits + (2.0 * new - old)
     ext_low = take(1)[0]
     mine, hours, width = prim[0].shape
     chip = lax.axis_index("reg") // 2
@@ -200,8 +192,6 @@
             if not last:
                 dual_out[s] = multipliers
         low = multipliers.astype(BF16)
-        if not last:
-            limit = limits[s:s + 1, :]
         before = near[mine + s:mine + s + 1, :]
         after = far[mine + s:mine + s + 1, :]
         if paired:
@@ -221,10 +211,6 @@
             prim_out[half][s, :, cols] = new
             ext = 2.0 * new - x
             ext_low[:, flat] = ext.astype(BF16)
-            if not last:
-                c = jnp.maximum(c + STEP_CAP * (ext - limit[:, flat]), 0.0)
-                cap_out[half][s, :, cols] = c
-                write_message(paired, near_out, far_out, s, flat, c, new)
         total = lax.dot_general(
             ext_low[...], matrix[...], (((1,), (1,)), ((), ())), preferred_element_type=F32
         )
@@ -241,6 +227,36 @@
             low_sum = total.astype(BF16)
             sent_out[s] = low_sum
             carry_out[s] = total - low_sum.astype(F32)
+
+
+def cap_body(hours_all, paired, sums_count, first, *refs):
+    refs = list(refs)
+    take = lambda count: [refs.pop(0) for _ in range(count)]
+    if first:
+        both = take(2)
+        prim, cap = [src.at[0] for src in both], [src.at[1] for src in both]
+    else:
+        prim, cap = take(2), take(2)
+    fresh = take(2)
+    invest, const = take(2)
+    sums = take(sums_count)
+    cap_out = take(2)
+    invest_out, near_out, far_out, mean_out = take(4)
+    olds, news = new_invest(hours_all, sums, invest, const)
+    limits = 0.0
+    for g, (old, new) in enumerate(zip(olds, news)):
+        invest_out[g] = new
+        limits = limits + (2.0 * new - old)
+    mine, _, width = prim[0].shape
+    for s in range(mine):
+        limit = limits[s:s + 1, :]
+        for half, cols, flat in tiles(width):
+            new = fresh[half][s, :, cols]
+            ext = 2.0 * new - prim[half][s, :, cols]
+            c = jnp.maximum(cap[half][s, :, cols] + STEP_CAP * (ext - limit[:, flat]), 0.0)
+            cap_out[half][s, :, cols] = c
+            write_message(paired, near_out, far_out, s, flat, c, new)
+    mean_out[...] = near_out[:mine, :]
 
 
 def join_body(*refs):
@@ -321,17 +337,17 @@
             out[g, s:s + 1] = mult[g, s:s + 1] + PENALTY * (capacity[g, s:s + 1] - mine)
 
 
-def hour_exchange(near, far, mine, paired):
+def hour_exchange(near, far, mean, paired):
     count = lax.axis_size("hour")
     if not paired:
         near_in = lax.ppermute(near, "hour", [(i, (i + 1) % count) for i in range(count)])
         far_in = lax.ppermute(far, "hour", [((i + 1) % count, i) for i in range(count)])
-        return near_in, far_in, (lax.psum(near[:mine], "hour"),)
+        return near_in, far_in, (lax.psum(mean, "hour"),)
     partners = lambda by: [(i, i ^ by) for i in range(count)]
     far_in = lax.ppermute(far, "hour", partners(3))
     near_in = lax.ppermute(near, "hour", partners(1))
-    across = lax.ppermute(near[:mine], "hour", partners(2))
-    return near_in, far_in, (near, near_in, across, far_in)
+    across = lax.ppermute(mean, "hour", partners(2))
+    return near_in, far_in, (mean, near_in, across, far_in)
 
 
 def shards(
@@ -363,6 +379,7 @@
     three = in_vmem((3, mine, hours, width))
     dual_like = in_vmem((mine, hours, rows))
     message = in_vmem((2 * mine, 2 * width))
+    mean_like = in_vmem((mine, 2 * width))
     invest_like = in_vmem((sections, mine, 2 * width))
     small_like = in_vmem((2 * sections, mine, width))
     inv_half = in_vmem((sections, mine, width))
@@ -388,12 +405,12 @@
         arg_specs=[IN_HBM] * 5,
         scratch=(pltpu.SemaphoreType.DMA((5,)),),
     )
-    matrix, const, invest, near, far = call(
+    matrix, const, invest, near, far, mean = call(
         functools.partial(message_body, paired),
-        (in_vmem((rows, 2 * width), BF16), invest_like, invest_like, message, message),
+        (in_vmem((rows, 2 * width), BF16), invest_like, invest_like, message, message, mean_like),
         (own, twin_in, part, part_in, small, small_in),
     )
-    near_in, far_in, sums = hour_exchange(near, far, mine, paired)
+    near_in, far_in, sums = hour_exchange(near, far, mean, paired)
 
     flops = 4 * mine * hours * rows * 2 * width
     prim = cap = ()
@@ -405,35 +422,40 @@
             args += [dem, sent, carry, received]
         outs = [half_full] * 2
         if last:
-            inv_keep, inv_give = call(
-                functools.partial(invest_body, hours_all, len(sums)),
-                (inv_half,) * 2,
-                (invest, const, *sums),
-            )
-            inv_got = lax.ppermute(inv_give, "reg", twin)
             outs += [in_vmem((mine, hours, rows // 2))] * 2
         else:
-            args += [invest, const, *sums]
-            outs += [half_full] * 2 + [invest_like, message, message]
             outs += [in_vmem((mine, hours, rows), BF16), dual_like]
             if not first:
                 outs += [dual_like]
         got = call(
-            functools.partial(step_body, hours_all, paired, len(sums), first, last),
+            functools.partial(primal_body, paired, first, last),
             outs,
             args,
             scratch=(pltpu.VMEM((hours, 2 * width), BF16),),
             flops=flops,
         )
-        prim = got[:2]
+        fresh = tuple(got[:2])
         if not last:
-            cap = got[2:4]
-            invest, near, far, sent, carry = got[4:9]
+            sent, carry = got[2:4]
             received = lax.ppermute(sent, "reg", other_chip)
             if not first:
-                dual_var = got[9]
-            near_in, far_in, sums = hour_exchange(near, far, mine, paired)
+                dual_var = got[4]
+            old = (own, twin_in) if first else (*prim, *cap)
+            *cap, invest, near, far, mean = call(
+                functools.partial(cap_body, hours_all, paired, len(sums), first),
+                (half_full, half_full, invest_like, message, message, mean_like),
+                (*old, *fresh, invest, const, *sums),
+            )
+            near_in, far_in, sums = hour_exchange(near, far, mean, paired)
+            prim = fresh
             continue
+        prim = fresh
+        inv_keep, inv_give = call(
+            functools.partial(invest_body, hours_all, len(sums)),
+            (inv_half,) * 2,
+            (invest, const, *sums),
+        )
+        inv_got = lax.ppermute(inv_give, "reg", twin)
         base, rows_give = got[2:]
         rows_got = lax.ppermute(rows_give, "reg", other_chip)
         prim_got = lax.ppermute(prim[1], "reg", twin)

time: 107 us -> 132 us (1.23)
  waiting for transfers between devices: 36.8 us -> 64.5 us
  starting transfers between devices: 47.5 us -> 43.1 us
  Pallas kernels: 20 us -> 22.1 us
    ppermute x8, waiting for transfers between devices: 3.54 us -> 16.5 us  [hour_exchange(): far_in = lax.ppermute(far, 'hour', partners(3))]
    ppermute x8, waiting for transfers between devices: 0.02 us -> 8.72 us  [hour_exchange(): near_in = lax.ppermute(near, 'hour', partners(1))]
    ppermute x8, waiting for transfers between devices: 22.7 us -> 28.5 us  [hour_exchange(): across = lax.ppermute(mean, 'hour', partners(2))]
    ppermute x8, starting transfers between devices: 13.8 us -> 8.06 us  [hour_exchange(): across = lax.ppermute(mean, 'hour', partners(2))]
    pallas_call x19 -> x26, Pallas kernels: 20 us -> 22.1 us  [call(): pl.pallas_call(body, out_shape=tuple(outs), in_specs=arg_specs or [IN_VME...]
    ppermute x8, starting transfers between devices: 2.26 us -> 4.15 us  [hour_exchange(): near_in = lax.ppermute(near, 'hour', partners(1))]
  transfers between devices with their start and end apart: 39 -> 39, of which waited for: 13 -> 27; matrix products, arithmetic and copies ran while one was open for 1% -> 1% of each run, Pallas kernels for 4% -> 6%
where the time goes in v4:
time: 132 us
  waiting for transfers between devices  64.5 us (49%)
  starting transfers between devices  43.1 us (33%)
  Pallas kernels  22.1 us (17%)
    ppermute x8, waiting for transfers between devices, hour_exchange(): across = lax.ppermute(mean, 'hour', partners(2))  28.5 us
    pallas_call x26, Pallas kernels, call(): pl.pallas_call(body, out_shape=tuple(outs), in_specs=arg_specs or [IN_VME...  22.1 us
    ppermute x8, starting transfers between devices, hour_exchange(): far_in = lax.ppermute(far, 'hour', partners(3))  19.2 us
    ppermute x8, waiting for transfers between devices, hour_exchange(): far_in = lax.ppermute(far, 'hour', partners(3))  16.5 us
    ppermute x8, waiting for transfers between devices, hour_exchange(): near_in = lax.ppermute(near, 'hour', partners(1))  8.72 us
    ppermute x7, starting transfers between devices, shards(): received = lax.ppermute(sent, 'reg', other_chip)  8.06 us
    ppermute x8, starting transfers between devices, hour_exchange(): across = lax.ppermute(mean, 'hour', partners(2))  8.06 us
    ppermute x1, waiting for transfers between devices, shards(): rows_got = lax.ppermute(rows_give, 'reg', other_chip)  6.17 us
  transfers between devices with their start and end apart: 39, of which 27 were waited for; matrix products, arithmetic and copies ran while one was open for 1% of the time, Pallas kernels for 6%

profile of v4, /device:TPU:0, one launch (start us, length us, event | category | flops | bytes accessed | tf_op | source)
XLA Modules:
  0.0 132.0 jit_solution(18228259139040634053)
XLA Ops:
  7.2 3.0 %collective-permute-start.3 = (f32[4,1024]{1,0:T(4,128)S(1)}, f32[4,1024]{1,0:T(4,128)S(1)}, u32[]{:S(2)}, u32[]{:S(2)}) collective-permute-start(f32[4,1024]{1,0:T(4,128)S(1)} %get-tuple-element.106), channel_id=1, source_target_pairs={{0,4},{4,0},{8,12},{12,8},{1,5},{5,1},{9,13},{13,9},{2,6},{6,2},{1... | collective-permute-start | bytes 49160 | tf_op jit(solution)/shard_map/ppermute | solution.py:348
  10.2 2.5 %collective-permute-start.4 = (f32[4,1024]{1,0:T(4,128)S(1)}, f32[4,1024]{1,0:T(4,128)S(1)}, u32[]{:S(2)}, u32[]{:S(2)}) collective-permute-start(f32[4,1024]{1,0:T(4,128)S(1)} %get-tuple-element.107), channel_id=1, source_target_pairs={{0,12},{4,8},{8,4},{12,0},{1,13},{5,9},{9,5},{13,1},{2,14},{6,10},... | collective-permute-start | bytes 49160 | tf_op jit(solution)/shard_map/ppermute | solution.py:347
  12.7 3.1 %collective-permute-done.4.refs_5_.refs_9_ = f32[4,1024]{1,0:T(4,128)S(1)} collective-permute-done((f32[4,1024]{1,0:T(4,128)S(1)}, f32[4,1024]{1,0:T(4,128)S(1)}, u32[]{:S(2)}, u32[]{:S(2)}) %collective-permute-start.4) | collective-permute-done | bytes 16416 | tf_op jit(solution)/shard_map/ppermute | solution.py:347
  19.4 3.8 %collective-permute-done.5.refs_8_ = f32[2,1024]{1,0:T(2,128)S(1)} collective-permute-done((f32[2,1024]{1,0:T(2,128)S(1)}, f32[2,1024]{1,0:T(2,128)S(1)}, u32[]{:S(2)}, u32[]{:S(2)}) %collective-permute-start.5) | collective-permute-done | bytes 8224 | tf_op jit(solution)/shard_map/ppermute | solution.py:349
  23.9 2.4 %collective-permute-start.7 = (f32[4,1024]{1,0:T(4,128)S(1)}, f32[4,1024]{1,0:T(4,128)S(1)}, u32[]{:S(2)}, u32[]{:S(2)}) collective-permute-start(f32[4,1024]{1,0:T(4,128)S(1)} %get-tuple-element.114), channel_id=1, source_target_pairs={{0,12},{4,8},{8,4},{12,0},{1,13},{5,9},{9,5},{13,1},{2,14},{6,10},... | collective-permute-start | bytes 49160 | tf_op jit(solution)/shard_map/ppermute | solution.py:347
  27.5 1.9 %collective-permute-done.7.refs_5_.refs_11_ = f32[4,1024]{1,0:T(4,128)S(1)} collective-permute-done((f32[4,1024]{1,0:T(4,128)S(1)}, f32[4,1024]{1,0:T(4,128)S(1)}, u32[]{:S(2)}, u32[]{:S(2)}) %collective-permute-start.7) | collective-permute-done | bytes 16416 | tf_op jit(solution)/shard_map/ppermute | solution.py:347
  32.5 3.5 %collective-permute-done.9.refs_10_ = f32[2,1024]{1,0:T(2,128)S(1)} collective-permute-done((f32[2,1024]{1,0:T(2,128)S(1)}, f32[2,1024]{1,0:T(2,128)S(1)}, u32[]{:S(2)}, u32[]{:S(2)}) %collective-permute-start.9) | collective-permute-done | bytes 8224 | tf_op jit(solution)/shard_map/ppermute | solution.py:349
  36.6 2.5 %collective-permute-start.11 = (f32[4,1024]{1,0:T(4,128)S(1)}, f32[4,1024]{1,0:T(4,128)S(1)}, u32[]{:S(2)}, u32[]{:S(2)}) collective-permute-start(f32[4,1024]{1,0:T(4,128)S(1)} %get-tuple-element.126), channel_id=1, source_target_pairs={{0,12},{4,8},{8,4},{12,0},{1,13},{5,9},{9,5},{13,1},{2,14},{6,10},... | collective-permute-start | bytes 49160 | tf_op jit(solution)/shard_map/ppermute | solution.py:347
  40.3 1.9 %collective-permute-done.11.refs_5_.refs_11_ = f32[4,1024]{1,0:T(4,128)S(1)} collective-permute-done((f32[4,1024]{1,0:T(4,128)S(1)}, f32[4,1024]{1,0:T(4,128)S(1)}, u32[]{:S(2)}, u32[]{:S(2)}) %collective-permute-start.11) | collective-permute-done | bytes 16416 | tf_op jit(solution)/shard_map/ppermute | solution.py:347
  46.2 3.4 %collective-permute-done.13.refs_10_ = f32[2,1024]{1,0:T(2,128)S(1)} collective-permute-done((f32[2,1024]{1,0:T(2,128)S(1)}, f32[2,1024]{1,0:T(2,128)S(1)}, u32[]{:S(2)}, u32[]{:S(2)}) %collective-permute-start.13) | collective-permute-done | bytes 8224 | tf_op jit(solution)/shard_map/ppermute | solution.py:349
  50.4 2.4 %collective-permute-start.15 = (f32[4,1024]{1,0:T(4,128)S(1)}, f32[4,1024]{1,0:T(4,128)S(1)}, u32[]{:S(2)}, u32[]{:S(2)}) collective-permute-start(f32[4,1024]{1,0:T(4,128)S(1)} %get-tuple-element.137), channel_id=1, source_target_pairs={{0,12},{4,8},{8,4},{12,0},{1,13},{5,9},{9,5},{13,1},{2,14},{6,10},... | collective-permute-start | bytes 49160 | tf_op jit(solution)/shard_map/ppermute | solution.py:347
  54.0 2.0 %collective-permute-done.15.refs_5_.refs_11_ = f32[4,1024]{1,0:T(4,128)S(1)} collective-permute-done((f32[4,1024]{1,0:T(4,128)S(1)}, f32[4,1024]{1,0:T(4,128)S(1)}, u32[]{:S(2)}, u32[]{:S(2)}) %collective-permute-start.15) | collective-permute-done | bytes 16416 | tf_op jit(solution)/shard_map/ppermute | solution.py:347
  58.9 3.6 %collective-permute-done.17.refs_10_ = f32[2,1024]{1,0:T(2,128)S(1)} collective-permute-done((f32[2,1024]{1,0:T(2,128)S(1)}, f32[2,1024]{1,0:T(2,128)S(1)}, u32[]{:S(2)}, u32[]{:S(2)}) %collective-permute-start.17) | collective-permute-done | bytes 8224 | tf_op jit(solution)/shard_map/ppermute | solution.py:349
  63.2 2.4 %collective-permute-start.19 = (f32[4,1024]{1,0:T(4,128)S(1)}, f32[4,1024]{1,0:T(4,128)S(1)}, u32[]{:S(2)}, u32[]{:S(2)}) collective-permute-start(f32[4,1024]{1,0:T(4,128)S(1)} %get-tuple-element.148), channel_id=1, source_target_pairs={{0,12},{4,8},{8,4},{12,0},{1,13},{5,9},{9,5},{13,1},{2,14},{6,10},... | collective-permute-start | bytes 49160 | tf_op jit(solution)/shard_map/ppermute | solution.py:347
  72.7 3.5 %collective-permute-done.21.refs_10_ = f32[2,1024]{1,0:T(2,128)S(1)} collective-permute-done((f32[2,1024]{1,0:T(2,128)S(1)}, f32[2,1024]{1,0:T(2,128)S(1)}, u32[]{:S(2)}, u32[]{:S(2)}) %collective-permute-start.21) | collective-permute-done | bytes 8224 | tf_op jit(solution)/shard_map/ppermute | solution.py:349
  77.0 2.3 %collective-permute-start.23 = (f32[4,1024]{1,0:T(4,128)S(1)}, f32[4,1024]{1,0:T(4,128)S(1)}, u32[]{:S(2)}, u32[]{:S(2)}) collective-permute-start(f32[4,1024]{1,0:T(4,128)S(1)} %get-tuple-element.159), channel_id=1, source_target_pairs={{0,12},{4,8},{8,4},{12,0},{1,13},{5,9},{9,5},{13,1},{2,14},{6,10},... | collective-permute-start | bytes 49160 | tf_op jit(solution)/shard_map/ppermute | solution.py:347
  80.5 1.9 %collective-permute-done.23.refs_5_.refs_11_ = f32[4,1024]{1,0:T(4,128)S(1)} collective-permute-done((f32[4,1024]{1,0:T(4,128)S(1)}, f32[4,1024]{1,0:T(4,128)S(1)}, u32[]{:S(2)}, u32[]{:S(2)}) %collective-permute-start.23) | collective-permute-done | bytes 16416 | tf_op jit(solution)/shard_map/ppermute | solution.py:347
  85.6 3.6 %collective-permute-done.25.refs_10_ = f32[2,1024]{1,0:T(2,128)S(1)} collective-permute-done((f32[2,1024]{1,0:T(2,128)S(1)}, f32[2,1024]{1,0:T(2,128)S(1)}, u32[]{:S(2)}, u32[]{:S(2)}) %collective-permute-start.25) | collective-permute-done | bytes 8224 | tf_op jit(solution)/shard_map/ppermute | solution.py:349
  89.9 2.4 %collective-permute-start.27 = (f32[4,1024]{1,0:T(4,128)S(1)}, f32[4,1024]{1,0:T(4,128)S(1)}, u32[]{:S(2)}, u32[]{:S(2)}) collective-permute-start(f32[4,1024]{1,0:T(4,128)S(1)} %get-tuple-element.170), channel_id=1, source_target_pairs={{0,12},{4,8},{8,4},{12,0},{1,13},{5,9},{9,5},{13,1},{2,14},{6,10},... | collective-permute-start | bytes 49160 | tf_op jit(solution)/shard_map/ppermute | solution.py:347
  99.3 3.5 %collective-permute-done.29.refs_10_ = f32[2,1024]{1,0:T(2,128)S(1)} collective-permute-done((f32[2,1024]{1,0:T(2,128)S(1)}, f32[2,1024]{1,0:T(2,128)S(1)}, u32[]{:S(2)}, u32[]{:S(2)}) %collective-permute-start.29) | collective-permute-done | bytes 8224 | tf_op jit(solution)/shard_map/ppermute | solution.py:349
  103.6 2.3 %collective-permute-start.31 = (f32[4,1024]{1,0:T(4,128)S(1)}, f32[4,1024]{1,0:T(4,128)S(1)}, u32[]{:S(2)}, u32[]{:S(2)}) collective-permute-start(f32[4,1024]{1,0:T(4,128)S(1)} %get-tuple-element.181), channel_id=1, source_target_pairs={{0,12},{4,8},{8,4},{12,0},{1,13},{5,9},{9,5},{13,1},{2,14},{6,10},... | collective-permute-start | bytes 49160 | tf_op jit(solution)/shard_map/ppermute | solution.py:347
  107.2 1.9 %collective-permute-done.31.refs_5_ = f32[4,1024]{1,0:T(4,128)S(1)} collective-permute-done((f32[4,1024]{1,0:T(4,128)S(1)}, f32[4,1024]{1,0:T(4,128)S(1)}, u32[]{:S(2)}, u32[]{:S(2)}) %collective-permute-start.31) | collective-permute-done | bytes 16416 | tf_op jit(solution)/shard_map/ppermute | solution.py:347
  111.2 6.2 %collective-permute-done.34.got = f32[2,168,128]{2,1,0:T(8,128)S(1)} collective-permute-done((f32[2,168,128]{2,1,0:T(8,128)S(1)}, f32[2,168,128]{2,1,0:T(8,128)S(1)}, u32[]{:S(2)}, u32[]{:S(2)}) %collective-permute-start.34) | collective-permute-done | bytes 172064 | tf_op jit(solution)/shard_map/ppermute | solution.py:460
  119.4 3.5 %collective-permute-done.36.refs_4_ = f32[2,1024]{1,0:T(2,128)S(1)} collective-permute-done((f32[2,1024]{1,0:T(2,128)S(1)}, f32[2,1024]{1,0:T(2,128)S(1)}, u32[]{:S(2)}, u32[]{:S(2)}) %collective-permute-start.36) | collective-permute-done | bytes 8224 | tf_op jit(solution)/shard_map/ppermute | solution.py:349
  (98 shorter events, 61.3 us)
Async XLA Ops:
  2.3 4.7 %collective-permute-start = (f32[3,2,168,512]{3,2,1,0:T(8,128)S(1)}, f32[3,2,168,512]{3,2,1,0:T(8,128)S(1)}, u32[]{:S(2)}, u32[]{:S(2)}) collective-permute-start(f32[3,2,168,512]{3,2,1,0:T(8,128)S(1)} %shard_map.157), channel_id=1, source_target_pairs={{0,1},{1,0},{2,3},{3,2},{4,5},{5,4},{6,7},{7,6},{8,9},{9,8},{10,11... | collective-permute-start | bytes 6193160 | tf_op jit(solution)/shard_map/ppermute | solution.py:396
  7.2 5.5 %collective-permute-start.3 = (f32[4,1024]{1,0:T(4,128)S(1)}, f32[4,1024]{1,0:T(4,128)S(1)}, u32[]{:S(2)}, u32[]{:S(2)}) collective-permute-start(f32[4,1024]{1,0:T(4,128)S(1)} %get-tuple-element.106), channel_id=1, source_target_pairs={{0,4},{4,0},{8,12},{12,8},{1,5},{5,1},{9,13},{13,9},{2,6},{6,2},{1... | collective-permute-start | bytes 49160 | tf_op jit(solution)/shard_map/ppermute | solution.py:348
  10.2 5.5 %collective-permute-start.4 = (f32[4,1024]{1,0:T(4,128)S(1)}, f32[4,1024]{1,0:T(4,128)S(1)}, u32[]{:S(2)}, u32[]{:S(2)}) collective-permute-start(f32[4,1024]{1,0:T(4,128)S(1)} %get-tuple-element.107), channel_id=1, source_target_pairs={{0,12},{4,8},{8,4},{12,0},{1,13},{5,9},{9,5},{13,1},{2,14},{6,10},... | collective-permute-start | bytes 49160 | tf_op jit(solution)/shard_map/ppermute | solution.py:347
  17.0 12.4 %collective-permute-start.8 = (bf16[2,168,256]{2,1,0:T(8,128)(2,1)S(1)}, bf16[2,168,256]{2,1,0:T(8,128)(2,1)S(1)}, u32[]{:S(2)}, u32[]{:S(2)}) collective-permute-start(bf16[2,168,256]{2,1,0:T(8,128)(2,1)S(1)} %get-tuple-element.118.refs_11_), channel_id=1, source_target_pairs={{0,2},{1,3},{2,0},{3,1},{4,6},{5,7},{6,4},{7,5},{8,10},{9,11},{10,... | collective-permute-start | bytes 516104 | tf_op jit(solution)/shard_map/ppermute | solution.py:440
  18.6 4.5 %collective-permute-start.5 = (f32[2,1024]{1,0:T(2,128)S(1)}, f32[2,1024]{1,0:T(2,128)S(1)}, u32[]{:S(2)}, u32[]{:S(2)}) collective-permute-start(f32[2,1024]{1,0:T(2,128)S(1)} %get-tuple-element.112.refs_6_), channel_id=1, source_target_pairs={{0,8},{4,12},{8,0},{12,4},{1,9},{5,13},{9,1},{13,5},{2,10},{6,14},... | collective-permute-start | bytes 24584 | tf_op jit(solution)/shard_map/ppermute | solution.py:349
  23.9 5.5 %collective-permute-start.7 = (f32[4,1024]{1,0:T(4,128)S(1)}, f32[4,1024]{1,0:T(4,128)S(1)}, u32[]{:S(2)}, u32[]{:S(2)}) collective-permute-start(f32[4,1024]{1,0:T(4,128)S(1)} %get-tuple-element.114), channel_id=1, source_target_pairs={{0,12},{4,8},{8,4},{12,0},{1,13},{5,9},{9,5},{13,1},{2,14},{6,10},... | collective-permute-start | bytes 49160 | tf_op jit(solution)/shard_map/ppermute | solution.py:347
  30.8 11.4 %collective-permute-start.12 = (bf16[2,168,256]{2,1,0:T(8,128)(2,1)S(1)}, bf16[2,168,256]{2,1,0:T(8,128)(2,1)S(1)}, u32[]{:S(2)}, u32[]{:S(2)}) collective-permute-start(bf16[2,168,256]{2,1,0:T(8,128)(2,1)S(1)} %get-tuple-element.129.refs_11_), channel_id=1, source_target_pairs={{0,2},{1,3},{2,0},{3,1},{4,6},{5,7},{6,4},{7,5},{8,10},{9,11},{10,... | collective-permute-start | bytes 516104 | tf_op jit(solution)/shard_map/ppermute | solution.py:440
  31.3 4.6 %collective-permute-start.9 = (f32[2,1024]{1,0:T(2,128)S(1)}, f32[2,1024]{1,0:T(2,128)S(1)}, u32[]{:S(2)}, u32[]{:S(2)}) collective-permute-start(f32[2,1024]{1,0:T(2,128)S(1)} %get-tuple-element.124.refs_8_), channel_id=1, source_target_pairs={{0,8},{4,12},{8,0},{12,4},{1,9},{5,13},{9,1},{13,5},{2,10},{6,14},... | collective-permute-start | bytes 24584 | tf_op jit(solution)/shard_map/ppermute | solution.py:349
  36.6 5.6 %collective-permute-start.11 = (f32[4,1024]{1,0:T(4,128)S(1)}, f32[4,1024]{1,0:T(4,128)S(1)}, u32[]{:S(2)}, u32[]{:S(2)}) collective-permute-start(f32[4,1024]{1,0:T(4,128)S(1)} %get-tuple-element.126), channel_id=1, source_target_pairs={{0,12},{4,8},{8,4},{12,0},{1,13},{5,9},{9,5},{13,1},{2,14},{6,10},... | collective-permute-start | bytes 49160 | tf_op jit(solution)/shard_map/ppermute | solution.py:347
  43.5 12.5 %collective-permute-start.16 = (bf16[2,168,256]{2,1,0:T(8,128)(2,1)S(1)}, bf16[2,168,256]{2,1,0:T(8,128)(2,1)S(1)}, u32[]{:S(2)}, u32[]{:S(2)}) collective-permute-start(bf16[2,168,256]{2,1,0:T(8,128)(2,1)S(1)} %get-tuple-element.140.refs_11_), channel_id=1, source_target_pairs={{0,2},{1,3},{2,0},{3,1},{4,6},{5,7},{6,4},{7,5},{8,10},{9,11},{10,... | collective-permute-start | bytes 516104 | tf_op jit(solution)/shard_map/ppermute | solution.py:440
  45.1 4.5 %collective-permute-start.13 = (f32[2,1024]{1,0:T(2,128)S(1)}, f32[2,1024]{1,0:T(2,128)S(1)}, u32[]{:S(2)}, u32[]{:S(2)}) collective-permute-start(f32[2,1024]{1,0:T(2,128)S(1)} %get-tuple-element.135.refs_8_), channel_id=1, source_target_pairs={{0,8},{4,12},{8,0},{12,4},{1,9},{5,13},{9,1},{13,5},{2,10},{6,14},... | collective-permute-start | bytes 24584 | tf_op jit(solution)/shard_map/ppermute | solution.py:349
  50.4 5.6 %collective-permute-start.15 = (f32[4,1024]{1,0:T(4,128)S(1)}, f32[4,1024]{1,0:T(4,128)S(1)}, u32[]{:S(2)}, u32[]{:S(2)}) collective-permute-start(f32[4,1024]{1,0:T(4,128)S(1)} %get-tuple-element.137), channel_id=1, source_target_pairs={{0,12},{4,8},{8,4},{12,0},{1,13},{5,9},{9,5},{13,1},{2,14},{6,10},... | collective-permute-start | bytes 49160 | tf_op jit(solution)/shard_map/ppermute | solution.py:347
  57.4 11.4 %collective-permute-start.20 = (bf16[2,168,256]{2,1,0:T(8,128)(2,1)S(1)}, bf16[2,168,256]{2,1,0:T(8,128)(2,1)S(1)}, u32[]{:S(2)}, u32[]{:S(2)}) collective-permute-start(bf16[2,168,256]{2,1,0:T(8,128)(2,1)S(1)} %get-tuple-element.151.refs_11_), channel_id=1, source_target_pairs={{0,2},{1,3},{2,0},{3,1},{4,6},{5,7},{6,4},{7,5},{8,10},{9,11},{10,... | collective-permute-start | bytes 516104 | tf_op jit(solution)/shard_map/ppermute | solution.py:440
  63.2 5.6 %collective-permute-start.19 = (f32[4,1024]{1,0:T(4,128)S(1)}, f32[4,1024]{1,0:T(4,128)S(1)}, u32[]{:S(2)}, u32[]{:S(2)}) collective-permute-start(f32[4,1024]{1,0:T(4,128)S(1)} %get-tuple-element.148), channel_id=1, source_target_pairs={{0,12},{4,8},{8,4},{12,0},{1,13},{5,9},{9,5},{13,1},{2,14},{6,10},... | collective-permute-start | bytes 49160 | tf_op jit(solution)/shard_map/ppermute | solution.py:347
  70.1 12.4 %collective-permute-start.24 = (bf16[2,168,256]{2,1,0:T(8,128)(2,1)S(1)}, bf16[2,168,256]{2,1,0:T(8,128)(2,1)S(1)}, u32[]{:S(2)}, u32[]{:S(2)}) collective-permute-start(bf16[2,168,256]{2,1,0:T(8,128)(2,1)S(1)} %get-tuple-element.162.refs_11_), channel_id=1, source_target_pairs={{0,2},{1,3},{2,0},{3,1},{4,6},{5,7},{6,4},{7,5},{8,10},{9,11},{10,... | collective-permute-start | bytes 516104 | tf_op jit(solution)/shard_map/ppermute | solution.py:440
  77.0 5.5 %collective-permute-start.23 = (f32[4,1024]{1,0:T(4,128)S(1)}, f32[4,1024]{1,0:T(4,128)S(1)}, u32[]{:S(2)}, u32[]{:S(2)}) collective-permute-start(f32[4,1024]{1,0:T(4,128)S(1)} %get-tuple-element.159), channel_id=1, source_target_pairs={{0,12},{4,8},{8,4},{12,0},{1,13},{5,9},{9,5},{13,1},{2,14},{6,10},... | collective-permute-start | bytes 49160 | tf_op jit(solution)/shard_map/ppermute | solution.py:347
  84.0 11.4 %collective-permute-start.28 = (bf16[2,168,256]{2,1,0:T(8,128)(2,1)S(1)}, bf16[2,168,256]{2,1,0:T(8,128)(2,1)S(1)}, u32[]{:S(2)}, u32[]{:S(2)}) collective-permute-start(bf16[2,168,256]{2,1,0:T(8,128)(2,1)S(1)} %get-tuple-element.173.refs_11_), channel_id=1, source_target_pairs={{0,2},{1,3},{2,0},{3,1},{4,6},{5,7},{6,4},{7,5},{8,10},{9,11},{10,... | collective-permute-start | bytes 516104 | tf_op jit(solution)/shard_map/ppermute | solution.py:440
  89.9 5.5 %collective-permute-start.27 = (f32[4,1024]{1,0:T(4,128)S(1)}, f32[4,1024]{1,0:T(4,128)S(1)}, u32[]{:S(2)}, u32[]{:S(2)}) collective-permute-start(f32[4,1024]{1,0:T(4,128)S(1)} %get-tuple-element.170), channel_id=1, source_target_pairs={{0,12},{4,8},{8,4},{12,0},{1,13},{5,9},{9,5},{13,1},{2,14},{6,10},... | collective-permute-start | bytes 49160 | tf_op jit(solution)/shard_map/ppermute | solution.py:347
  96.8 12.4 %collective-permute-start.32 = (bf16[2,168,256]{2,1,0:T(8,128)(2,1)S(1)}, bf16[2,168,256]{2,1,0:T(8,128)(2,1)S(1)}, u32[]{:S(2)}, u32[]{:S(2)}) collective-permute-start(bf16[2,168,256]{2,1,0:T(8,128)(2,1)S(1)} %get-tuple-element.184.refs_11_), channel_id=1, source_target_pairs={{0,2},{1,3},{2,0},{3,1},{4,6},{5,7},{6,4},{7,5},{8,10},{9,11},{10,... | collective-permute-start | bytes 516104 | tf_op jit(solution)/shard_map/ppermute | solution.py:440
  103.6 5.5 %collective-permute-start.31 = (f32[4,1024]{1,0:T(4,128)S(1)}, f32[4,1024]{1,0:T(4,128)S(1)}, u32[]{:S(2)}, u32[]{:S(2)}) collective-permute-start(f32[4,1024]{1,0:T(4,128)S(1)} %get-tuple-element.181), channel_id=1, source_target_pairs={{0,12},{4,8},{8,4},{12,0},{1,13},{5,9},{9,5},{13,1},{2,14},{6,10},... | collective-permute-start | bytes 49160 | tf_op jit(solution)/shard_map/ppermute | solution.py:347
  110.5 20.2 %collective-permute-start.33 = (f32[2,168,512]{2,1,0:T(8,128)S(1)}, f32[2,168,512]{2,1,0:T(8,128)S(1)}, u32[]{:S(2)}, u32[]{:S(2)}) collective-permute-start(f32[2,168,512]{2,1,0:T(8,128)S(1)} %get-tuple-element.187), channel_id=1, source_target_pairs={{0,1},{1,0},{2,3},{3,2},{4,5},{5,4},{6,7},{7,6},{8,9},{9,8},{10,11... | collective-permute-start | bytes 2064392 | tf_op jit(solution)/shard_map/ppermute | solution.py:461
  110.6 6.8 %collective-permute-start.34 = (f32[2,168,128]{2,1,0:T(8,128)S(1)}, f32[2,168,128]{2,1,0:T(8,128)S(1)}, u32[]{:S(2)}, u32[]{:S(2)}) collective-permute-start(f32[2,168,128]{2,1,0:T(8,128)S(1)} %get-tuple-element.189), channel_id=1, source_target_pairs={{0,2},{1,3},{2,0},{3,1},{4,6},{5,7},{6,4},{7,5},{8,10},{9,11},{10,... | collective-permute-start | bytes 516104 | tf_op jit(solution)/shard_map/ppermute | solution.py:460
  118.2 11.9 %collective-permute-start.35 = (f32[2,64,168]{2,1,0:T(8,128)S(1)}, f32[2,64,168]{2,1,0:T(8,128)S(1)}, u32[]{:S(2)}, u32[]{:S(2)}) collective-permute-start(f32[2,64,168]{2,1,0:T(8,128)S(1)} %get-tuple-element.190), channel_id=1, source_target_pairs={{0,1},{1,0},{2,3},{3,2},{4,5},{5,4},{6,7},{7,6},{8,9},{9,8},{10,11... | collective-permute-start | bytes 258056 | tf_op jit(solution)/shard_map/ppermute | solution.py:491
  118.3 4.6 %collective-permute-start.36 = (f32[2,1024]{1,0:T(2,128)S(1)}, f32[2,1024]{1,0:T(2,128)S(1)}, u32[]{:S(2)}, u32[]{:S(2)}) collective-permute-start(f32[2,1024]{1,0:T(2,128)S(1)} %get-tuple-element.193.refs_2_), channel_id=1, source_target_pairs={{0,8},{4,12},{8,0},{12,4},{1,9},{5,13},{9,1},{13,5},{2,10},{6,14},... | collective-permute-start | bytes 24584 | tf_op jit(solution)/shard_map/ppermute | solution.py:349
  (23 other events, 102.0 us)

commit v5 on v4

--- a/solution.py
+++ b/solution.py
@@ -78,12 +78,12 @@
     run_copies([(src.at[given], out.at[i]) for i, src in enumerate(sources)], sems)
 
 
-def held_body(mine, *refs):
-    *sources, out, dual_out, dem_out, sems = refs
+def load_body(mine, cost, prim, cap, dual, dem, give, own, dual_out, dem_out, sems):
     core = lax.rem(lax.axis_index("reg"), 2)
     held = pl.ds(core * mine, mine)
-    targets = [out.at[0], out.at[1], out.at[2], dual_out, dem_out]
-    run_copies([(src.at[held], dst) for src, dst in zip(sources, targets)], sems)
+    pairs = [(cost.at[pl.ds((1 - core) * mine, mine)], give)]
+    targets = ((prim, own.at[0]), (cap, own.at[1]), (cost, own.at[2]), (dual, dual_out), (dem, dem_out))
+    run_copies(pairs + [(src.at[held], dst) for src, dst in targets], sems)
 
 
 def small_body(cost, mult, cons, capacity, own, give):
@@ -162,10 +162,10 @@
 def primal_body(paired, first, last, *refs):
     refs = list(refs)
     take = lambda count: [refs.pop(0) for _ in range(count)]
-    matrix, own, twin, dual, near, far = take(6)
-    both = (own, twin)
-    cost = [src.at[2] for src in both]
+    matrix, own, twin_cost, dual, near, far = take(6)
+    cost = (own.at[2], twin_cost)
     if first:
+        both = take(2)
         prim, cap = [src.at[0] for src in both], [src.at[1] for src in both]
     else:
         prim, cap = take(2), take(2)
@@ -177,56 +177,59 @@
         sent_out, carry_out = take(2)
         if not first:
             dual_out = take(1)[0]
-    ext_low = take(1)[0]
     mine, hours, width = prim[0].shape
     chip = lax.axis_index("reg") // 2
     place = lax.axis_index("hour")
     has_prev = (place > 0).astype(F32)
     has_next = (place < lax.axis_size("hour") - 1).astype(F32)
-    row = lax.broadcasted_iota(jnp.int32, (hours, COL_TILE), 0)
-    for s in range(mine):
-        multipliers = dual[s]
-        if not first:
-            image = sent[s].astype(F32) + received[s].astype(F32)
-            multipliers = jnp.maximum(multipliers + STEP_DUAL * (dem[s] - image), 0.0)
-            if not last:
-                dual_out[s] = multipliers
-        low = multipliers.astype(BF16)
-        before = near[mine + s:mine + s + 1, :]
-        after = far[mine + s:mine + s + 1, :]
-        if paired:
-            odd = is_odd()
-            before, after = jnp.where(odd, before, after), jnp.where(odd, after, before)
-        before = before * has_prev
-        after = after * has_next
-        for half, cols, flat in tiles(width):
-            pulled = jnp.dot(low, matrix[:, flat], preferred_element_type=F32)
-            x = prim[half][s, :, cols]
-            prev = jnp.where(row == 0, before[:, flat], pltpu.roll(x, 1, 0))
-            follow = jnp.where(row == hours - 1, after[:, flat], pltpu.roll(x, hours - 1, 0))
-            rough = 2.0 * x - prev - follow
-            c = cap[half][s, :, cols]
-            grad = cost[half][s, :, cols] + RAMP_WEIGHT * rough - pulled + c
-            new = jnp.maximum(x - STEP_PRIMAL * grad, 0.0)
-            prim_out[half][s, :, cols] = new
-            ext = 2.0 * new - x
-            ext_low[:, flat] = ext.astype(BF16)
-        total = lax.dot_general(
-            ext_low[...], matrix[...], (((1,), (1,)), ((), ())), preferred_element_type=F32
+    height = mine * hours
+    row = lax.broadcasted_iota(jnp.int32, (height, COL_TILE), 0)
+    flatten = lambda x: x.reshape(height, x.shape[-1])
+    multipliers = flatten(dual[...])
+    if not first:
+        image = sent[...].astype(F32) + received[...].astype(F32)
+        multipliers = jnp.maximum(multipliers + STEP_DUAL * flatten(dem[...] - image), 0.0)
+        if not last:
+            dual_out[...] = multipliers.reshape(dual_out.shape)
+    low = multipliers.astype(BF16)
+    before = near[mine:, :]
+    after = far[mine:, :]
+    if paired:
+        odd = is_odd()
+        before, after = jnp.where(odd, before, after), jnp.where(odd, after, before)
+    before = before * has_prev
+    after = after * has_next
+    total = None if first else flatten(carry[...])
+    for half, cols, flat in tiles(width):
+        pulled = jnp.dot(low, matrix[:, flat], preferred_element_type=F32)
+        x = flatten(prim[half][:, :, cols])
+        prev = pltpu.roll(x, 1, 0)
+        follow = pltpu.roll(x, height - 1, 0)
+        for s in range(mine):
+            prev = jnp.where(row == s * hours, before[s:s + 1, flat], prev)
+            follow = jnp.where(row == (s + 1) * hours - 1, after[s:s + 1, flat], follow)
+        rough = 2.0 * x - prev - follow
+        grad = flatten(cost[half][:, :, cols]) + RAMP_WEIGHT * rough - pulled
+        grad = grad + flatten(cap[half][:, :, cols])
+        new = jnp.maximum(x - STEP_PRIMAL * grad, 0.0)
+        prim_out[half][:, :, cols] = new.reshape(mine, hours, COL_TILE)
+        ext = (2.0 * new - x).astype(BF16)
+        sums = lax.dot_general(
+            ext, matrix[:, flat], (((1,), (1,)), ((), ())), preferred_element_type=F32
         )
-        if not first:
-            total = total + carry[s]
-        if last:
-            rows = total.shape[1] // 2
-            low_chip = chip == 0
-            keep = jnp.where(low_chip, total[:, :rows], total[:, rows:])
-            rows_give[s] = jnp.where(low_chip, total[:, rows:], total[:, :rows])
-            base = multipliers + STEP_DUAL * dem[s]
-            base_out[s] = jnp.where(low_chip, base[:, :rows], base[:, rows:]) - STEP_DUAL * keep
-        else:
-            low_sum = total.astype(BF16)
-            sent_out[s] = low_sum
-            carry_out[s] = total - low_sum.astype(F32)
+        total = sums if total is None else total + sums
+    split = lambda x: x.reshape(mine, hours, x.shape[-1])
+    if last:
+        rows = total.shape[1] // 2
+        low_chip = chip == 0
+        keep = jnp.where(low_chip, total[:, :rows], total[:, rows:])
+        rows_give[...] = split(jnp.where(low_chip, total[:, rows:], total[:, :rows]))
+        base = multipliers + STEP_DUAL * flatten(dem[...])
+        base_out[...] = split(jnp.where(low_chip, base[:, :rows], base[:, rows:]) - STEP_DUAL * keep)
+    else:
+        low_sum = total.astype(BF16)
+        sent_out[...] = split(low_sum.astype(F32)).astype(BF16)
+        carry_out[...] = split(total - low_sum.astype(F32))
 
 
 def cap_body(hours_all, paired, sums_count, first, *refs):
@@ -280,61 +283,72 @@
     )[0]
 
 
-def dual_body(base, got, out, give, kept, sem):
+def dual_body(base, got, keep, give):
     core = lax.rem(lax.axis_index("reg"), 2)
     mine, part = give.shape[:2]
     for s in range(mine):
         new = jnp.maximum(base[s] - STEP_DUAL * got[s], 0.0).T
         low, high = new[:part], new[part:]
-        kept[s] = jnp.where(core == 0, low, high)
+        keep[s] = jnp.where(core == 0, low, high)
         give[s] = jnp.where(core == 0, high, low)
-    run_copies([(kept, out.at[pl.ds(core * mine, mine)])], sem)
-
-
-def rest_body(got, _, out, sem):
-    core = lax.rem(lax.axis_index("reg"), 2)
-    mine = got.shape[0]
-    run_copies([(got, out.at[pl.ds((1 - core) * mine, mine)])], sem)
-
-
-def node_weights(nodes, weights, g, s, n):
-    return jnp.where(nodes[g, s] == n, weights[s], 0.0)
-
-
-def nodes_body(node_count, keep, got, nodes, weights, capacity, packed):
+
+
+def member_body(nodes, weights, hot, weighted):
+    sections, count, scens, lanes = hot.shape
+    one, zero = jnp.ones((1, lanes), F32), jnp.zeros((1, lanes), F32)
+    for g in range(sections):
+        for n in range(count):
+            for s in range(scens):
+                held = jnp.where(nodes[g, s] == n, one, zero)
+                hot[g, n, s:s + 1] = held
+                weighted[g, n, s:s + 1] = held * weights[s]
+
+
+def widen(x, width):
+    return jnp.concatenate([x] * (width // x.shape[-1]), axis=-1)
+
+
+def nodes_body(keep, got, weighted, capacity, packed):
     core = lax.rem(lax.axis_index("reg"), 2)
     sections, mine, width = keep.shape
     for g in range(sections):
-        first = jnp.where(core == 0, keep[g], got[g])
-        second = jnp.where(core == 0, got[g], keep[g])
-        capacity[g, :mine] = first
-        capacity[g, mine:] = second
-        for n in range(node_count):
-            total = jnp.zeros((1, width), F32)
-            mass = jnp.zeros((1, 128), F32)
-            for s in range(2 * mine):
-                weight = node_weights(nodes, weights, g, s, n)
-                row = first[s:s + 1] if s < mine else second[s - mine:s - mine + 1]
-                total = total + weight * row
-                mass = mass + weight
-            packed[g, n:n + 1, :width] = total
-            packed[g, n:n + 1, width:] = mass
-
-
-def multiplier_body(mult, capacity, nodes, *refs):
-    *packs, out = refs
+        capacity[g, :mine] = jnp.where(core == 0, keep[g], got[g])
+        capacity[g, mine:] = jnp.where(core == 0, got[g], keep[g])
+        built = capacity[g]
+        for n in range(packed.shape[1]):
+            weight = weighted[g, n]
+            packed[g, n:n + 1, :width] = jnp.sum(widen(weight, width) * built, axis=0, keepdims=True)
+            packed[g, n:n + 1, width:] = jnp.sum(weight, axis=0, keepdims=True)
+
+
+def finish_body(packs_count, *refs):
+    kept, got, mult, capacity, hot = refs[:5]
+    packs = refs[5:5 + packs_count]
+    dual_out, capacity_out, mult_out, mult_new, sems = refs[5 + packs_count:]
+    core = lax.rem(lax.axis_index("reg"), 2)
     sections, scens, width = capacity.shape
+    mine = scens // 2
+    copies = [
+        pltpu.make_async_copy(kept, dual_out.at[pl.ds(core * mine, mine)], sems.at[0]),
+        pltpu.make_async_copy(got, dual_out.at[pl.ds((1 - core) * mine, mine)], sems.at[1]),
+        pltpu.make_async_copy(capacity, capacity_out, sems.at[2]),
+        pltpu.make_async_copy(mult_new, mult_out, sems.at[3]),
+    ]
+    for copy in copies[:3]:
+        copy.start()
     for g in range(sections):
         packed = packs[0][g]
         for other in packs[1:]:
             packed = packed + other[g]
         mass = packed[:, width:width + 1]
         average = packed[:, :width] / jnp.where(mass > 0.0, mass, 1.0)
-        for s in range(scens):
-            mine = jnp.zeros((1, width), F32)
-            for n in range(packed.shape[0]):
-                mine = mine + jnp.where(nodes[g, s] == n, average[n:n + 1], 0.0)
-            out[g, s:s + 1] = mult[g, s:s + 1] + PENALTY * (capacity[g, s:s + 1] - mine)
+        back = jnp.zeros((scens, width), F32)
+        for n in range(packed.shape[0]):
+            back = back + widen(hot[g, n], width) * average[n:n + 1]
+        mult_new[g] = mult[g] + PENALTY * (capacity[g] - back)
+    copies[3].start()
+    for copy in copies:
+        copy.wait()
 
 
 def hour_exchange(near, far, mean, paired):
@@ -388,36 +402,40 @@
 
     (give,) = call(
         functools.partial(give_body, mine),
-        (three,),
-        (dispatch, cap_dual, cost_rate),
-        arg_specs=[IN_HBM] * 3,
-        scratch=(pltpu.SemaphoreType.DMA((3,)),),
-    )
-    twin_in = lax.ppermute(give, "reg", twin)
+        (in_vmem((2, mine, hours, width)),),
+        (dispatch, cap_dual),
+        arg_specs=[IN_HBM] * 2,
+        scratch=(pltpu.SemaphoreType.DMA((2,)),),
+    )
+    twin_state = lax.ppermute(give, "reg", twin)
     (part,) = call(matrix_body, (in_vmem(tile.shape[1:], BF16),), (tile, tile_mask))
     part_in = lax.ppermute(part, "reg", twin)
     small, small_give = call(small_body, (small_like,) * 2, (invest_cost, mult, cons, caps))
     small_in = lax.ppermute(small_give, "reg", twin)
-    own, dual_var, dem = call(
-        functools.partial(held_body, mine),
-        (three, dual_like, dual_like),
-        (dispatch, cap_dual, cost_rate, dual, demand),
+    cost_give, own, dual_var, dem = call(
+        functools.partial(load_body, mine),
+        (half_full, three, dual_like, dual_like),
+        (cost_rate, dispatch, cap_dual, dual, demand),
         arg_specs=[IN_HBM] * 5,
-        scratch=(pltpu.SemaphoreType.DMA((5,)),),
-    )
+        scratch=(pltpu.SemaphoreType.DMA((6,)),),
+    )
+    twin_cost = lax.ppermute(cost_give, "reg", twin)
     matrix, const, invest, near, far, mean = call(
         functools.partial(message_body, paired),
         (in_vmem((rows, 2 * width), BF16), invest_like, invest_like, message, message, mean_like),
-        (own, twin_in, part, part_in, small, small_in),
+        (own, twin_state, part, part_in, small, small_in),
     )
     near_in, far_in, sums = hour_exchange(near, far, mean, paired)
 
+    scen_count = lax.axis_size("scen")
+    node_count = node_of.shape[1] * scen_count // 2
     flops = 4 * mine * hours * rows * 2 * width
     prim = cap = ()
     sent = carry = received = None
     for step in range(ITERS):
         first, last = step == 0, step + 1 == ITERS
-        args = [matrix, own, twin_in, dual_var, near_in, far_in, *prim, *cap]
+        state = (own, twin_state) if first else (*prim, *cap)
+        args = [matrix, own, twin_cost, dual_var, near_in, far_in, *state]
         if not first:
             args += [dem, sent, carry, received]
         outs = [half_full] * 2
@@ -427,26 +445,27 @@
             outs += [in_vmem((mine, hours, rows), BF16), dual_like]
             if not first:
                 outs += [dual_like]
-        got = call(
-            functools.partial(primal_body, paired, first, last),
-            outs,
-            args,
-            scratch=(pltpu.VMEM((hours, 2 * width), BF16),),
-            flops=flops,
-        )
+        got = call(functools.partial(primal_body, paired, first, last), outs, args, flops=flops)
         fresh = tuple(got[:2])
         if not last:
             sent, carry = got[2:4]
             received = lax.ppermute(sent, "reg", other_chip)
             if not first:
                 dual_var = got[4]
-            old = (own, twin_in) if first else (*prim, *cap)
             *cap, invest, near, far, mean = call(
                 functools.partial(cap_body, hours_all, paired, len(sums), first),
                 (half_full, half_full, invest_like, message, message, mean_like),
-                (*old, *fresh, invest, const, *sums),
+                (*state, *fresh, invest, const, *sums),
             )
             near_in, far_in, sums = hour_exchange(near, far, mean, paired)
+            if step == ITERS // 2:
+                member_like = in_vmem((sections, node_count, nscen, 128))
+                hot, weighted = call(
+                    member_body,
+                    (member_like, member_like),
+                    (node_of, scen_weight),
+                    arg_specs=[IN_SMEM, IN_SMEM],
+                )
             prim = fresh
             continue
         prim = fresh
@@ -459,44 +478,31 @@
         base, rows_give = got[2:]
         rows_got = lax.ppermute(rows_give, "reg", other_chip)
         prim_got = lax.ppermute(prim[1], "reg", twin)
-        scen_count = lax.axis_size("scen")
-        node_count = node_of.shape[1] * scen_count // 2
-        packed_like = in_vmem((sections, node_count, width + 128))
-        by_scen = in_vmem((sections, nscen, width))
-        capacity_out, packed = call(
-            functools.partial(nodes_body, node_count),
-            (by_scen, packed_like),
-            (inv_keep, inv_got, node_of, scen_weight),
-            arg_specs=[IN_VMEM, IN_VMEM, IN_SMEM, IN_SMEM],
+        capacity_all, packed = call(
+            nodes_body,
+            (in_vmem((sections, nscen, width)), in_vmem((sections, node_count, width + 128))),
+            (inv_keep, inv_got, weighted),
         )
         if scen_count == 2:
             packs = (packed, lax.ppermute(packed, "scen", [(0, 1), (1, 0)]))
         else:
             packs = (lax.psum(packed, "scen"),)
-        (multiplier_out,) = call(
-            multiplier_body,
-            (by_scen,),
-            (mult, capacity_out, node_of, *packs),
-            arg_specs=[IN_VMEM, IN_VMEM, IN_SMEM] + [IN_VMEM] * len(packs),
-        )
         dispatch_out = join(prim[0], prim_got)
         own_rows = rows // reg_count
-        dual_half, dual_give = call(
-            dual_body,
-            (shape((nscen, own_rows, hours)), in_vmem((mine, own_rows, hours))),
-            (base, rows_got),
-            out_specs=(IN_HBM, IN_VMEM),
-            scratch=(pltpu.VMEM((mine, own_rows, hours), F32), pltpu.SemaphoreType.DMA((1,))),
+        dual_keep, dual_give = call(
+            dual_body, (in_vmem((mine, own_rows, hours)),) * 2, (base, rows_got)
         )
         dual_got = lax.ppermute(dual_give, "reg", twin)
-        (dual_out,) = call(
-            rest_body,
-            (shape(dual_half.shape),),
-            (dual_got, dual_half),
-            arg_specs=[IN_VMEM, IN_HBM],
-            out_specs=(IN_HBM,),
-            scratch=(pltpu.SemaphoreType.DMA((1,)),),
-            aliases={1: 0},
+        dual_out, capacity_out, multiplier_out = call(
+            functools.partial(finish_body, len(packs)),
+            (
+                pltpu.HBM((nscen, own_rows, hours), F32),
+                pltpu.HBM((sections, nscen, width), F32),
+                pltpu.HBM((sections, nscen, width), F32),
+            ),
+            (dual_keep, dual_got, mult, capacity_all, hot, *packs),
+            out_specs=(IN_HBM,) * 3,
+            scratch=(pltpu.VMEM((sections, nscen, width), F32), pltpu.SemaphoreType.DMA((4,))),
         )
     return (
         dispatch_out,

time: 132 us -> 128 us (0.970)
  Pallas kernels: 22.1 us -> 18.9 us
    pallas_call x26, Pallas kernels: 22.1 us -> 18.9 us  [call(): pl.pallas_call(body, out_shape=tuple(outs), in_specs=arg_specs or [IN_VME...]
  transfers between devices with their start and end apart: 39 -> 40, of which waited for: 27 -> 27; matrix products, arithmetic and copies ran while one was open for 1% -> 0% of each run, Pallas kernels for 6% -> 6%
where the time goes in v5:
time: 128 us; the launch traced here: 127 us
  waiting for transfers between devices  63.8 us (50%)
  starting transfers between devices  43.7 us (34%)
  Pallas kernels  18.9 us (15%)
    ppermute x8, waiting for transfers between devices, hour_exchange(): across = lax.ppermute(mean, 'hour', partners(2))  28.1 us
    ppermute x8, starting transfers between devices, hour_exchange(): far_in = lax.ppermute(far, 'hour', partners(3))  19.5 us
    pallas_call x26, Pallas kernels, call(): pl.pallas_call(body, out_shape=tuple(outs), in_specs=arg_specs or [IN_VME...  18.9 us
    ppermute x8, waiting for transfers between devices, hour_exchange(): far_in = lax.ppermute(far, 'hour', partners(3))  16.4 us
    ppermute x8, starting transfers between devices, hour_exchange(): across = lax.ppermute(mean, 'hour', partners(2))  8.4 us
    ppermute x8, waiting for transfers between devices, hour_exchange(): near_in = lax.ppermute(near, 'hour', partners(1))  8.4 us
    ppermute x7, starting transfers between devices, shards(): received = lax.ppermute(sent, 'reg', other_chip)  8.18 us
    ppermute x1, waiting for transfers between devices, shards(): rows_got = lax.ppermute(rows_give, 'reg', other_chip)  6.23 us
  transfers between devices with their start and end apart: 40, of which 27 were waited for; matrix products, arithmetic and copies ran while one was open for 0% of the time, Pallas kernels for 6%

profile of v5, /device:TPU:0, one launch (start us, length us, event | category | flops | bytes accessed | tf_op | source)
XLA Modules:
  0.0 127.5 jit_solution(14923129341640674254)
XLA Ops:
  2.6 2.0 %shard_map.156 = (f32[2,168,512]{2,1,0:T(8,128)S(1)}, f32[3,2,168,512]{3,2,1,0:T(8,128)S(1)}, f32[2,168,256]{2,1,0:T(8,128)S(1)}, f32[2,168,256]{2,1,0:T(8,128)S(1)}) custom-call(f32[4,168,512]{2,1,0:T(8,128)} %cost.2, f32[4,168,512]{2,1,0:T(8,128)} %refs_0_.1, f32[4,168,512]{2,1,0:T(8,128)} %refs_1_.1, f32[4,168,256]{2,1,0:T(8,128)} %dual.1, f32[4,168,256]{2,1,0:T(8,128)} %dem.1), custom_call_target="tpu_custom_call" | custom-call | bytes 8945664 | tf_op jit(solution)/shard_map/pallas_call | solution.py:38
  7.3 2.8 %collective-permute-start.4 = (f32[4,1024]{1,0:T(4,128)S(1)}, f32[4,1024]{1,0:T(4,128)S(1)}, u32[]{:S(2)}, u32[]{:S(2)}) collective-permute-start(f32[4,1024]{1,0:T(4,128)S(1)} %get-tuple-element.113), channel_id=1, source_target_pairs={{0,4},{4,0},{8,12},{12,8},{1,5},{5,1},{9,13},{13,9},{2,6},{6,2},{1... | collective-permute-start | bytes 49160 | tf_op jit(solution)/shard_map/ppermute | solution.py:362
  10.1 2.5 %collective-permute-start.5 = (f32[4,1024]{1,0:T(4,128)S(1)}, f32[4,1024]{1,0:T(4,128)S(1)}, u32[]{:S(2)}, u32[]{:S(2)}) collective-permute-start(f32[4,1024]{1,0:T(4,128)S(1)} %get-tuple-element.114), channel_id=1, source_target_pairs={{0,12},{4,8},{8,4},{12,0},{1,13},{5,9},{9,5},{13,1},{2,14},{6,10},... | collective-permute-start | bytes 49160 | tf_op jit(solution)/shard_map/ppermute | solution.py:361
  12.6 3.1 %collective-permute-done.5.refs_5_.refs_9_ = f32[4,1024]{1,0:T(4,128)S(1)} collective-permute-done((f32[4,1024]{1,0:T(4,128)S(1)}, f32[4,1024]{1,0:T(4,128)S(1)}, u32[]{:S(2)}, u32[]{:S(2)}) %collective-permute-start.5) | collective-permute-done | bytes 16416 | tf_op jit(solution)/shard_map/ppermute | solution.py:361
  19.1 3.7 %collective-permute-done.6.refs_8_ = f32[2,1024]{1,0:T(2,128)S(1)} collective-permute-done((f32[2,1024]{1,0:T(2,128)S(1)}, f32[2,1024]{1,0:T(2,128)S(1)}, u32[]{:S(2)}, u32[]{:S(2)}) %collective-permute-start.6) | collective-permute-done | bytes 8224 | tf_op jit(solution)/shard_map/ppermute | solution.py:363
  23.5 2.4 %collective-permute-start.8 = (f32[4,1024]{1,0:T(4,128)S(1)}, f32[4,1024]{1,0:T(4,128)S(1)}, u32[]{:S(2)}, u32[]{:S(2)}) collective-permute-start(f32[4,1024]{1,0:T(4,128)S(1)} %get-tuple-element.121), channel_id=1, source_target_pairs={{0,12},{4,8},{8,4},{12,0},{1,13},{5,9},{9,5},{13,1},{2,14},{6,10},... | collective-permute-start | bytes 49160 | tf_op jit(solution)/shard_map/ppermute | solution.py:361
  27.2 1.9 %collective-permute-done.8.refs_5_.refs_11_ = f32[4,1024]{1,0:T(4,128)S(1)} collective-permute-done((f32[4,1024]{1,0:T(4,128)S(1)}, f32[4,1024]{1,0:T(4,128)S(1)}, u32[]{:S(2)}, u32[]{:S(2)}) %collective-permute-start.8) | collective-permute-done | bytes 16416 | tf_op jit(solution)/shard_map/ppermute | solution.py:361
  31.9 3.4 %collective-permute-done.10.refs_10_ = f32[2,1024]{1,0:T(2,128)S(1)} collective-permute-done((f32[2,1024]{1,0:T(2,128)S(1)}, f32[2,1024]{1,0:T(2,128)S(1)}, u32[]{:S(2)}, u32[]{:S(2)}) %collective-permute-start.10) | collective-permute-done | bytes 8224 | tf_op jit(solution)/shard_map/ppermute | solution.py:363
  36.1 2.4 %collective-permute-start.12 = (f32[4,1024]{1,0:T(4,128)S(1)}, f32[4,1024]{1,0:T(4,128)S(1)}, u32[]{:S(2)}, u32[]{:S(2)}) collective-permute-start(f32[4,1024]{1,0:T(4,128)S(1)} %get-tuple-element.133), channel_id=1, source_target_pairs={{0,12},{4,8},{8,4},{12,0},{1,13},{5,9},{9,5},{13,1},{2,14},{6,10},... | collective-permute-start | bytes 49160 | tf_op jit(solution)/shard_map/ppermute | solution.py:361
  39.7 2.0 %collective-permute-done.12.refs_5_.refs_11_ = f32[4,1024]{1,0:T(4,128)S(1)} collective-permute-done((f32[4,1024]{1,0:T(4,128)S(1)}, f32[4,1024]{1,0:T(4,128)S(1)}, u32[]{:S(2)}, u32[]{:S(2)}) %collective-permute-start.12) | collective-permute-done | bytes 16416 | tf_op jit(solution)/shard_map/ppermute | solution.py:361
  45.3 3.5 %collective-permute-done.14.refs_10_ = f32[2,1024]{1,0:T(2,128)S(1)} collective-permute-done((f32[2,1024]{1,0:T(2,128)S(1)}, f32[2,1024]{1,0:T(2,128)S(1)}, u32[]{:S(2)}, u32[]{:S(2)}) %collective-permute-start.14) | collective-permute-done | bytes 8224 | tf_op jit(solution)/shard_map/ppermute | solution.py:363
  49.5 2.4 %collective-permute-start.16 = (f32[4,1024]{1,0:T(4,128)S(1)}, f32[4,1024]{1,0:T(4,128)S(1)}, u32[]{:S(2)}, u32[]{:S(2)}) collective-permute-start(f32[4,1024]{1,0:T(4,128)S(1)} %get-tuple-element.144), channel_id=1, source_target_pairs={{0,12},{4,8},{8,4},{12,0},{1,13},{5,9},{9,5},{13,1},{2,14},{6,10},... | collective-permute-start | bytes 49160 | tf_op jit(solution)/shard_map/ppermute | solution.py:361
  57.9 3.5 %collective-permute-done.18.refs_10_ = f32[2,1024]{1,0:T(2,128)S(1)} collective-permute-done((f32[2,1024]{1,0:T(2,128)S(1)}, f32[2,1024]{1,0:T(2,128)S(1)}, u32[]{:S(2)}, u32[]{:S(2)}) %collective-permute-start.18) | collective-permute-done | bytes 8224 | tf_op jit(solution)/shard_map/ppermute | solution.py:363
  62.0 2.4 %collective-permute-start.20 = (f32[4,1024]{1,0:T(4,128)S(1)}, f32[4,1024]{1,0:T(4,128)S(1)}, u32[]{:S(2)}, u32[]{:S(2)}) collective-permute-start(f32[4,1024]{1,0:T(4,128)S(1)} %get-tuple-element.155), channel_id=1, source_target_pairs={{0,12},{4,8},{8,4},{12,0},{1,13},{5,9},{9,5},{13,1},{2,14},{6,10},... | collective-permute-start | bytes 49160 | tf_op jit(solution)/shard_map/ppermute | solution.py:361
  71.3 3.5 %collective-permute-done.22.refs_10_ = f32[2,1024]{1,0:T(2,128)S(1)} collective-permute-done((f32[2,1024]{1,0:T(2,128)S(1)}, f32[2,1024]{1,0:T(2,128)S(1)}, u32[]{:S(2)}, u32[]{:S(2)}) %collective-permute-start.22) | collective-permute-done | bytes 8224 | tf_op jit(solution)/shard_map/ppermute | solution.py:363
  75.5 2.4 %collective-permute-start.24 = (f32[4,1024]{1,0:T(4,128)S(1)}, f32[4,1024]{1,0:T(4,128)S(1)}, u32[]{:S(2)}, u32[]{:S(2)}) collective-permute-start(f32[4,1024]{1,0:T(4,128)S(1)} %get-tuple-element.166), channel_id=1, source_target_pairs={{0,12},{4,8},{8,4},{12,0},{1,13},{5,9},{9,5},{13,1},{2,14},{6,10},... | collective-permute-start | bytes 49160 | tf_op jit(solution)/shard_map/ppermute | solution.py:361
  83.8 3.5 %collective-permute-done.26.refs_10_ = f32[2,1024]{1,0:T(2,128)S(1)} collective-permute-done((f32[2,1024]{1,0:T(2,128)S(1)}, f32[2,1024]{1,0:T(2,128)S(1)}, u32[]{:S(2)}, u32[]{:S(2)}) %collective-permute-start.26) | collective-permute-done | bytes 8224 | tf_op jit(solution)/shard_map/ppermute | solution.py:363
  88.2 2.4 %collective-permute-start.28 = (f32[4,1024]{1,0:T(4,128)S(1)}, f32[4,1024]{1,0:T(4,128)S(1)}, u32[]{:S(2)}, u32[]{:S(2)}) collective-permute-start(f32[4,1024]{1,0:T(4,128)S(1)} %get-tuple-element.177), channel_id=1, source_target_pairs={{0,12},{4,8},{8,4},{12,0},{1,13},{5,9},{9,5},{13,1},{2,14},{6,10},... | collective-permute-start | bytes 49160 | tf_op jit(solution)/shard_map/ppermute | solution.py:361
  97.5 3.5 %collective-permute-done.30.refs_10_ = f32[2,1024]{1,0:T(2,128)S(1)} collective-permute-done((f32[2,1024]{1,0:T(2,128)S(1)}, f32[2,1024]{1,0:T(2,128)S(1)}, u32[]{:S(2)}, u32[]{:S(2)}) %collective-permute-start.30) | collective-permute-done | bytes 8224 | tf_op jit(solution)/shard_map/ppermute | solution.py:363
  101.8 2.4 %collective-permute-start.32 = (f32[4,1024]{1,0:T(4,128)S(1)}, f32[4,1024]{1,0:T(4,128)S(1)}, u32[]{:S(2)}, u32[]{:S(2)}) collective-permute-start(f32[4,1024]{1,0:T(4,128)S(1)} %get-tuple-element.188), channel_id=1, source_target_pairs={{0,12},{4,8},{8,4},{12,0},{1,13},{5,9},{9,5},{13,1},{2,14},{6,10},... | collective-permute-start | bytes 49160 | tf_op jit(solution)/shard_map/ppermute | solution.py:361
  105.4 1.9 %collective-permute-done.32.refs_5_ = f32[4,1024]{1,0:T(4,128)S(1)} collective-permute-done((f32[4,1024]{1,0:T(4,128)S(1)}, f32[4,1024]{1,0:T(4,128)S(1)}, u32[]{:S(2)}, u32[]{:S(2)}) %collective-permute-start.32) | collective-permute-done | bytes 16416 | tf_op jit(solution)/shard_map/ppermute | solution.py:361
  109.0 6.2 %collective-permute-done.35.got = f32[2,168,128]{2,1,0:T(8,128)S(1)} collective-permute-done((f32[2,168,128]{2,1,0:T(8,128)S(1)}, f32[2,168,128]{2,1,0:T(8,128)S(1)}, u32[]{:S(2)}, u32[]{:S(2)}) %collective-permute-start.35) | collective-permute-done | bytes 172064 | tf_op jit(solution)/shard_map/ppermute | solution.py:479
  116.7 3.4 %collective-permute-done.37.refs_4_ = f32[2,1024]{1,0:T(2,128)S(1)} collective-permute-done((f32[2,1024]{1,0:T(2,128)S(1)}, f32[2,1024]{1,0:T(2,128)S(1)}, u32[]{:S(2)}, u32[]{:S(2)}) %collective-permute-start.37) | collective-permute-done | bytes 8224 | tf_op jit(solution)/shard_map/ppermute | solution.py:363
  123.0 2.4 %collective-permute-done.39.refs_6_ = f32[3,4,640]{2,1,0:T(4,128)S(1)} collective-permute-done((f32[3,4,640]{2,1,0:T(4,128)S(1)}, f32[3,4,640]{2,1,0:T(4,128)S(1)}, u32[]{:S(2)}, u32[]{:S(2)}) %collective-permute-start.39) | collective-permute-done | bytes 30752 | tf_op jit(solution)/shard_map/ppermute | solution.py:487
  (98 shorter events, 56.6 us)
Async XLA Ops:
  2.0 5.2 %collective-permute-start = (f32[2,2,168,512]{3,2,1,0:T(8,128)S(1)}, f32[2,2,168,512]{3,2,1,0:T(8,128)S(1)}, u32[]{:S(2)}, u32[]{:S(2)}) collective-permute-start(f32[2,2,168,512]{3,2,1,0:T(8,128)S(1)} %shard_map.157), channel_id=1, source_target_pairs={{0,1},{1,0},{2,3},{3,2},{4,5},{5,4},{6,7},{7,6},{8,9},{9,8},{10,11... | collective-permute-start | bytes 4128776 | tf_op jit(solution)/shard_map/ppermute | solution.py:410
  4.6 8.0 %collective-permute-start.3 = (f32[2,168,512]{2,1,0:T(8,128)S(1)}, f32[2,168,512]{2,1,0:T(8,128)S(1)}, u32[]{:S(2)}, u32[]{:S(2)}) collective-permute-start(f32[2,168,512]{2,1,0:T(8,128)S(1)} %get-tuple-element.111), channel_id=1, source_target_pairs={{0,1},{1,0},{2,3},{3,2},{4,5},{5,4},{6,7},{7,6},{8,9},{9,8},{10,11... | collective-permute-start | bytes 2064392 | tf_op jit(solution)/shard_map/ppermute | solution.py:422
  7.3 5.2 %collective-permute-start.4 = (f32[4,1024]{1,0:T(4,128)S(1)}, f32[4,1024]{1,0:T(4,128)S(1)}, u32[]{:S(2)}, u32[]{:S(2)}) collective-permute-start(f32[4,1024]{1,0:T(4,128)S(1)} %get-tuple-element.113), channel_id=1, source_target_pairs={{0,4},{4,0},{8,12},{12,8},{1,5},{5,1},{9,13},{13,9},{2,6},{6,2},{1... | collective-permute-start | bytes 49160 | tf_op jit(solution)/shard_map/ppermute | solution.py:362
  10.1 5.5 %collective-permute-start.5 = (f32[4,1024]{1,0:T(4,128)S(1)}, f32[4,1024]{1,0:T(4,128)S(1)}, u32[]{:S(2)}, u32[]{:S(2)}) collective-permute-start(f32[4,1024]{1,0:T(4,128)S(1)} %get-tuple-element.114), channel_id=1, source_target_pairs={{0,12},{4,8},{8,4},{12,0},{1,13},{5,9},{9,5},{13,1},{2,14},{6,10},... | collective-permute-start | bytes 49160 | tf_op jit(solution)/shard_map/ppermute | solution.py:361
  16.7 12.4 %collective-permute-start.9 = (bf16[2,168,256]{2,1,0:T(8,128)(2,1)S(1)}, bf16[2,168,256]{2,1,0:T(8,128)(2,1)S(1)}, u32[]{:S(2)}, u32[]{:S(2)}) collective-permute-start(bf16[2,168,256]{2,1,0:T(8,128)(2,1)S(1)} %get-tuple-element.125.refs_11_), channel_id=1, source_target_pairs={{0,2},{1,3},{2,0},{3,1},{4,6},{5,7},{6,4},{7,5},{8,10},{9,11},{10,... | collective-permute-start | bytes 516104 | tf_op jit(solution)/shard_map/ppermute | solution.py:452
  18.3 4.5 %collective-permute-start.6 = (f32[2,1024]{1,0:T(2,128)S(1)}, f32[2,1024]{1,0:T(2,128)S(1)}, u32[]{:S(2)}, u32[]{:S(2)}) collective-permute-start(f32[2,1024]{1,0:T(2,128)S(1)} %get-tuple-element.119.refs_6_), channel_id=1, source_target_pairs={{0,8},{4,12},{8,0},{12,4},{1,9},{5,13},{9,1},{13,5},{2,10},{6,14},... | collective-permute-start | bytes 24584 | tf_op jit(solution)/shard_map/ppermute | solution.py:363
  23.5 5.5 %collective-permute-start.8 = (f32[4,1024]{1,0:T(4,128)S(1)}, f32[4,1024]{1,0:T(4,128)S(1)}, u32[]{:S(2)}, u32[]{:S(2)}) collective-permute-start(f32[4,1024]{1,0:T(4,128)S(1)} %get-tuple-element.121), channel_id=1, source_target_pairs={{0,12},{4,8},{8,4},{12,0},{1,13},{5,9},{9,5},{13,1},{2,14},{6,10},... | collective-permute-start | bytes 49160 | tf_op jit(solution)/shard_map/ppermute | solution.py:361
  30.2 11.4 %collective-permute-start.13 = (bf16[2,168,256]{2,1,0:T(8,128)(2,1)S(1)}, bf16[2,168,256]{2,1,0:T(8,128)(2,1)S(1)}, u32[]{:S(2)}, u32[]{:S(2)}) collective-permute-start(bf16[2,168,256]{2,1,0:T(8,128)(2,1)S(1)} %get-tuple-element.136.refs_11_), channel_id=1, source_target_pairs={{0,2},{1,3},{2,0},{3,1},{4,6},{5,7},{6,4},{7,5},{8,10},{9,11},{10,... | collective-permute-start | bytes 516104 | tf_op jit(solution)/shard_map/ppermute | solution.py:452
  30.8 4.5 %collective-permute-start.10 = (f32[2,1024]{1,0:T(2,128)S(1)}, f32[2,1024]{1,0:T(2,128)S(1)}, u32[]{:S(2)}, u32[]{:S(2)}) collective-permute-start(f32[2,1024]{1,0:T(2,128)S(1)} %get-tuple-element.131.refs_8_), channel_id=1, source_target_pairs={{0,8},{4,12},{8,0},{12,4},{1,9},{5,13},{9,1},{13,5},{2,10},{6,14},... | collective-permute-start | bytes 24584 | tf_op jit(solution)/shard_map/ppermute | solution.py:363
  36.1 5.5 %collective-permute-start.12 = (f32[4,1024]{1,0:T(4,128)S(1)}, f32[4,1024]{1,0:T(4,128)S(1)}, u32[]{:S(2)}, u32[]{:S(2)}) collective-permute-start(f32[4,1024]{1,0:T(4,128)S(1)} %get-tuple-element.133), channel_id=1, source_target_pairs={{0,12},{4,8},{8,4},{12,0},{1,13},{5,9},{9,5},{13,1},{2,14},{6,10},... | collective-permute-start | bytes 49160 | tf_op jit(solution)/shard_map/ppermute | solution.py:361
  42.7 12.4 %collective-permute-start.17 = (bf16[2,168,256]{2,1,0:T(8,128)(2,1)S(1)}, bf16[2,168,256]{2,1,0:T(8,128)(2,1)S(1)}, u32[]{:S(2)}, u32[]{:S(2)}) collective-permute-start(bf16[2,168,256]{2,1,0:T(8,128)(2,1)S(1)} %get-tuple-element.147.refs_11_), channel_id=1, source_target_pairs={{0,2},{1,3},{2,0},{3,1},{4,6},{5,7},{6,4},{7,5},{8,10},{9,11},{10,... | collective-permute-start | bytes 516104 | tf_op jit(solution)/shard_map/ppermute | solution.py:452
  49.5 5.6 %collective-permute-start.16 = (f32[4,1024]{1,0:T(4,128)S(1)}, f32[4,1024]{1,0:T(4,128)S(1)}, u32[]{:S(2)}, u32[]{:S(2)}) collective-permute-start(f32[4,1024]{1,0:T(4,128)S(1)} %get-tuple-element.144), channel_id=1, source_target_pairs={{0,12},{4,8},{8,4},{12,0},{1,13},{5,9},{9,5},{13,1},{2,14},{6,10},... | collective-permute-start | bytes 49160 | tf_op jit(solution)/shard_map/ppermute | solution.py:361
  56.2 11.4 %collective-permute-start.21 = (bf16[2,168,256]{2,1,0:T(8,128)(2,1)S(1)}, bf16[2,168,256]{2,1,0:T(8,128)(2,1)S(1)}, u32[]{:S(2)}, u32[]{:S(2)}) collective-permute-start(bf16[2,168,256]{2,1,0:T(8,128)(2,1)S(1)} %get-tuple-element.158.refs_11_), channel_id=1, source_target_pairs={{0,2},{1,3},{2,0},{3,1},{4,6},{5,7},{6,4},{7,5},{8,10},{9,11},{10,... | collective-permute-start | bytes 516104 | tf_op jit(solution)/shard_map/ppermute | solution.py:452
  62.0 5.6 %collective-permute-start.20 = (f32[4,1024]{1,0:T(4,128)S(1)}, f32[4,1024]{1,0:T(4,128)S(1)}, u32[]{:S(2)}, u32[]{:S(2)}) collective-permute-start(f32[4,1024]{1,0:T(4,128)S(1)} %get-tuple-element.155), channel_id=1, source_target_pairs={{0,12},{4,8},{8,4},{12,0},{1,13},{5,9},{9,5},{13,1},{2,14},{6,10},... | collective-permute-start | bytes 49160 | tf_op jit(solution)/shard_map/ppermute | solution.py:361
  68.7 12.4 %collective-permute-start.25 = (bf16[2,168,256]{2,1,0:T(8,128)(2,1)S(1)}, bf16[2,168,256]{2,1,0:T(8,128)(2,1)S(1)}, u32[]{:S(2)}, u32[]{:S(2)}) collective-permute-start(bf16[2,168,256]{2,1,0:T(8,128)(2,1)S(1)} %get-tuple-element.169.refs_11_), channel_id=1, source_target_pairs={{0,2},{1,3},{2,0},{3,1},{4,6},{5,7},{6,4},{7,5},{8,10},{9,11},{10,... | collective-permute-start | bytes 516104 | tf_op jit(solution)/shard_map/ppermute | solution.py:452
  75.5 5.5 %collective-permute-start.24 = (f32[4,1024]{1,0:T(4,128)S(1)}, f32[4,1024]{1,0:T(4,128)S(1)}, u32[]{:S(2)}, u32[]{:S(2)}) collective-permute-start(f32[4,1024]{1,0:T(4,128)S(1)} %get-tuple-element.166), channel_id=1, source_target_pairs={{0,12},{4,8},{8,4},{12,0},{1,13},{5,9},{9,5},{13,1},{2,14},{6,10},... | collective-permute-start | bytes 49160 | tf_op jit(solution)/shard_map/ppermute | solution.py:361
  82.2 11.6 %collective-permute-start.29 = (bf16[2,168,256]{2,1,0:T(8,128)(2,1)S(1)}, bf16[2,168,256]{2,1,0:T(8,128)(2,1)S(1)}, u32[]{:S(2)}, u32[]{:S(2)}) collective-permute-start(bf16[2,168,256]{2,1,0:T(8,128)(2,1)S(1)} %get-tuple-element.180.refs_11_), channel_id=1, source_target_pairs={{0,2},{1,3},{2,0},{3,1},{4,6},{5,7},{6,4},{7,5},{8,10},{9,11},{10,... | collective-permute-start | bytes 516104 | tf_op jit(solution)/shard_map/ppermute | solution.py:452
  88.2 5.5 %collective-permute-start.28 = (f32[4,1024]{1,0:T(4,128)S(1)}, f32[4,1024]{1,0:T(4,128)S(1)}, u32[]{:S(2)}, u32[]{:S(2)}) collective-permute-start(f32[4,1024]{1,0:T(4,128)S(1)} %get-tuple-element.177), channel_id=1, source_target_pairs={{0,12},{4,8},{8,4},{12,0},{1,13},{5,9},{9,5},{13,1},{2,14},{6,10},... | collective-permute-start | bytes 49160 | tf_op jit(solution)/shard_map/ppermute | solution.py:361
  94.8 12.4 %collective-permute-start.33 = (bf16[2,168,256]{2,1,0:T(8,128)(2,1)S(1)}, bf16[2,168,256]{2,1,0:T(8,128)(2,1)S(1)}, u32[]{:S(2)}, u32[]{:S(2)}) collective-permute-start(bf16[2,168,256]{2,1,0:T(8,128)(2,1)S(1)} %get-tuple-element.191.refs_11_), channel_id=1, source_target_pairs={{0,2},{1,3},{2,0},{3,1},{4,6},{5,7},{6,4},{7,5},{8,10},{9,11},{10,... | collective-permute-start | bytes 516104 | tf_op jit(solution)/shard_map/ppermute | solution.py:452
  101.8 5.5 %collective-permute-start.32 = (f32[4,1024]{1,0:T(4,128)S(1)}, f32[4,1024]{1,0:T(4,128)S(1)}, u32[]{:S(2)}, u32[]{:S(2)}) collective-permute-start(f32[4,1024]{1,0:T(4,128)S(1)} %get-tuple-element.188), channel_id=1, source_target_pairs={{0,12},{4,8},{8,4},{12,0},{1,13},{5,9},{9,5},{13,1},{2,14},{6,10},... | collective-permute-start | bytes 49160 | tf_op jit(solution)/shard_map/ppermute | solution.py:361
  108.4 17.8 %collective-permute-start.34 = (f32[2,168,512]{2,1,0:T(8,128)S(1)}, f32[2,168,512]{2,1,0:T(8,128)S(1)}, u32[]{:S(2)}, u32[]{:S(2)}) collective-permute-start(f32[2,168,512]{2,1,0:T(8,128)S(1)} %get-tuple-element.194), channel_id=1, source_target_pairs={{0,1},{1,0},{2,3},{3,2},{4,5},{5,4},{6,7},{7,6},{8,9},{9,8},{10,11... | collective-permute-start | bytes 2064392 | tf_op jit(solution)/shard_map/ppermute | solution.py:480
  108.5 6.8 %collective-permute-start.35 = (f32[2,168,128]{2,1,0:T(8,128)S(1)}, f32[2,168,128]{2,1,0:T(8,128)S(1)}, u32[]{:S(2)}, u32[]{:S(2)}) collective-permute-start(f32[2,168,128]{2,1,0:T(8,128)S(1)} %get-tuple-element.196), channel_id=1, source_target_pairs={{0,2},{1,3},{2,0},{3,1},{4,6},{5,7},{6,4},{7,5},{8,10},{9,11},{10,... | collective-permute-start | bytes 516104 | tf_op jit(solution)/shard_map/ppermute | solution.py:479
  115.4 10.0 %collective-permute-start.36 = (f32[2,64,168]{2,1,0:T(8,128)S(1)}, f32[2,64,168]{2,1,0:T(8,128)S(1)}, u32[]{:S(2)}, u32[]{:S(2)}) collective-permute-start(f32[2,64,168]{2,1,0:T(8,128)S(1)} %get-tuple-element.198), channel_id=1, source_target_pairs={{0,1},{1,0},{2,3},{3,2},{4,5},{5,4},{6,7},{7,6},{8,9},{9,8},{10,11... | collective-permute-start | bytes 258056 | tf_op jit(solution)/shard_map/ppermute | solution.py:495
  115.5 4.6 %collective-permute-start.37 = (f32[2,1024]{1,0:T(2,128)S(1)}, f32[2,1024]{1,0:T(2,128)S(1)}, u32[]{:S(2)}, u32[]{:S(2)}) collective-permute-start(f32[2,1024]{1,0:T(2,128)S(1)} %get-tuple-element.200.refs_2_), channel_id=1, source_target_pairs={{0,8},{4,12},{8,0},{12,4},{1,9},{5,13},{9,1},{13,5},{2,10},{6,14},... | collective-permute-start | bytes 24584 | tf_op jit(solution)/shard_map/ppermute | solution.py:363
  (24 other events, 103.3 us)

commit v6 on v5

--- a/solution.py
+++ b/solution.py
@@ -102,11 +102,13 @@
 
 
 def message_body(paired, own, twin, part, part_in, small, small_in, *outs):
-    matrix, const, invest, near, far, mean = outs
+    matrix, turned, const, invest, near, far, mean = outs
     _, mine, _, width = own.shape
     sections = invest.shape[0]
-    matrix[:, :width] = part[...]
-    matrix[:, width:] = part_in[...]
+    for half, src in enumerate((part, part_in)):
+        cols = slice(half * width, (half + 1) * width)
+        matrix[:, cols] = src[...]
+        turned[cols, :] = src[...].T
     for src, cols in ((small, slice(0, width)), (small_in, slice(width, 2 * width))):
         const[:, :, cols] = src[:sections]
         invest[:, :, cols] = src[sections:]
@@ -139,6 +141,10 @@
 def new_invest(hours_all, sums, invest, const):
     mine = invest.shape[1]
     parts = [part[:mine, :] for part in sums]
+    if len(parts) > 1:
+        place = lax.axis_index("hour")
+        at_end = jnp.logical_or(place == 0, place == lax.axis_size("hour") - 1)
+        parts[3:] = [jnp.where(at_end, parts[4], parts[3])]
     while len(parts) > 1:
         parts = [u + v for u, v in zip(parts[0::2], parts[1::2])]
     mean = parts[0] / hours_all
@@ -159,10 +165,22 @@
         give[g] = new[:, width:]
 
 
+def patch(x, rows, at, hours):
+    start = at // 8 * 8
+    row = lax.broadcasted_iota(jnp.int32, (8, x.shape[1]), 0)
+    pieces = []
+    for s in range(rows.shape[0]):
+        base = s * hours
+        pieces.append(x[base:base + start])
+        pieces.append(jnp.where(row == at - start, rows[s:s + 1], x[base + start:base + start + 8]))
+        pieces.append(x[base + start + 8:base + hours])
+    return jnp.concatenate([p for p in pieces if p.shape[0]], axis=0)
+
+
 def primal_body(paired, first, last, *refs):
     refs = list(refs)
     take = lambda count: [refs.pop(0) for _ in range(count)]
-    matrix, own, twin_cost, dual, near, far = take(6)
+    matrix, turned, own, twin_cost, dual, near, far = take(7)
     cost = (own.at[2], twin_cost)
     if first:
         both = take(2)
@@ -183,7 +201,6 @@
     has_prev = (place > 0).astype(F32)
     has_next = (place < lax.axis_size("hour") - 1).astype(F32)
     height = mine * hours
-    row = lax.broadcasted_iota(jnp.int32, (height, COL_TILE), 0)
     flatten = lambda x: x.reshape(height, x.shape[-1])
     multipliers = flatten(dual[...])
     if not first:
@@ -205,18 +222,15 @@
         x = flatten(prim[half][:, :, cols])
         prev = pltpu.roll(x, 1, 0)
         follow = pltpu.roll(x, height - 1, 0)
-        for s in range(mine):
-            prev = jnp.where(row == s * hours, before[s:s + 1, flat], prev)
-            follow = jnp.where(row == (s + 1) * hours - 1, after[s:s + 1, flat], follow)
+        prev = patch(prev, before[:, flat], 0, hours)
+        follow = patch(follow, after[:, flat], hours - 1, hours)
         rough = 2.0 * x - prev - follow
         grad = flatten(cost[half][:, :, cols]) + RAMP_WEIGHT * rough - pulled
         grad = grad + flatten(cap[half][:, :, cols])
         new = jnp.maximum(x - STEP_PRIMAL * grad, 0.0)
         prim_out[half][:, :, cols] = new.reshape(mine, hours, COL_TILE)
         ext = (2.0 * new - x).astype(BF16)
-        sums = lax.dot_general(
-            ext, matrix[:, flat], (((1,), (1,)), ((), ())), preferred_element_type=F32
-        )
+        sums = jnp.dot(ext, turned[flat, :], preferred_element_type=F32)
         total = sums if total is None else total + sums
     split = lambda x: x.reshape(mine, hours, x.shape[-1])
     if last:
@@ -357,11 +371,19 @@
         near_in = lax.ppermute(near, "hour", [(i, (i + 1) % count) for i in range(count)])
         far_in = lax.ppermute(far, "hour", [((i + 1) % count, i) for i in range(count)])
         return near_in, far_in, (lax.psum(mean, "hour"),)
+    reg_count = lax.axis_size("reg")
     partners = lambda by: [(i, i ^ by) for i in range(count)]
-    far_in = lax.ppermute(far, "hour", partners(3))
+    place = lambda z, r: z * reg_count + r
+    mirror = lambda places: [
+        (place(z, r), place(count - 1 - z, r) if z in places else place(z, r ^ 1))
+        for z in range(count)
+        for r in range(reg_count)
+    ]
     near_in = lax.ppermute(near, "hour", partners(1))
+    far_in = lax.ppermute(mean, ("hour", "reg"), mirror((0, count - 1)))
+    mid_in = lax.ppermute(far, ("hour", "reg"), mirror(range(1, count - 1)))
     across = lax.ppermute(mean, "hour", partners(2))
-    return near_in, far_in, (mean, near_in, across, far_in)
+    return near_in, mid_in, (mean, near_in, across, mid_in, far_in)
 
 
 def shards(
@@ -420,9 +442,9 @@
         scratch=(pltpu.SemaphoreType.DMA((6,)),),
     )
     twin_cost = lax.ppermute(cost_give, "reg", twin)
-    matrix, const, invest, near, far, mean = call(
+    matrix, turned, const, invest, near, far, mean = call(
         functools.partial(message_body, paired),
-        (in_vmem((rows, 2 * width), BF16), invest_like, invest_like, message, message, mean_like),
+        (in_vmem((rows, 2 * width), BF16), in_vmem((2 * width, rows), BF16), invest_like, invest_like, message, message, mean_like),
         (own, twin_state, part, part_in, small, small_in),
     )
     near_in, far_in, sums = hour_exchange(near, far, mean, paired)
@@ -435,7 +457,7 @@
     for step in range(ITERS):
         first, last = step == 0, step + 1 == ITERS
         state = (own, twin_state) if first else (*prim, *cap)
-        args = [matrix, own, twin_cost, dual_var, near_in, far_in, *state]
+        args = [matrix, turned, own, twin_cost, dual_var, near_in, far_in, *state]
         if not first:
             args += [dem, sent, carry, received]
         outs = [half_full] * 2

time: 128 us -> 138 us (1.078)
  starting transfers between devices: 43.7 us -> 52 us
  waiting for transfers between devices: 63.8 us -> 66.4 us
    ppermute x8, waiting for transfers between devices: 28.1 us -> 3.58 us  [hour_exchange(): across = lax.ppermute(mean, 'hour', partners(2))]
    ppermute x8, waiting for transfers between devices: 8.4 us -> 27.1 us  [hour_exchange(): near_in = lax.ppermute(near, 'hour', partners(1))]
    ppermute x8, starting transfers between devices: 8.4 us -> 20.5 us  [hour_exchange(): across = lax.ppermute(mean, 'hour', partners(2))]
    ppermute x8 -> x16, waiting for transfers between devices: 16.4 us -> 24.8 us  [the longest x8 24.8 us: hour_exchange(): far_in = lax.ppermute(mean, ('hour', 'reg'), mirror((0, count - 1)))]
    ppermute x8 -> x16, starting transfers between devices: 19.5 us -> 15.9 us  [the longest x8 15.3 us: hour_exchange(): far_in = lax.ppermute(mean, ('hour', 'reg'), mirror((0, count - 1)))]
  transfers between devices with their start and end apart: 40 -> 48, of which waited for: 27 -> 28; matrix products, arithmetic and copies ran while one was open for 0% -> 0% of each run, Pallas kernels for 6% -> 6%
where the time goes in v6:
time: 138 us
  waiting for transfers between devices  66.4 us (48%)
  starting transfers between devices  52 us (38%)
  Pallas kernels  18.7 us (14%)
    ppermute x8, waiting for transfers between devices, hour_exchange(): near_in = lax.ppermute(near, 'hour', partners(1))  27.1 us
    ppermute x8, waiting for transfers between devices, hour_exchange(): far_in = lax.ppermute(mean, ('hour', 'reg'), mirror((0, count - 1)))  24.8 us
    ppermute x8, starting transfers between devices, hour_exchange(): across = lax.ppermute(mean, 'hour', partners(2))  20.5 us
    pallas_call x26, Pallas kernels, call(): pl.pallas_call(body, out_shape=tuple(outs), in_specs=arg_specs or [IN_VME...  18.7 us
    ppermute x8, starting transfers between devices, hour_exchange(): far_in = lax.ppermute(mean, ('hour', 'reg'), mirror((0, count - 1)))  15.3 us
    ppermute x7, starting transfers between devices, shards(): received = lax.ppermute(sent, 'reg', other_chip)  8.68 us
    ppermute x1, waiting for transfers between devices, shards(): rows_got = lax.ppermute(rows_give, 'reg', other_chip)  6.21 us
    ppermute x8, waiting for transfers between devices, hour_exchange(): across = lax.ppermute(mean, 'hour', partners(2))  3.58 us
  transfers between devices with their start and end apart: 48, of which 28 were waited for; matrix products, arithmetic and copies ran while one was open for 0% of the time, Pallas kernels for 6%

profile of v6, /device:TPU:0, one launch (start us, length us, event | category | flops | bytes accessed | tf_op | source)
XLA Modules:
  0.0 138.3 jit_solution(3733953340371324999)
XLA Ops:
  7.4 2.8 %collective-permute-start.4 = (f32[4,1024]{1,0:T(4,128)S(1)}, f32[4,1024]{1,0:T(4,128)S(1)}, u32[]{:S(2)}, u32[]{:S(2)}) collective-permute-start(f32[4,1024]{1,0:T(4,128)S(1)} %get-tuple-element.115), channel_id=1, source_target_pairs={{0,4},{4,0},{8,12},{12,8},{1,5},{5,1},{9,13},{13,9},{2,6},{6,2},{1... | collective-permute-start | bytes 49160 | tf_op jit(solution)/shard_map/ppermute | solution.py:382
  15.0 4.2 %collective-permute-start.6 = (f32[2,1024]{1,0:T(2,128)S(1)}, f32[2,1024]{1,0:T(2,128)S(1)}, u32[]{:S(2)}, u32[]{:S(2)}) collective-permute-start(f32[2,1024]{1,0:T(2,128)S(1)} %get-tuple-element.121.refs_6_), channel_id=1, source_target_pairs={{0,8},{4,12},{8,0},{12,4},{1,9},{5,13},{9,1},{13,5},{2,10},{6,14},... | collective-permute-start | bytes 24584 | tf_op jit(solution)/shard_map/ppermute | solution.py:385
  20.8 3.9 %collective-permute-done.7.refs_10_ = f32[2,1024]{1,0:T(2,128)S(1)} collective-permute-done((f32[2,1024]{1,0:T(2,128)S(1)}, f32[2,1024]{1,0:T(2,128)S(1)}, u32[]{:S(2)}, u32[]{:S(2)}) %collective-permute-start.7) | collective-permute-done | bytes 8224 | tf_op jit(solution)/shard_map/ppermute | solution.py:383
  25.4 3.6 %collective-permute-done.8.refs_5_.refs_9_ = f32[4,1024]{1,0:T(4,128)S(1)} collective-permute-done((f32[4,1024]{1,0:T(4,128)S(1)}, f32[4,1024]{1,0:T(4,128)S(1)}, u32[]{:S(2)}, u32[]{:S(2)}) %collective-permute-start.8) | collective-permute-done | bytes 16416 | tf_op jit(solution)/shard_map/ppermute | solution.py:382
  32.1 2.9 %collective-permute-start.12 = (f32[2,1024]{1,0:T(2,128)S(1)}, f32[2,1024]{1,0:T(2,128)S(1)}, u32[]{:S(2)}, u32[]{:S(2)}) collective-permute-start(f32[2,1024]{1,0:T(2,128)S(1)} %get-tuple-element.133.refs_8_), channel_id=1, source_target_pairs={{0,12},{1,13},{2,14},{3,15},{4,5},{5,4},{6,7},{7,6},{8,9},{9,8},{1... | collective-permute-start | bytes 24584 | tf_op jit(solution)/shard_map/ppermute | solution.py:383
  38.3 3.6 %collective-permute-done.13.refs_5_.refs_9_ = f32[4,1024]{1,0:T(4,128)S(1)} collective-permute-done((f32[4,1024]{1,0:T(4,128)S(1)}, f32[4,1024]{1,0:T(4,128)S(1)}, u32[]{:S(2)}, u32[]{:S(2)}) %collective-permute-start.13) | collective-permute-done | bytes 16416 | tf_op jit(solution)/shard_map/ppermute | solution.py:382
  44.6 3.5 %collective-permute-start.16 = (f32[2,1024]{1,0:T(2,128)S(1)}, f32[2,1024]{1,0:T(2,128)S(1)}, u32[]{:S(2)}, u32[]{:S(2)}) collective-permute-start(f32[2,1024]{1,0:T(2,128)S(1)} %get-tuple-element.144.refs_8_), channel_id=1, source_target_pairs={{0,8},{4,12},{8,0},{12,4},{1,9},{5,13},{9,1},{13,5},{2,10},{6,14},... | collective-permute-start | bytes 24584 | tf_op jit(solution)/shard_map/ppermute | solution.py:385
  49.7 3.8 %collective-permute-done.17.refs_12_ = f32[2,1024]{1,0:T(2,128)S(1)} collective-permute-done((f32[2,1024]{1,0:T(2,128)S(1)}, f32[2,1024]{1,0:T(2,128)S(1)}, u32[]{:S(2)}, u32[]{:S(2)}) %collective-permute-start.17) | collective-permute-done | bytes 8224 | tf_op jit(solution)/shard_map/ppermute | solution.py:383
  54.3 3.6 %collective-permute-done.18.refs_5_.refs_9_ = f32[4,1024]{1,0:T(4,128)S(1)} collective-permute-done((f32[4,1024]{1,0:T(4,128)S(1)}, f32[4,1024]{1,0:T(4,128)S(1)}, u32[]{:S(2)}, u32[]{:S(2)}) %collective-permute-start.18) | collective-permute-done | bytes 16416 | tf_op jit(solution)/shard_map/ppermute | solution.py:382
  61.0 2.9 %collective-permute-start.22 = (f32[2,1024]{1,0:T(2,128)S(1)}, f32[2,1024]{1,0:T(2,128)S(1)}, u32[]{:S(2)}, u32[]{:S(2)}) collective-permute-start(f32[2,1024]{1,0:T(2,128)S(1)} %get-tuple-element.155.refs_8_), channel_id=1, source_target_pairs={{0,12},{1,13},{2,14},{3,15},{4,5},{5,4},{6,7},{7,6},{8,9},{9,8},{1... | collective-permute-start | bytes 24584 | tf_op jit(solution)/shard_map/ppermute | solution.py:383
  64.1 2.4 %collective-permute-done.22.refs_12_ = f32[2,1024]{1,0:T(2,128)S(1)} collective-permute-done((f32[2,1024]{1,0:T(2,128)S(1)}, f32[2,1024]{1,0:T(2,128)S(1)}, u32[]{:S(2)}, u32[]{:S(2)}) %collective-permute-start.22) | collective-permute-done | bytes 8224 | tf_op jit(solution)/shard_map/ppermute | solution.py:383
  67.2 3.6 %collective-permute-done.23.refs_5_.refs_9_ = f32[4,1024]{1,0:T(4,128)S(1)} collective-permute-done((f32[4,1024]{1,0:T(4,128)S(1)}, f32[4,1024]{1,0:T(4,128)S(1)}, u32[]{:S(2)}, u32[]{:S(2)}) %collective-permute-start.23) | collective-permute-done | bytes 16416 | tf_op jit(solution)/shard_map/ppermute | solution.py:382
  73.5 3.5 %collective-permute-start.26 = (f32[2,1024]{1,0:T(2,128)S(1)}, f32[2,1024]{1,0:T(2,128)S(1)}, u32[]{:S(2)}, u32[]{:S(2)}) collective-permute-start(f32[2,1024]{1,0:T(2,128)S(1)} %get-tuple-element.166.refs_8_), channel_id=1, source_target_pairs={{0,8},{4,12},{8,0},{12,4},{1,9},{5,13},{9,1},{13,5},{2,10},{6,14},... | collective-permute-start | bytes 24584 | tf_op jit(solution)/shard_map/ppermute | solution.py:385
  78.6 3.8 %collective-permute-done.27.refs_12_ = f32[2,1024]{1,0:T(2,128)S(1)} collective-permute-done((f32[2,1024]{1,0:T(2,128)S(1)}, f32[2,1024]{1,0:T(2,128)S(1)}, u32[]{:S(2)}, u32[]{:S(2)}) %collective-permute-start.27) | collective-permute-done | bytes 8224 | tf_op jit(solution)/shard_map/ppermute | solution.py:383
  83.1 3.6 %collective-permute-done.28.refs_5_.refs_9_ = f32[4,1024]{1,0:T(4,128)S(1)} collective-permute-done((f32[4,1024]{1,0:T(4,128)S(1)}, f32[4,1024]{1,0:T(4,128)S(1)}, u32[]{:S(2)}, u32[]{:S(2)}) %collective-permute-start.28) | collective-permute-done | bytes 16416 | tf_op jit(solution)/shard_map/ppermute | solution.py:382
  90.0 2.9 %collective-permute-start.32 = (f32[2,1024]{1,0:T(2,128)S(1)}, f32[2,1024]{1,0:T(2,128)S(1)}, u32[]{:S(2)}, u32[]{:S(2)}) collective-permute-start(f32[2,1024]{1,0:T(2,128)S(1)} %get-tuple-element.177.refs_8_), channel_id=1, source_target_pairs={{0,12},{1,13},{2,14},{3,15},{4,5},{5,4},{6,7},{7,6},{8,9},{9,8},{1... | collective-permute-start | bytes 24584 | tf_op jit(solution)/shard_map/ppermute | solution.py:383
  93.1 2.4 %collective-permute-done.32.refs_12_ = f32[2,1024]{1,0:T(2,128)S(1)} collective-permute-done((f32[2,1024]{1,0:T(2,128)S(1)}, f32[2,1024]{1,0:T(2,128)S(1)}, u32[]{:S(2)}, u32[]{:S(2)}) %collective-permute-start.32) | collective-permute-done | bytes 8224 | tf_op jit(solution)/shard_map/ppermute | solution.py:383
  96.2 3.6 %collective-permute-done.33.refs_5_.refs_9_ = f32[4,1024]{1,0:T(4,128)S(1)} collective-permute-done((f32[4,1024]{1,0:T(4,128)S(1)}, f32[4,1024]{1,0:T(4,128)S(1)}, u32[]{:S(2)}, u32[]{:S(2)}) %collective-permute-start.33) | collective-permute-done | bytes 16416 | tf_op jit(solution)/shard_map/ppermute | solution.py:382
  102.5 3.5 %collective-permute-start.36 = (f32[2,1024]{1,0:T(2,128)S(1)}, f32[2,1024]{1,0:T(2,128)S(1)}, u32[]{:S(2)}, u32[]{:S(2)}) collective-permute-start(f32[2,1024]{1,0:T(2,128)S(1)} %get-tuple-element.188.refs_8_), channel_id=1, source_target_pairs={{0,8},{4,12},{8,0},{12,4},{1,9},{5,13},{9,1},{13,5},{2,10},{6,14},... | collective-permute-start | bytes 24584 | tf_op jit(solution)/shard_map/ppermute | solution.py:385
  107.6 3.8 %collective-permute-done.37.refs_12_ = f32[2,1024]{1,0:T(2,128)S(1)} collective-permute-done((f32[2,1024]{1,0:T(2,128)S(1)}, f32[2,1024]{1,0:T(2,128)S(1)}, u32[]{:S(2)}, u32[]{:S(2)}) %collective-permute-start.37) | collective-permute-done | bytes 8224 | tf_op jit(solution)/shard_map/ppermute | solution.py:383
  112.2 3.6 %collective-permute-done.38.refs_5_.refs_3_ = f32[4,1024]{1,0:T(4,128)S(1)} collective-permute-done((f32[4,1024]{1,0:T(4,128)S(1)}, f32[4,1024]{1,0:T(4,128)S(1)}, u32[]{:S(2)}, u32[]{:S(2)}) %collective-permute-start.38) | collective-permute-done | bytes 16416 | tf_op jit(solution)/shard_map/ppermute | solution.py:382
  117.6 6.2 %collective-permute-done.42.got = f32[2,168,128]{2,1,0:T(8,128)S(1)} collective-permute-done((f32[2,168,128]{2,1,0:T(8,128)S(1)}, f32[2,168,128]{2,1,0:T(8,128)S(1)}, u32[]{:S(2)}, u32[]{:S(2)}) %collective-permute-start.42) | collective-permute-done | bytes 172064 | tf_op jit(solution)/shard_map/ppermute | solution.py:501
  125.5 2.9 %collective-permute-start.45 = (f32[2,1024]{1,0:T(2,128)S(1)}, f32[2,1024]{1,0:T(2,128)S(1)}, u32[]{:S(2)}, u32[]{:S(2)}) collective-permute-start(f32[2,1024]{1,0:T(2,128)S(1)} %get-tuple-element.202.refs_2_), channel_id=1, source_target_pairs={{0,12},{1,13},{2,14},{3,15},{4,5},{5,4},{6,7},{7,6},{8,9},{9,8},{1... | collective-permute-start | bytes 24584 | tf_op jit(solution)/shard_map/ppermute | solution.py:383
  133.9 2.4 %collective-permute-done.47.refs_6_ = f32[3,4,640]{2,1,0:T(4,128)S(1)} collective-permute-done((f32[3,4,640]{2,1,0:T(4,128)S(1)}, f32[3,4,640]{2,1,0:T(4,128)S(1)}, u32[]{:S(2)}, u32[]{:S(2)}) %collective-permute-start.47) | collective-permute-done | bytes 30752 | tf_op jit(solution)/shard_map/ppermute | solution.py:509
  (114 shorter events, 53.9 us)
Async XLA Ops:
  2.0 5.2 %collective-permute-start = (f32[2,2,168,512]{3,2,1,0:T(8,128)S(1)}, f32[2,2,168,512]{3,2,1,0:T(8,128)S(1)}, u32[]{:S(2)}, u32[]{:S(2)}) collective-permute-start(f32[2,2,168,512]{3,2,1,0:T(8,128)S(1)} %shard_map.157), channel_id=1, source_target_pairs={{0,1},{1,0},{2,3},{3,2},{4,5},{5,4},{6,7},{7,6},{8,9},{9,8},{10,11... | collective-permute-start | bytes 4128776 | tf_op jit(solution)/shard_map/ppermute | solution.py:432
  4.6 5.7 %collective-permute-start.3 = (f32[2,168,512]{2,1,0:T(8,128)S(1)}, f32[2,168,512]{2,1,0:T(8,128)S(1)}, u32[]{:S(2)}, u32[]{:S(2)}) collective-permute-start(f32[2,168,512]{2,1,0:T(8,128)S(1)} %get-tuple-element.113), channel_id=1, source_target_pairs={{0,1},{1,0},{2,3},{3,2},{4,5},{5,4},{6,7},{7,6},{8,9},{9,8},{10,11... | collective-permute-start | bytes 2064392 | tf_op jit(solution)/shard_map/ppermute | solution.py:444
  13.0 16.1 %collective-permute-start.10 = (bf16[2,168,256]{2,1,0:T(8,128)(2,1)S(1)}, bf16[2,168,256]{2,1,0:T(8,128)(2,1)S(1)}, u32[]{:S(2)}, u32[]{:S(2)}) collective-permute-start(bf16[2,168,256]{2,1,0:T(8,128)(2,1)S(1)} %get-tuple-element.127.refs_12_), channel_id=1, source_target_pairs={{0,2},{1,3},{2,0},{3,1},{4,6},{5,7},{6,4},{7,5},{8,10},{9,11},{10,... | collective-permute-start | bytes 516104 | tf_op jit(solution)/shard_map/ppermute | solution.py:474
  15.0 5.8 %collective-permute-start.6 = (f32[2,1024]{1,0:T(2,128)S(1)}, f32[2,1024]{1,0:T(2,128)S(1)}, u32[]{:S(2)}, u32[]{:S(2)}) collective-permute-start(f32[2,1024]{1,0:T(2,128)S(1)} %get-tuple-element.121.refs_6_), channel_id=1, source_target_pairs={{0,8},{4,12},{8,0},{12,4},{1,9},{5,13},{9,1},{13,5},{2,10},{6,14},... | collective-permute-start | bytes 24584 | tf_op jit(solution)/shard_map/ppermute | solution.py:385
  19.2 5.5 %collective-permute-start.7 = (f32[2,1024]{1,0:T(2,128)S(1)}, f32[2,1024]{1,0:T(2,128)S(1)}, u32[]{:S(2)}, u32[]{:S(2)}) collective-permute-start(f32[2,1024]{1,0:T(2,128)S(1)} %get-tuple-element.121.refs_6_), channel_id=1, source_target_pairs={{0,12},{1,13},{2,14},{3,15},{4,5},{5,4},{6,7},{7,6},{8,9},{9,8},{1... | collective-permute-start | bytes 24584 | tf_op jit(solution)/shard_map/ppermute | solution.py:383
  30.1 11.8 %collective-permute-start.15 = (bf16[2,168,256]{2,1,0:T(8,128)(2,1)S(1)}, bf16[2,168,256]{2,1,0:T(8,128)(2,1)S(1)}, u32[]{:S(2)}, u32[]{:S(2)}) collective-permute-start(bf16[2,168,256]{2,1,0:T(8,128)(2,1)S(1)} %get-tuple-element.138.refs_12_), channel_id=1, source_target_pairs={{0,2},{1,3},{2,0},{3,1},{4,6},{5,7},{6,4},{7,5},{8,10},{9,11},{10,... | collective-permute-start | bytes 516104 | tf_op jit(solution)/shard_map/ppermute | solution.py:474
  32.1 5.4 %collective-permute-start.12 = (f32[2,1024]{1,0:T(2,128)S(1)}, f32[2,1024]{1,0:T(2,128)S(1)}, u32[]{:S(2)}, u32[]{:S(2)}) collective-permute-start(f32[2,1024]{1,0:T(2,128)S(1)} %get-tuple-element.133.refs_8_), channel_id=1, source_target_pairs={{0,12},{1,13},{2,14},{3,15},{4,5},{5,4},{6,7},{7,6},{8,9},{9,8},{1... | collective-permute-start | bytes 24584 | tf_op jit(solution)/shard_map/ppermute | solution.py:383
  43.0 14.9 %collective-permute-start.20 = (bf16[2,168,256]{2,1,0:T(8,128)(2,1)S(1)}, bf16[2,168,256]{2,1,0:T(8,128)(2,1)S(1)}, u32[]{:S(2)}, u32[]{:S(2)}) collective-permute-start(bf16[2,168,256]{2,1,0:T(8,128)(2,1)S(1)} %get-tuple-element.149.refs_12_), channel_id=1, source_target_pairs={{0,2},{1,3},{2,0},{3,1},{4,6},{5,7},{6,4},{7,5},{8,10},{9,11},{10,... | collective-permute-start | bytes 516104 | tf_op jit(solution)/shard_map/ppermute | solution.py:474
  44.6 5.1 %collective-permute-start.16 = (f32[2,1024]{1,0:T(2,128)S(1)}, f32[2,1024]{1,0:T(2,128)S(1)}, u32[]{:S(2)}, u32[]{:S(2)}) collective-permute-start(f32[2,1024]{1,0:T(2,128)S(1)} %get-tuple-element.144.refs_8_), channel_id=1, source_target_pairs={{0,8},{4,12},{8,0},{12,4},{1,9},{5,13},{9,1},{13,5},{2,10},{6,14},... | collective-permute-start | bytes 24584 | tf_op jit(solution)/shard_map/ppermute | solution.py:385
  48.1 5.4 %collective-permute-start.17 = (f32[2,1024]{1,0:T(2,128)S(1)}, f32[2,1024]{1,0:T(2,128)S(1)}, u32[]{:S(2)}, u32[]{:S(2)}) collective-permute-start(f32[2,1024]{1,0:T(2,128)S(1)} %get-tuple-element.144.refs_8_), channel_id=1, source_target_pairs={{0,12},{1,13},{2,14},{3,15},{4,5},{5,4},{6,7},{7,6},{8,9},{9,8},{1... | collective-permute-start | bytes 24584 | tf_op jit(solution)/shard_map/ppermute | solution.py:383
  59.0 11.8 %collective-permute-start.25 = (bf16[2,168,256]{2,1,0:T(8,128)(2,1)S(1)}, bf16[2,168,256]{2,1,0:T(8,128)(2,1)S(1)}, u32[]{:S(2)}, u32[]{:S(2)}) collective-permute-start(bf16[2,168,256]{2,1,0:T(8,128)(2,1)S(1)} %get-tuple-element.160.refs_12_), channel_id=1, source_target_pairs={{0,2},{1,3},{2,0},{3,1},{4,6},{5,7},{6,4},{7,5},{8,10},{9,11},{10,... | collective-permute-start | bytes 516104 | tf_op jit(solution)/shard_map/ppermute | solution.py:474
  61.0 5.4 %collective-permute-start.22 = (f32[2,1024]{1,0:T(2,128)S(1)}, f32[2,1024]{1,0:T(2,128)S(1)}, u32[]{:S(2)}, u32[]{:S(2)}) collective-permute-start(f32[2,1024]{1,0:T(2,128)S(1)} %get-tuple-element.155.refs_8_), channel_id=1, source_target_pairs={{0,12},{1,13},{2,14},{3,15},{4,5},{5,4},{6,7},{7,6},{8,9},{9,8},{1... | collective-permute-start | bytes 24584 | tf_op jit(solution)/shard_map/ppermute | solution.py:383
  71.9 14.9 %collective-permute-start.30 = (bf16[2,168,256]{2,1,0:T(8,128)(2,1)S(1)}, bf16[2,168,256]{2,1,0:T(8,128)(2,1)S(1)}, u32[]{:S(2)}, u32[]{:S(2)}) collective-permute-start(bf16[2,168,256]{2,1,0:T(8,128)(2,1)S(1)} %get-tuple-element.171.refs_12_), channel_id=1, source_target_pairs={{0,2},{1,3},{2,0},{3,1},{4,6},{5,7},{6,4},{7,5},{8,10},{9,11},{10,... | collective-permute-start | bytes 516104 | tf_op jit(solution)/shard_map/ppermute | solution.py:474
  73.5 5.1 %collective-permute-start.26 = (f32[2,1024]{1,0:T(2,128)S(1)}, f32[2,1024]{1,0:T(2,128)S(1)}, u32[]{:S(2)}, u32[]{:S(2)}) collective-permute-start(f32[2,1024]{1,0:T(2,128)S(1)} %get-tuple-element.166.refs_8_), channel_id=1, source_target_pairs={{0,8},{4,12},{8,0},{12,4},{1,9},{5,13},{9,1},{13,5},{2,10},{6,14},... | collective-permute-start | bytes 24584 | tf_op jit(solution)/shard_map/ppermute | solution.py:385
  77.0 5.4 %collective-permute-start.27 = (f32[2,1024]{1,0:T(2,128)S(1)}, f32[2,1024]{1,0:T(2,128)S(1)}, u32[]{:S(2)}, u32[]{:S(2)}) collective-permute-start(f32[2,1024]{1,0:T(2,128)S(1)} %get-tuple-element.166.refs_8_), channel_id=1, source_target_pairs={{0,12},{1,13},{2,14},{3,15},{4,5},{5,4},{6,7},{7,6},{8,9},{9,8},{1... | collective-permute-start | bytes 24584 | tf_op jit(solution)/shard_map/ppermute | solution.py:383
  87.8 12.0 %collective-permute-start.35 = (bf16[2,168,256]{2,1,0:T(8,128)(2,1)S(1)}, bf16[2,168,256]{2,1,0:T(8,128)(2,1)S(1)}, u32[]{:S(2)}, u32[]{:S(2)}) collective-permute-start(bf16[2,168,256]{2,1,0:T(8,128)(2,1)S(1)} %get-tuple-element.182.refs_12_), channel_id=1, source_target_pairs={{0,2},{1,3},{2,0},{3,1},{4,6},{5,7},{6,4},{7,5},{8,10},{9,11},{10,... | collective-permute-start | bytes 516104 | tf_op jit(solution)/shard_map/ppermute | solution.py:474
  90.0 5.4 %collective-permute-start.32 = (f32[2,1024]{1,0:T(2,128)S(1)}, f32[2,1024]{1,0:T(2,128)S(1)}, u32[]{:S(2)}, u32[]{:S(2)}) collective-permute-start(f32[2,1024]{1,0:T(2,128)S(1)} %get-tuple-element.177.refs_8_), channel_id=1, source_target_pairs={{0,12},{1,13},{2,14},{3,15},{4,5},{5,4},{6,7},{7,6},{8,9},{9,8},{1... | collective-permute-start | bytes 24584 | tf_op jit(solution)/shard_map/ppermute | solution.py:383
  100.9 14.9 %collective-permute-start.40 = (bf16[2,168,256]{2,1,0:T(8,128)(2,1)S(1)}, bf16[2,168,256]{2,1,0:T(8,128)(2,1)S(1)}, u32[]{:S(2)}, u32[]{:S(2)}) collective-permute-start(bf16[2,168,256]{2,1,0:T(8,128)(2,1)S(1)} %get-tuple-element.193.refs_12_), channel_id=1, source_target_pairs={{0,2},{1,3},{2,0},{3,1},{4,6},{5,7},{6,4},{7,5},{8,10},{9,11},{10,... | collective-permute-start | bytes 516104 | tf_op jit(solution)/shard_map/ppermute | solution.py:474
  102.5 5.1 %collective-permute-start.36 = (f32[2,1024]{1,0:T(2,128)S(1)}, f32[2,1024]{1,0:T(2,128)S(1)}, u32[]{:S(2)}, u32[]{:S(2)}) collective-permute-start(f32[2,1024]{1,0:T(2,128)S(1)} %get-tuple-element.188.refs_8_), channel_id=1, source_target_pairs={{0,8},{4,12},{8,0},{12,4},{1,9},{5,13},{9,1},{13,5},{2,10},{6,14},... | collective-permute-start | bytes 24584 | tf_op jit(solution)/shard_map/ppermute | solution.py:385
  106.0 5.4 %collective-permute-start.37 = (f32[2,1024]{1,0:T(2,128)S(1)}, f32[2,1024]{1,0:T(2,128)S(1)}, u32[]{:S(2)}, u32[]{:S(2)}) collective-permute-start(f32[2,1024]{1,0:T(2,128)S(1)} %get-tuple-element.188.refs_8_), channel_id=1, source_target_pairs={{0,12},{1,13},{2,14},{3,15},{4,5},{5,4},{6,7},{7,6},{8,9},{9,8},{1... | collective-permute-start | bytes 24584 | tf_op jit(solution)/shard_map/ppermute | solution.py:383
  116.9 20.1 %collective-permute-start.41 = (f32[2,168,512]{2,1,0:T(8,128)S(1)}, f32[2,168,512]{2,1,0:T(8,128)S(1)}, u32[]{:S(2)}, u32[]{:S(2)}) collective-permute-start(f32[2,168,512]{2,1,0:T(8,128)S(1)} %get-tuple-element.196), channel_id=1, source_target_pairs={{0,1},{1,0},{2,3},{3,2},{4,5},{5,4},{6,7},{7,6},{8,9},{9,8},{10,11... | collective-permute-start | bytes 2064392 | tf_op jit(solution)/shard_map/ppermute | solution.py:502
  117.0 6.8 %collective-permute-start.42 = (f32[2,168,128]{2,1,0:T(8,128)S(1)}, f32[2,168,128]{2,1,0:T(8,128)S(1)}, u32[]{:S(2)}, u32[]{:S(2)}) collective-permute-start(f32[2,168,128]{2,1,0:T(8,128)S(1)} %get-tuple-element.198), channel_id=1, source_target_pairs={{0,2},{1,3},{2,0},{3,1},{4,6},{5,7},{6,4},{7,5},{8,10},{9,11},{10,... | collective-permute-start | bytes 516104 | tf_op jit(solution)/shard_map/ppermute | solution.py:501
  123.9 12.4 %collective-permute-start.43 = (f32[2,64,168]{2,1,0:T(8,128)S(1)}, f32[2,64,168]{2,1,0:T(8,128)S(1)}, u32[]{:S(2)}, u32[]{:S(2)}) collective-permute-start(f32[2,64,168]{2,1,0:T(8,128)S(1)} %get-tuple-element.200), channel_id=1, source_target_pairs={{0,1},{1,0},{2,3},{3,2},{4,5},{5,4},{6,7},{7,6},{8,9},{9,8},{10,11... | collective-permute-start | bytes 258056 | tf_op jit(solution)/shard_map/ppermute | solution.py:517
  125.5 5.4 %collective-permute-start.45 = (f32[2,1024]{1,0:T(2,128)S(1)}, f32[2,1024]{1,0:T(2,128)S(1)}, u32[]{:S(2)}, u32[]{:S(2)}) collective-permute-start(f32[2,1024]{1,0:T(2,128)S(1)} %get-tuple-element.202.refs_2_), channel_id=1, source_target_pairs={{0,12},{1,13},{2,14},{3,15},{4,5},{5,4},{6,7},{7,6},{8,9},{9,8},{1... | collective-permute-start | bytes 24584 | tf_op jit(solution)/shard_map/ppermute | solution.py:383
  (32 other events, 135.8 us)

commit v7 on v6

--- a/solution.py
+++ b/solution.py
@@ -101,23 +101,24 @@
     out[...] = tile[0] * mask[0].astype(F32).astype(BF16)
 
 
-def message_body(paired, own, twin, part, part_in, small, small_in, *outs):
-    matrix, turned, const, invest, near, far, mean = outs
+def message_body(paired, own, twin, near, far, mean):
     _, mine, _, width = own.shape
-    sections = invest.shape[0]
-    for half, src in enumerate((part, part_in)):
-        cols = slice(half * width, (half + 1) * width)
-        matrix[:, cols] = src[...]
-        turned[cols, :] = src[...].T
-    for src, cols in ((small, slice(0, width)), (small_in, slice(width, 2 * width))):
-        const[:, :, cols] = src[:sections]
-        invest[:, :, cols] = src[sections:]
     both = (own, twin)
     for s in range(mine):
         for half, cols, flat in tiles(width):
             src = both[half]
             write_message(paired, near, far, s, flat, src[1, s, :, cols], src[0, s, :, cols])
     mean[...] = near[:mine, :]
+
+
+def assemble_body(part, part_in, small, small_in, matrix, turned, const, invest):
+    sections, width = invest.shape[0], part.shape[1]
+    for half, src, rest in ((0, part, small), (1, part_in, small_in)):
+        cols = slice(half * width, (half + 1) * width)
+        matrix[:, cols] = src[...]
+        turned[cols, :] = src[...].T
+        const[:, :, cols] = rest[:sections]
+        invest[:, :, cols] = rest[sections:]
 
 
 def is_odd():
@@ -442,10 +443,13 @@
         scratch=(pltpu.SemaphoreType.DMA((6,)),),
     )
     twin_cost = lax.ppermute(cost_give, "reg", twin)
-    matrix, turned, const, invest, near, far, mean = call(
-        functools.partial(message_body, paired),
-        (in_vmem((rows, 2 * width), BF16), in_vmem((2 * width, rows), BF16), invest_like, invest_like, message, message, mean_like),
-        (own, twin_state, part, part_in, small, small_in),
+    near, far, mean = call(
+        functools.partial(message_body, paired), (message, message, mean_like), (own, twin_state)
+    )
+    matrix, turned, const, invest = call(
+        assemble_body,
+        (in_vmem((rows, 2 * width), BF16), in_vmem((2 * width, rows), BF16), invest_like, invest_like),
+        (part, part_in, small, small_in),
     )
     near_in, far_in, sums = hour_exchange(near, far, mean, paired)
 

time: 138 us -> 137 us (level)
  waiting for transfers between devices: 66.4 us -> 64.5 us
    ppermute x1, waiting for transfers between devices: 1.7 us -> 0.01 us  [shards(): small_in = lax.ppermute(small_give, 'reg', twin)]
    pallas_call x26 -> x27, Pallas kernels: 18.7 us -> 19 us  [call(): pl.pallas_call(body, out_shape=tuple(outs), in_specs=arg_specs or [IN_VME...]
  transfers between devices with their start and end apart: 48 -> 48, of which waited for: 28 -> 27; matrix products, arithmetic and copies ran while one was open for 0% -> 0% of each run, Pallas kernels for 6% -> 6%
where the time goes in v7:
time: 137 us
  waiting for transfers between devices  64.5 us (47%)
  starting transfers between devices  52 us (38%)
  Pallas kernels  19 us (14%)
    ppermute x8, waiting for transfers between devices, hour_exchange(): near_in = lax.ppermute(near, 'hour', partners(1))  27 us
    ppermute x8, waiting for transfers between devices, hour_exchange(): far_in = lax.ppermute(mean, ('hour', 'reg'), mirror((0, count - 1)))  24.7 us
    ppermute x8, starting transfers between devices, hour_exchange(): across = lax.ppermute(mean, 'hour', partners(2))  20.5 us
    pallas_call x27, Pallas kernels, call(): pl.pallas_call(body, out_shape=tuple(outs), in_specs=arg_specs or [IN_VME...  19 us
    ppermute x8, starting transfers between devices, hour_exchange(): far_in = lax.ppermute(mean, ('hour', 'reg'), mirror((0, count - 1)))  15.3 us
    ppermute x7, starting transfers between devices, shards(): received = lax.ppermute(sent, 'reg', other_chip)  8.5 us
    ppermute x1, waiting for transfers between devices, shards(): rows_got = lax.ppermute(rows_give, 'reg', other_chip)  6.21 us
    ppermute x8, waiting for transfers between devices, hour_exchange(): across = lax.ppermute(mean, 'hour', partners(2))  3.58 us
  transfers between devices with their start and end apart: 48, of which 27 were waited for; matrix products, arithmetic and copies ran while one was open for 0% of the time, Pallas kernels for 6%

profile of v7, /device:TPU:0, one launch (start us, length us, event | category | flops | bytes accessed | tf_op | source)
XLA Modules:
  0.0 136.7 jit_solution(9819498728922282845)
XLA Ops:
  5.6 3.0 %collective-permute-start.4 = (f32[4,1024]{1,0:T(4,128)S(1)}, f32[4,1024]{1,0:T(4,128)S(1)}, u32[]{:S(2)}, u32[]{:S(2)}) collective-permute-start(f32[4,1024]{1,0:T(4,128)S(1)} %get-tuple-element.115), channel_id=1, source_target_pairs={{0,4},{4,0},{8,12},{12,8},{1,5},{5,1},{9,13},{13,9},{2,6},{6,2},{1... | collective-permute-start | bytes 49160 | tf_op jit(solution)/shard_map/ppermute | solution.py:383
  13.4 4.2 %collective-permute-start.6 = (f32[2,1024]{1,0:T(2,128)S(1)}, f32[2,1024]{1,0:T(2,128)S(1)}, u32[]{:S(2)}, u32[]{:S(2)}) collective-permute-start(f32[2,1024]{1,0:T(2,128)S(1)} %get-tuple-element.121.refs_6_), channel_id=1, source_target_pairs={{0,8},{4,12},{8,0},{12,4},{1,9},{5,13},{9,1},{13,5},{2,10},{6,14},... | collective-permute-start | bytes 24584 | tf_op jit(solution)/shard_map/ppermute | solution.py:386
  19.2 3.8 %collective-permute-done.7.refs_10_ = f32[2,1024]{1,0:T(2,128)S(1)} collective-permute-done((f32[2,1024]{1,0:T(2,128)S(1)}, f32[2,1024]{1,0:T(2,128)S(1)}, u32[]{:S(2)}, u32[]{:S(2)}) %collective-permute-start.7) | collective-permute-done | bytes 8224 | tf_op jit(solution)/shard_map/ppermute | solution.py:384
  23.7 3.6 %collective-permute-done.8.refs_5_.refs_9_ = f32[4,1024]{1,0:T(4,128)S(1)} collective-permute-done((f32[4,1024]{1,0:T(4,128)S(1)}, f32[4,1024]{1,0:T(4,128)S(1)}, u32[]{:S(2)}, u32[]{:S(2)}) %collective-permute-start.8) | collective-permute-done | bytes 16416 | tf_op jit(solution)/shard_map/ppermute | solution.py:383
  30.5 2.9 %collective-permute-start.12 = (f32[2,1024]{1,0:T(2,128)S(1)}, f32[2,1024]{1,0:T(2,128)S(1)}, u32[]{:S(2)}, u32[]{:S(2)}) collective-permute-start(f32[2,1024]{1,0:T(2,128)S(1)} %get-tuple-element.133.refs_8_), channel_id=1, source_target_pairs={{0,12},{1,13},{2,14},{3,15},{4,5},{5,4},{6,7},{7,6},{8,9},{9,8},{1... | collective-permute-start | bytes 24584 | tf_op jit(solution)/shard_map/ppermute | solution.py:384
  33.6 2.4 %collective-permute-done.12.refs_12_ = f32[2,1024]{1,0:T(2,128)S(1)} collective-permute-done((f32[2,1024]{1,0:T(2,128)S(1)}, f32[2,1024]{1,0:T(2,128)S(1)}, u32[]{:S(2)}, u32[]{:S(2)}) %collective-permute-start.12) | collective-permute-done | bytes 8224 | tf_op jit(solution)/shard_map/ppermute | solution.py:384
  36.7 3.6 %collective-permute-done.13.refs_5_.refs_9_ = f32[4,1024]{1,0:T(4,128)S(1)} collective-permute-done((f32[4,1024]{1,0:T(4,128)S(1)}, f32[4,1024]{1,0:T(4,128)S(1)}, u32[]{:S(2)}, u32[]{:S(2)}) %collective-permute-start.13) | collective-permute-done | bytes 16416 | tf_op jit(solution)/shard_map/ppermute | solution.py:383
  43.0 3.5 %collective-permute-start.16 = (f32[2,1024]{1,0:T(2,128)S(1)}, f32[2,1024]{1,0:T(2,128)S(1)}, u32[]{:S(2)}, u32[]{:S(2)}) collective-permute-start(f32[2,1024]{1,0:T(2,128)S(1)} %get-tuple-element.144.refs_8_), channel_id=1, source_target_pairs={{0,8},{4,12},{8,0},{12,4},{1,9},{5,13},{9,1},{13,5},{2,10},{6,14},... | collective-permute-start | bytes 24584 | tf_op jit(solution)/shard_map/ppermute | solution.py:386
  48.1 3.8 %collective-permute-done.17.refs_12_ = f32[2,1024]{1,0:T(2,128)S(1)} collective-permute-done((f32[2,1024]{1,0:T(2,128)S(1)}, f32[2,1024]{1,0:T(2,128)S(1)}, u32[]{:S(2)}, u32[]{:S(2)}) %collective-permute-start.17) | collective-permute-done | bytes 8224 | tf_op jit(solution)/shard_map/ppermute | solution.py:384
  52.6 3.6 %collective-permute-done.18.refs_5_.refs_9_ = f32[4,1024]{1,0:T(4,128)S(1)} collective-permute-done((f32[4,1024]{1,0:T(4,128)S(1)}, f32[4,1024]{1,0:T(4,128)S(1)}, u32[]{:S(2)}, u32[]{:S(2)}) %collective-permute-start.18) | collective-permute-done | bytes 16416 | tf_op jit(solution)/shard_map/ppermute | solution.py:383
  59.4 2.9 %collective-permute-start.22 = (f32[2,1024]{1,0:T(2,128)S(1)}, f32[2,1024]{1,0:T(2,128)S(1)}, u32[]{:S(2)}, u32[]{:S(2)}) collective-permute-start(f32[2,1024]{1,0:T(2,128)S(1)} %get-tuple-element.155.refs_8_), channel_id=1, source_target_pairs={{0,12},{1,13},{2,14},{3,15},{4,5},{5,4},{6,7},{7,6},{8,9},{9,8},{1... | collective-permute-start | bytes 24584 | tf_op jit(solution)/shard_map/ppermute | solution.py:384
  65.5 3.6 %collective-permute-done.23.refs_5_.refs_9_ = f32[4,1024]{1,0:T(4,128)S(1)} collective-permute-done((f32[4,1024]{1,0:T(4,128)S(1)}, f32[4,1024]{1,0:T(4,128)S(1)}, u32[]{:S(2)}, u32[]{:S(2)}) %collective-permute-start.23) | collective-permute-done | bytes 16416 | tf_op jit(solution)/shard_map/ppermute | solution.py:383
  71.8 3.5 %collective-permute-start.26 = (f32[2,1024]{1,0:T(2,128)S(1)}, f32[2,1024]{1,0:T(2,128)S(1)}, u32[]{:S(2)}, u32[]{:S(2)}) collective-permute-start(f32[2,1024]{1,0:T(2,128)S(1)} %get-tuple-element.166.refs_8_), channel_id=1, source_target_pairs={{0,8},{4,12},{8,0},{12,4},{1,9},{5,13},{9,1},{13,5},{2,10},{6,14},... | collective-permute-start | bytes 24584 | tf_op jit(solution)/shard_map/ppermute | solution.py:386
  77.0 3.8 %collective-permute-done.27.refs_12_ = f32[2,1024]{1,0:T(2,128)S(1)} collective-permute-done((f32[2,1024]{1,0:T(2,128)S(1)}, f32[2,1024]{1,0:T(2,128)S(1)}, u32[]{:S(2)}, u32[]{:S(2)}) %collective-permute-start.27) | collective-permute-done | bytes 8224 | tf_op jit(solution)/shard_map/ppermute | solution.py:384
  81.5 3.6 %collective-permute-done.28.refs_5_.refs_9_ = f32[4,1024]{1,0:T(4,128)S(1)} collective-permute-done((f32[4,1024]{1,0:T(4,128)S(1)}, f32[4,1024]{1,0:T(4,128)S(1)}, u32[]{:S(2)}, u32[]{:S(2)}) %collective-permute-start.28) | collective-permute-done | bytes 16416 | tf_op jit(solution)/shard_map/ppermute | solution.py:383
  88.4 2.9 %collective-permute-start.32 = (f32[2,1024]{1,0:T(2,128)S(1)}, f32[2,1024]{1,0:T(2,128)S(1)}, u32[]{:S(2)}, u32[]{:S(2)}) collective-permute-start(f32[2,1024]{1,0:T(2,128)S(1)} %get-tuple-element.177.refs_8_), channel_id=1, source_target_pairs={{0,12},{1,13},{2,14},{3,15},{4,5},{5,4},{6,7},{7,6},{8,9},{9,8},{1... | collective-permute-start | bytes 24584 | tf_op jit(solution)/shard_map/ppermute | solution.py:384
  91.5 2.4 %collective-permute-done.32.refs_12_ = f32[2,1024]{1,0:T(2,128)S(1)} collective-permute-done((f32[2,1024]{1,0:T(2,128)S(1)}, f32[2,1024]{1,0:T(2,128)S(1)}, u32[]{:S(2)}, u32[]{:S(2)}) %collective-permute-start.32) | collective-permute-done | bytes 8224 | tf_op jit(solution)/shard_map/ppermute | solution.py:384
  94.6 3.6 %collective-permute-done.33.refs_5_.refs_9_ = f32[4,1024]{1,0:T(4,128)S(1)} collective-permute-done((f32[4,1024]{1,0:T(4,128)S(1)}, f32[4,1024]{1,0:T(4,128)S(1)}, u32[]{:S(2)}, u32[]{:S(2)}) %collective-permute-start.33) | collective-permute-done | bytes 16416 | tf_op jit(solution)/shard_map/ppermute | solution.py:383
  100.9 3.5 %collective-permute-start.36 = (f32[2,1024]{1,0:T(2,128)S(1)}, f32[2,1024]{1,0:T(2,128)S(1)}, u32[]{:S(2)}, u32[]{:S(2)}) collective-permute-start(f32[2,1024]{1,0:T(2,128)S(1)} %get-tuple-element.188.refs_8_), channel_id=1, source_target_pairs={{0,8},{4,12},{8,0},{12,4},{1,9},{5,13},{9,1},{13,5},{2,10},{6,14},... | collective-permute-start | bytes 24584 | tf_op jit(solution)/shard_map/ppermute | solution.py:386
  106.0 3.8 %collective-permute-done.37.refs_12_ = f32[2,1024]{1,0:T(2,128)S(1)} collective-permute-done((f32[2,1024]{1,0:T(2,128)S(1)}, f32[2,1024]{1,0:T(2,128)S(1)}, u32[]{:S(2)}, u32[]{:S(2)}) %collective-permute-start.37) | collective-permute-done | bytes 8224 | tf_op jit(solution)/shard_map/ppermute | solution.py:384
  110.5 3.6 %collective-permute-done.38.refs_5_.refs_3_ = f32[4,1024]{1,0:T(4,128)S(1)} collective-permute-done((f32[4,1024]{1,0:T(4,128)S(1)}, f32[4,1024]{1,0:T(4,128)S(1)}, u32[]{:S(2)}, u32[]{:S(2)}) %collective-permute-start.38) | collective-permute-done | bytes 16416 | tf_op jit(solution)/shard_map/ppermute | solution.py:383
  116.0 6.2 %collective-permute-done.42.got = f32[2,168,128]{2,1,0:T(8,128)S(1)} collective-permute-done((f32[2,168,128]{2,1,0:T(8,128)S(1)}, f32[2,168,128]{2,1,0:T(8,128)S(1)}, u32[]{:S(2)}, u32[]{:S(2)}) %collective-permute-start.42) | collective-permute-done | bytes 172064 | tf_op jit(solution)/shard_map/ppermute | solution.py:505
  123.9 2.9 %collective-permute-start.45 = (f32[2,1024]{1,0:T(2,128)S(1)}, f32[2,1024]{1,0:T(2,128)S(1)}, u32[]{:S(2)}, u32[]{:S(2)}) collective-permute-start(f32[2,1024]{1,0:T(2,128)S(1)} %get-tuple-element.202.refs_2_), channel_id=1, source_target_pairs={{0,12},{1,13},{2,14},{3,15},{4,5},{5,4},{6,7},{7,6},{8,9},{9,8},{1... | collective-permute-start | bytes 24584 | tf_op jit(solution)/shard_map/ppermute | solution.py:384
  132.3 2.4 %collective-permute-done.47.refs_6_ = f32[3,4,640]{2,1,0:T(4,128)S(1)} collective-permute-done((f32[3,4,640]{2,1,0:T(4,128)S(1)}, f32[3,4,640]{2,1,0:T(4,128)S(1)}, u32[]{:S(2)}, u32[]{:S(2)}) %collective-permute-start.47) | collective-permute-done | bytes 30752 | tf_op jit(solution)/shard_map/ppermute | solution.py:513
  (115 shorter events, 52.1 us)
Async XLA Ops:
  5.6 4.7 %collective-permute-start.4 = (f32[4,1024]{1,0:T(4,128)S(1)}, f32[4,1024]{1,0:T(4,128)S(1)}, u32[]{:S(2)}, u32[]{:S(2)}) collective-permute-start(f32[4,1024]{1,0:T(4,128)S(1)} %get-tuple-element.115), channel_id=1, source_target_pairs={{0,4},{4,0},{8,12},{12,8},{1,5},{5,1},{9,13},{13,9},{2,6},{6,2},{1... | collective-permute-start | bytes 49160 | tf_op jit(solution)/shard_map/ppermute | solution.py:383
  11.4 16.0 %collective-permute-start.10 = (bf16[2,168,256]{2,1,0:T(8,128)(2,1)S(1)}, bf16[2,168,256]{2,1,0:T(8,128)(2,1)S(1)}, u32[]{:S(2)}, u32[]{:S(2)}) collective-permute-start(bf16[2,168,256]{2,1,0:T(8,128)(2,1)S(1)} %get-tuple-element.127.refs_12_), channel_id=1, source_target_pairs={{0,2},{1,3},{2,0},{3,1},{4,6},{5,7},{6,4},{7,5},{8,10},{9,11},{10,... | collective-permute-start | bytes 516104 | tf_op jit(solution)/shard_map/ppermute | solution.py:478
  13.4 5.8 %collective-permute-start.6 = (f32[2,1024]{1,0:T(2,128)S(1)}, f32[2,1024]{1,0:T(2,128)S(1)}, u32[]{:S(2)}, u32[]{:S(2)}) collective-permute-start(f32[2,1024]{1,0:T(2,128)S(1)} %get-tuple-element.121.refs_6_), channel_id=1, source_target_pairs={{0,8},{4,12},{8,0},{12,4},{1,9},{5,13},{9,1},{13,5},{2,10},{6,14},... | collective-permute-start | bytes 24584 | tf_op jit(solution)/shard_map/ppermute | solution.py:386
  17.6 5.4 %collective-permute-start.7 = (f32[2,1024]{1,0:T(2,128)S(1)}, f32[2,1024]{1,0:T(2,128)S(1)}, u32[]{:S(2)}, u32[]{:S(2)}) collective-permute-start(f32[2,1024]{1,0:T(2,128)S(1)} %get-tuple-element.121.refs_6_), channel_id=1, source_target_pairs={{0,12},{1,13},{2,14},{3,15},{4,5},{5,4},{6,7},{7,6},{8,9},{9,8},{1... | collective-permute-start | bytes 24584 | tf_op jit(solution)/shard_map/ppermute | solution.py:384
  28.5 11.9 %collective-permute-start.15 = (bf16[2,168,256]{2,1,0:T(8,128)(2,1)S(1)}, bf16[2,168,256]{2,1,0:T(8,128)(2,1)S(1)}, u32[]{:S(2)}, u32[]{:S(2)}) collective-permute-start(bf16[2,168,256]{2,1,0:T(8,128)(2,1)S(1)} %get-tuple-element.138.refs_12_), channel_id=1, source_target_pairs={{0,2},{1,3},{2,0},{3,1},{4,6},{5,7},{6,4},{7,5},{8,10},{9,11},{10,... | collective-permute-start | bytes 516104 | tf_op jit(solution)/shard_map/ppermute | solution.py:478
  30.5 5.4 %collective-permute-start.12 = (f32[2,1024]{1,0:T(2,128)S(1)}, f32[2,1024]{1,0:T(2,128)S(1)}, u32[]{:S(2)}, u32[]{:S(2)}) collective-permute-start(f32[2,1024]{1,0:T(2,128)S(1)} %get-tuple-element.133.refs_8_), channel_id=1, source_target_pairs={{0,12},{1,13},{2,14},{3,15},{4,5},{5,4},{6,7},{7,6},{8,9},{9,8},{1... | collective-permute-start | bytes 24584 | tf_op jit(solution)/shard_map/ppermute | solution.py:384
  41.4 14.9 %collective-permute-start.20 = (bf16[2,168,256]{2,1,0:T(8,128)(2,1)S(1)}, bf16[2,168,256]{2,1,0:T(8,128)(2,1)S(1)}, u32[]{:S(2)}, u32[]{:S(2)}) collective-permute-start(bf16[2,168,256]{2,1,0:T(8,128)(2,1)S(1)} %get-tuple-element.149.refs_12_), channel_id=1, source_target_pairs={{0,2},{1,3},{2,0},{3,1},{4,6},{5,7},{6,4},{7,5},{8,10},{9,11},{10,... | collective-permute-start | bytes 516104 | tf_op jit(solution)/shard_map/ppermute | solution.py:478
  43.0 5.1 %collective-permute-start.16 = (f32[2,1024]{1,0:T(2,128)S(1)}, f32[2,1024]{1,0:T(2,128)S(1)}, u32[]{:S(2)}, u32[]{:S(2)}) collective-permute-start(f32[2,1024]{1,0:T(2,128)S(1)} %get-tuple-element.144.refs_8_), channel_id=1, source_target_pairs={{0,8},{4,12},{8,0},{12,4},{1,9},{5,13},{9,1},{13,5},{2,10},{6,14},... | collective-permute-start | bytes 24584 | tf_op jit(solution)/shard_map/ppermute | solution.py:386
  46.5 5.4 %collective-permute-start.17 = (f32[2,1024]{1,0:T(2,128)S(1)}, f32[2,1024]{1,0:T(2,128)S(1)}, u32[]{:S(2)}, u32[]{:S(2)}) collective-permute-start(f32[2,1024]{1,0:T(2,128)S(1)} %get-tuple-element.144.refs_8_), channel_id=1, source_target_pairs={{0,12},{1,13},{2,14},{3,15},{4,5},{5,4},{6,7},{7,6},{8,9},{9,8},{1... | collective-permute-start | bytes 24584 | tf_op jit(solution)/shard_map/ppermute | solution.py:384
  57.3 11.9 %collective-permute-start.25 = (bf16[2,168,256]{2,1,0:T(8,128)(2,1)S(1)}, bf16[2,168,256]{2,1,0:T(8,128)(2,1)S(1)}, u32[]{:S(2)}, u32[]{:S(2)}) collective-permute-start(bf16[2,168,256]{2,1,0:T(8,128)(2,1)S(1)} %get-tuple-element.160.refs_12_), channel_id=1, source_target_pairs={{0,2},{1,3},{2,0},{3,1},{4,6},{5,7},{6,4},{7,5},{8,10},{9,11},{10,... | collective-permute-start | bytes 516104 | tf_op jit(solution)/shard_map/ppermute | solution.py:478
  59.4 5.4 %collective-permute-start.22 = (f32[2,1024]{1,0:T(2,128)S(1)}, f32[2,1024]{1,0:T(2,128)S(1)}, u32[]{:S(2)}, u32[]{:S(2)}) collective-permute-start(f32[2,1024]{1,0:T(2,128)S(1)} %get-tuple-element.155.refs_8_), channel_id=1, source_target_pairs={{0,12},{1,13},{2,14},{3,15},{4,5},{5,4},{6,7},{7,6},{8,9},{9,8},{1... | collective-permute-start | bytes 24584 | tf_op jit(solution)/shard_map/ppermute | solution.py:384
  70.3 14.9 %collective-permute-start.30 = (bf16[2,168,256]{2,1,0:T(8,128)(2,1)S(1)}, bf16[2,168,256]{2,1,0:T(8,128)(2,1)S(1)}, u32[]{:S(2)}, u32[]{:S(2)}) collective-permute-start(bf16[2,168,256]{2,1,0:T(8,128)(2,1)S(1)} %get-tuple-element.171.refs_12_), channel_id=1, source_target_pairs={{0,2},{1,3},{2,0},{3,1},{4,6},{5,7},{6,4},{7,5},{8,10},{9,11},{10,... | collective-permute-start | bytes 516104 | tf_op jit(solution)/shard_map/ppermute | solution.py:478
  71.8 5.1 %collective-permute-start.26 = (f32[2,1024]{1,0:T(2,128)S(1)}, f32[2,1024]{1,0:T(2,128)S(1)}, u32[]{:S(2)}, u32[]{:S(2)}) collective-permute-start(f32[2,1024]{1,0:T(2,128)S(1)} %get-tuple-element.166.refs_8_), channel_id=1, source_target_pairs={{0,8},{4,12},{8,0},{12,4},{1,9},{5,13},{9,1},{13,5},{2,10},{6,14},... | collective-permute-start | bytes 24584 | tf_op jit(solution)/shard_map/ppermute | solution.py:386
  75.3 5.4 %collective-permute-start.27 = (f32[2,1024]{1,0:T(2,128)S(1)}, f32[2,1024]{1,0:T(2,128)S(1)}, u32[]{:S(2)}, u32[]{:S(2)}) collective-permute-start(f32[2,1024]{1,0:T(2,128)S(1)} %get-tuple-element.166.refs_8_), channel_id=1, source_target_pairs={{0,12},{1,13},{2,14},{3,15},{4,5},{5,4},{6,7},{7,6},{8,9},{9,8},{1... | collective-permute-start | bytes 24584 | tf_op jit(solution)/shard_map/ppermute | solution.py:384
  86.4 11.9 %collective-permute-start.35 = (bf16[2,168,256]{2,1,0:T(8,128)(2,1)S(1)}, bf16[2,168,256]{2,1,0:T(8,128)(2,1)S(1)}, u32[]{:S(2)}, u32[]{:S(2)}) collective-permute-start(bf16[2,168,256]{2,1,0:T(8,128)(2,1)S(1)} %get-tuple-element.182.refs_12_), channel_id=1, source_target_pairs={{0,2},{1,3},{2,0},{3,1},{4,6},{5,7},{6,4},{7,5},{8,10},{9,11},{10,... | collective-permute-start | bytes 516104 | tf_op jit(solution)/shard_map/ppermute | solution.py:478
  88.4 5.4 %collective-permute-start.32 = (f32[2,1024]{1,0:T(2,128)S(1)}, f32[2,1024]{1,0:T(2,128)S(1)}, u32[]{:S(2)}, u32[]{:S(2)}) collective-permute-start(f32[2,1024]{1,0:T(2,128)S(1)} %get-tuple-element.177.refs_8_), channel_id=1, source_target_pairs={{0,12},{1,13},{2,14},{3,15},{4,5},{5,4},{6,7},{7,6},{8,9},{9,8},{1... | collective-permute-start | bytes 24584 | tf_op jit(solution)/shard_map/ppermute | solution.py:384
  99.3 14.9 %collective-permute-start.40 = (bf16[2,168,256]{2,1,0:T(8,128)(2,1)S(1)}, bf16[2,168,256]{2,1,0:T(8,128)(2,1)S(1)}, u32[]{:S(2)}, u32[]{:S(2)}) collective-permute-start(bf16[2,168,256]{2,1,0:T(8,128)(2,1)S(1)} %get-tuple-element.193.refs_12_), channel_id=1, source_target_pairs={{0,2},{1,3},{2,0},{3,1},{4,6},{5,7},{6,4},{7,5},{8,10},{9,11},{10,... | collective-permute-start | bytes 516104 | tf_op jit(solution)/shard_map/ppermute | solution.py:478
  100.9 5.1 %collective-permute-start.36 = (f32[2,1024]{1,0:T(2,128)S(1)}, f32[2,1024]{1,0:T(2,128)S(1)}, u32[]{:S(2)}, u32[]{:S(2)}) collective-permute-start(f32[2,1024]{1,0:T(2,128)S(1)} %get-tuple-element.188.refs_8_), channel_id=1, source_target_pairs={{0,8},{4,12},{8,0},{12,4},{1,9},{5,13},{9,1},{13,5},{2,10},{6,14},... | collective-permute-start | bytes 24584 | tf_op jit(solution)/shard_map/ppermute | solution.py:386
  104.4 5.4 %collective-permute-start.37 = (f32[2,1024]{1,0:T(2,128)S(1)}, f32[2,1024]{1,0:T(2,128)S(1)}, u32[]{:S(2)}, u32[]{:S(2)}) collective-permute-start(f32[2,1024]{1,0:T(2,128)S(1)} %get-tuple-element.188.refs_8_), channel_id=1, source_target_pairs={{0,12},{1,13},{2,14},{3,15},{4,5},{5,4},{6,7},{7,6},{8,9},{9,8},{1... | collective-permute-start | bytes 24584 | tf_op jit(solution)/shard_map/ppermute | solution.py:384
  115.3 20.1 %collective-permute-start.41 = (f32[2,168,512]{2,1,0:T(8,128)S(1)}, f32[2,168,512]{2,1,0:T(8,128)S(1)}, u32[]{:S(2)}, u32[]{:S(2)}) collective-permute-start(f32[2,168,512]{2,1,0:T(8,128)S(1)} %get-tuple-element.196), channel_id=1, source_target_pairs={{0,1},{1,0},{2,3},{3,2},{4,5},{5,4},{6,7},{7,6},{8,9},{9,8},{10,11... | collective-permute-start | bytes 2064392 | tf_op jit(solution)/shard_map/ppermute | solution.py:506
  115.4 6.8 %collective-permute-start.42 = (f32[2,168,128]{2,1,0:T(8,128)S(1)}, f32[2,168,128]{2,1,0:T(8,128)S(1)}, u32[]{:S(2)}, u32[]{:S(2)}) collective-permute-start(f32[2,168,128]{2,1,0:T(8,128)S(1)} %get-tuple-element.198), channel_id=1, source_target_pairs={{0,2},{1,3},{2,0},{3,1},{4,6},{5,7},{6,4},{7,5},{8,10},{9,11},{10,... | collective-permute-start | bytes 516104 | tf_op jit(solution)/shard_map/ppermute | solution.py:505
  122.3 12.4 %collective-permute-start.43 = (f32[2,64,168]{2,1,0:T(8,128)S(1)}, f32[2,64,168]{2,1,0:T(8,128)S(1)}, u32[]{:S(2)}, u32[]{:S(2)}) collective-permute-start(f32[2,64,168]{2,1,0:T(8,128)S(1)} %get-tuple-element.200), channel_id=1, source_target_pairs={{0,1},{1,0},{2,3},{3,2},{4,5},{5,4},{6,7},{7,6},{8,9},{9,8},{10,11... | collective-permute-start | bytes 258056 | tf_op jit(solution)/shard_map/ppermute | solution.py:521
  122.4 4.6 %collective-permute-start.44 = (f32[2,1024]{1,0:T(2,128)S(1)}, f32[2,1024]{1,0:T(2,128)S(1)}, u32[]{:S(2)}, u32[]{:S(2)}) collective-permute-start(f32[2,1024]{1,0:T(2,128)S(1)} %get-tuple-element.202.refs_2_), channel_id=1, source_target_pairs={{0,8},{4,12},{8,0},{12,4},{1,9},{5,13},{9,1},{13,5},{2,10},{6,14},... | collective-permute-start | bytes 24584 | tf_op jit(solution)/shard_map/ppermute | solution.py:386
  123.9 5.4 %collective-permute-start.45 = (f32[2,1024]{1,0:T(2,128)S(1)}, f32[2,1024]{1,0:T(2,128)S(1)}, u32[]{:S(2)}, u32[]{:S(2)}) collective-permute-start(f32[2,1024]{1,0:T(2,128)S(1)} %get-tuple-element.202.refs_2_), channel_id=1, source_target_pairs={{0,12},{1,13},{2,14},{3,15},{4,5},{5,4},{6,7},{7,6},{8,9},{9,8},{1... | collective-permute-start | bytes 24584 | tf_op jit(solution)/shard_map/ppermute | solution.py:384
  (32 other events, 137.2 us)
